TPU v7x, 32 devices: a whole 2x2x4 slice. The times are simulated.
32 devices in a mesh: dp: 8 (over z, core), space: 4 (over y, x).
Axes of the slice: x: 2, y: 2, z: 4, core: 2. Of those that a mesh axis runs over, the one named last changes fastest.
Arguments:
- fields: bfloat16 [8, 8, 96, 128], P('dp', 'space'), may hold values from -6 to 6
- cotangent: bfloat16 [8, 8, 96, 128], P('dp', 'space'), may hold values from -6 to 6
- weights: bfloat16 [2, 1152, 128], replicated, may hold values from -6 to 6
- master: float32 [2, 147456], P(None, ('dp', 'space')), may hold values from -6 to 6
- momentum: float32 [2, 147456], P(None, ('dp', 'space')), may hold values from -6 to 6
Outputs:
- result_fields: bfloat16 [8, 8, 96, 128], P('dp', 'space')
- input_grad: bfloat16 [8, 8, 96, 128], P('dp', 'space')
- momentum_next: float32 [2, 147456], P(None, ('dp', 'space'))
- master_next: float32 [2, 147456], P(None, ('dp', 'space'))
- weights_next: bfloat16 [2, 1152, 128], replicated
All inputs are finite; a program needn't handle non-finite values.
Results may differ from a plain program's by a relative error of at most 0.006.
Values may be sent and summed in bfloat16 or wider, within the bound.
No kernel may reach another device: no remote copies, remote signals or barrier semaphores. Data moves between devices by JAX's collectives and lax.ppermute only.
A program may use at most 64 MiB of HBM per device.

v0:
```python
import jax
import jax.numpy as jnp
from jax import lax
from jax.sharding import PartitionSpec as P

momentum_rate = 0.9
learn_rate = 0.1


def with_halo(shard, sides, width):
    for axis, dim in sides:
        devices, length = (lax.axis_size(axis), shard.shape[dim])
        up = [(i, (i + 1) % devices) for i in range(devices - 1)]
        down = [(j, i) for i, j in up]
        last = lax.slice_in_dim(shard, length - width, length, axis=dim)
        leading = lax.slice_in_dim(shard, 0, width, axis=dim)
        before = lax.ppermute(last, axis, up)
        after = lax.ppermute(leading, axis, down)
        shard = jnp.concatenate([before, shard, after], axis=dim)
    return shard


def taps(padded, dilation, height, col_count):
    channels = padded.shape[-1]
    padded = jnp.pad(padded, ((0, 0), (dilation, dilation), (0, 0)))
    pieces = [
        padded[
            tap_row * dilation : tap_row * dilation + height,
            tap_col * dilation : tap_col * dilation + col_count,
            :,
        ]
        for tap_row in range(3)
        for tap_col in range(3)
    ]
    return jnp.concatenate(pieces, axis=-1).reshape(height * col_count, 9 * channels)


def flipped(kernel):
    channels = kernel.shape[-1]
    return (
        kernel.reshape(3, 3, channels, channels)[::-1, ::-1]
        .transpose(0, 1, 3, 2)
        .reshape(9 * channels, channels)
    )


def swish_slope(pre_act):
    sigmoid_value = jax.nn.sigmoid(pre_act)
    return sigmoid_value * (1.0 + pre_act * (1.0 - sigmoid_value))


def contract_rows(left_mat, right_mat):
    return lax.dot_general(
        left_mat, right_mat, (((0,), (0,)), ((), ())), preferred_element_type=jnp.float32
    )


def near_rims(array):
    return with_halo(array, (("space", 0),), 1)


def far_rims(array):
    return with_halo(array, (("space", 0),), 2)


def local(fields, cotangent, weights, master, momentum):
    sample_cells = fields[0]
    height, col_count, channels = sample_cells.shape
    layers = weights.shape[0]
    fan_scale = (9.0 * channels) ** (-0.5)
    inner_taps = taps(near_rims(sample_cells), 1, height, col_count)
    pre_one = jnp.dot(inner_taps, weights[0], preferred_element_type=jnp.float32) * fan_scale
    hidden = jax.nn.silu(pre_one).astype(jnp.bfloat16)
    outer_taps = taps(far_rims(hidden.reshape(height, col_count, channels)), 2, height, col_count)
    pre_two = jnp.dot(outer_taps, weights[1], preferred_element_type=jnp.float32) * fan_scale
    flat_cot = cotangent[0].reshape(height * col_count, channels).astype(jnp.float32)
    result = (jax.nn.silu(pre_two) + hidden.astype(jnp.float32)).astype(jnp.bfloat16)
    delta_two = (flat_cot * swish_slope(pre_two)).astype(jnp.bfloat16)
    back_two = taps(far_rims(delta_two.reshape(height, col_count, channels)), 2, height, col_count)
    mid_grad = (
        jnp.dot(back_two, flipped(weights[1]), preferred_element_type=jnp.float32) * fan_scale
        + flat_cot
    )
    delta_one = (mid_grad * swish_slope(pre_one)).astype(jnp.bfloat16)
    back_one = taps(near_rims(delta_one.reshape(height, col_count, channels)), 1, height, col_count)
    input_grad = (
        jnp.dot(back_one, flipped(weights[0]), preferred_element_type=jnp.float32) * fan_scale
    ).astype(jnp.bfloat16)
    grad_one = contract_rows(inner_taps, delta_one)
    grad_two = contract_rows(outer_taps, delta_two)
    dp_count = lax.axis_size("dp")
    space_count = lax.axis_size("space")
    pixel_total = dp_count * space_count * fields.shape[0] * height * col_count
    grad_factor = fan_scale * (9.0 * channels / pixel_total) ** 0.5
    grad_flat = (jnp.stack([grad_one, grad_two]) * grad_factor).reshape(
        layers, 9 * channels * channels
    )
    shard_len = grad_flat.shape[1] // (dp_count * space_count)
    grad_blocks = grad_flat.reshape(layers, dp_count, space_count, shard_len)
    strip_summed = lax.psum_scatter(
        grad_blocks.astype(jnp.bfloat16), "space", scatter_dimension=2, tiled=True
    ).astype(jnp.float32)
    gradient = lax.psum_scatter(strip_summed, "dp", scatter_dimension=1, tiled=True).reshape(
        layers, shard_len
    )
    momentum_next = momentum_rate * momentum + gradient
    master_next = master - learn_rate * momentum_next
    rounded_master = master_next.astype(jnp.bfloat16)
    piece_view = rounded_master.reshape(layers, 1, 1, shard_len)
    across_samples = lax.all_gather(piece_view, "dp", axis=1, tiled=True)
    gathered = lax.all_gather(across_samples, "space", axis=2, tiled=True)
    weights_next = gathered.reshape(layers, 9 * channels, channels)
    return (
        result.reshape(1, height, col_count, channels),
        input_grad.reshape(1, height, col_count, channels),
        momentum_next,
        master_next,
        weights_next,
    )


def solution(mesh):
    in_specs = (
        P("dp", "space", None, None),
        P("dp", "space", None, None),
        P(),
        P(None, ("dp", "space")),
        P(None, ("dp", "space")),
    )
    out_specs = (
        P("dp", "space", None, None),
        P("dp", "space", None, None),
        P(None, ("dp", "space")),
        P(None, ("dp", "space")),
        P(),
    )
    return jax.shard_map(local, mesh=mesh, in_specs=in_specs, out_specs=out_specs, check_vma=False)
```

profile of v0, /device:TPU:0, one launch (start us, length us, event | category | flops | bytes accessed | tf_op | source)
XLA Modules:
  0.0 168.0 jit_solution(13340392315351826461)
XLA Ops:
  7.2 0.0 reduce-scatter.4.cloned.1.call-start
  7.2 0.8 slice_bitcast_fusion.3
  8.0 4.9 %collective-permute-start = (bf16[1,96,128]{2,1,0:T(8,128)(2,1)S(1)}, bf16[1,96,128]{2,1,0:T(8,128)(2,1)S(1)}, u32[]{:S(2)}, u32[]{:S(2)}) collective-permute-start(bf16[1,96,128]{2,1,0:T(8,128)(2,1)S(1)} %get-tuple-element.42), channel_id=1, source_target_pairs={{0,1},{1,2},{2,3},{4,5},{5,6},{6,7},{8,9},{9,10},{10,11},{12,13},{... | collective-permute-start | bytes 73736 | tf_op jit(solution)/shard_map/ppermute | solution.py:17
  12.8 1.3 collective-permute-start.1
  14.1 1.1 fusion.17
  15.2 0.0 copy-start
  15.3 0.0 collective-permute-done
  15.3 3.3 %collective-permute-done.1 = bf16[1,96,128]{2,1,0:T(8,128)(2,1)S(1)} collective-permute-done((bf16[1,96,128]{2,1,0:T(8,128)(2,1)S(1)}, bf16[1,96,128]{2,1,0:T(8,128)(2,1)S(1)}, u32[]{:S(2)}, u32[]{:S(2)}) %collective-permute-start.1) | collective-permute-done | bytes 24608 | tf_op jit(solution)/shard_map/ppermute | solution.py:18
  18.6 0.0 copy-done
  18.7 0.0 copy-start.1
  18.9 0.8 copy-done.1
  19.7 0.3 multiply_convert_fusion
  20.0 4.3 %collective-permute-start.2 = (bf16[2,96,128]{2,1,0:T(8,128)(2,1)S(1)}, bf16[2,96,128]{2,1,0:T(8,128)(2,1)S(1)}, u32[]{:S(2)}, u32[]{:S(2)}) collective-permute-start(bf16[2,96,128]{2,1,0:T(8,128)(2,1)S(1)} %bitcast.105), channel_id=1, source_target_pairs={{0,1},{1,2},{2,3},{4,5},{5,6},{6,7},{8,9},{9,10},{10,11},{12,13},{... | collective-permute-start | bytes 147464 | tf_op jit(solution)/shard_map/ppermute | solution.py:17
  24.3 1.3 collective-permute-start.3
  25.7 0.0 copy-start.5
  25.7 0.2 copy.26
  25.9 0.2 copy.27
  26.1 0.2 copy-done.5
  26.3 0.6 dynamic-slice.2
  26.9 0.0 collective-permute-done.2
  26.9 3.4 %collective-permute-done.3 = bf16[2,96,128]{2,1,0:T(8,128)(2,1)S(1)} collective-permute-done((bf16[2,96,128]{2,1,0:T(8,128)(2,1)S(1)}, bf16[2,96,128]{2,1,0:T(8,128)(2,1)S(1)}, u32[]{:S(2)}, u32[]{:S(2)}) %collective-permute-start.3) | collective-permute-done | bytes 49184 | tf_op jit(solution)/shard_map/ppermute | solution.py:18
  30.3 0.1 select_maximum_fusion.2
  30.4 0.1 fusion.19
  30.4 0.0 copy-start.4
  30.6 0.6 copy-done.4
  31.2 0.9 fusion.11
  32.2 3.4 %collective-permute-start.4 = (bf16[2,96,128]{2,1,0:T(8,128)(2,1)S(1)}, bf16[2,96,128]{2,1,0:T(8,128)(2,1)S(1)}, u32[]{:S(2)}, u32[]{:S(2)}) collective-permute-start(bf16[2,96,128]{2,1,0:T(8,128)(2,1)S(1)} %bitcast.101), channel_id=1, source_target_pairs={{0,1},{1,2},{2,3},{4,5},{5,6},{6,7},{8,9},{9,10},{10,11},{12,13},{... | collective-permute-start | bytes 147464 | tf_op jit(solution)/shard_map/ppermute | solution.py:17
  35.6 1.3 collective-permute-start.5
  36.9 0.4 fusion.23
  37.2 0.2 stack.10
  37.5 0.2 copy.29
  37.7 0.0 collective-permute-done.4
  37.7 3.9 %collective-permute-done.5 = bf16[2,96,128]{2,1,0:T(8,128)(2,1)S(1)} collective-permute-done((bf16[2,96,128]{2,1,0:T(8,128)(2,1)S(1)}, bf16[2,96,128]{2,1,0:T(8,128)(2,1)S(1)}, u32[]{:S(2)}, u32[]{:S(2)}) %collective-permute-start.5) | collective-permute-done | bytes 49184 | tf_op jit(solution)/shard_map/ppermute | solution.py:18
  41.6 0.1 select_maximum_fusion
  41.6 0.1 fusion.18
  41.9 0.3 fusion.3
  42.2 0.4 fusion.22
  42.5 0.2 stack.9
  42.8 0.2 copy.28
  43.0 2.8 %collective-permute-start.6 = (bf16[1,96,128]{2,1,0:T(8,128)(2,1)S(1)}, bf16[1,96,128]{2,1,0:T(8,128)(2,1)S(1)}, u32[]{:S(2)}, u32[]{:S(2)}) collective-permute-start(bf16[1,96,128]{2,1,0:T(8,128)(2,1)S(1)} %get-tuple-element.38), channel_id=1, source_target_pairs={{0,1},{1,2},{2,3},{4,5},{5,6},{6,7},{8,9},{9,10},{10,11},{12,13},{... | collective-permute-start | bytes 73736 | tf_op jit(solution)/shard_map/ppermute | solution.py:17
  45.8 1.3 collective-permute-start.7
  47.1 0.9 fusion
  48.0 0.0 reduce-scatter.4.cloned.1.call-update
  48.0 0.0 all-reduce.8.cloned.1.call-start
  48.1 0.0 collective-permute-done.6
  48.1 3.4 %collective-permute-done.7 = bf16[1,96,128]{2,1,0:T(8,128)(2,1)S(1)} collective-permute-done((bf16[1,96,128]{2,1,0:T(8,128)(2,1)S(1)}, bf16[1,96,128]{2,1,0:T(8,128)(2,1)S(1)}, u32[]{:S(2)}, u32[]{:S(2)}) %collective-permute-start.7) | collective-permute-done | bytes 24608 | tf_op jit(solution)/shard_map/ppermute | solution.py:18
  51.8 23.2 %reduce-scatter.4.cloned.1.call-done = bf16[2,8,1,4608]{3,1,0,2:T(8,128)(2,1)} async-done(((bf16[2,8,4,4608]{3,1,0,2:T(8,128)(2,1)}), bf16[2,8,1,4608]{3,1,0,2:T(8,128)(2,1)}) %reduce-scatter.4.cloned.1.call-update) | async-done | bytes 147472
  75.1 1.7 %copy.30 = f32[2,8,1,4608]{3,0,2,1:T(2,128)} copy(bf16[2,8,1,4608]{3,1,0,2:T(8,128)(2,1)} %reduce-scatter.4.cloned.1.call-done) | data formatting | bytes 442368 | tf_op jit(solution)/shard_map/convert_element_type | solution.py:102
  76.8 0.0 copy-start.2
  76.8 0.0 copy-start.3
  76.8 0.0 all-reduce.8.cloned.1.call-update
  76.8 0.9 fusion.4
  77.7 53.5 %all-reduce.8.cloned.1.call-done = f32[2,8,1,4608]{3,0,2,1:T(2,128)} async-done(((f32[2,8,1,4608]{3,0,2,1:T(2,128)}), f32[2,8,1,4608]{3,0,2,1:T(2,128)}) %all-reduce.8.cloned.1.call-update) | async-done | bytes 294928
  131.3 0.0 copy-done.2
  131.3 0.0 copy-done.3
  131.3 2.1 %fusion.15 = (bf16[2,4608]{1,0:T(2,128)(2,1)S(1)}, f32[2,4608]{1,0:T(2,128)}, f32[2,4608]{1,0:T(2,128)}) fusion(f32[2,4608]{1,0:T(2,128)S(1)} %copy-done.2, f32[2,8,1,4608]{3,0,2,1:T(2,128)} %all-reduce.8.cloned.1.call-done, u32[]{:T(128)} %bitcast.55, f32[2,4608]{1,0:T(2,128)S(1)} %copy-done.3), kind=kLoop, calls=%fused_computation.86 | loop fusion | flops 46080 | bytes 202756 | tf_op jit(solution)/shard_map/convert_element_type | solution.py:108
  133.3 15.5 %all-gather = bf16[2,36864]{1,0:T(2,128)(2,1)S(1)} all-gather(bf16[2,4608]{1,0:T(2,128)(2,1)S(1)} %get-tuple-element.5), channel_id=2, replica_groups=mesh['dp'=8,'space'=4] {'dp'}, dimensions={1}, use_global_device_ids=true | all-gather | bytes 165888 | tf_op jit(solution)/shard_map/all_gather | solution.py:110
  148.8 10.8 %all_gather.7 = bf16[2,8,4,4608]{3,1,0,2:T(8,128)(2,1)S(1)} all-gather(bf16[2,8,1,4608]{3,1,0,2:T(8,128)(2,1)S(1)} %bitcast.100), channel_id=1, replica_groups=mesh['dp'=8,'space'=4] {'space'}, dimensions={2}, use_global_device_ids=true | all-gather | bytes 737280 | tf_op jit(solution)/shard_map/all_gather | solution.py:111
  159.6 0.5 copy.31
  160.1 1.0 reshape.103
  (46 shorter events, 0.8 us)
Async XLA Ops:
  7.2 67.9 %reduce-scatter.4.cloned.1.call-start = ((), (), s32[]{:S(2)}) async-start(), calls=%async_computation.2 | async-start | bytes 737280
  8.0 7.3 %collective-permute-start = (bf16[1,96,128]{2,1,0:T(8,128)(2,1)S(1)}, bf16[1,96,128]{2,1,0:T(8,128)(2,1)S(1)}, u32[]{:S(2)}, u32[]{:S(2)}) collective-permute-start(bf16[1,96,128]{2,1,0:T(8,128)(2,1)S(1)} %get-tuple-element.42), channel_id=1, source_target_pairs={{0,1},{1,2},{2,3},{4,5},{5,6},{6,7},{8,9},{9,10},{10,11},{12,13},{... | collective-permute-start | bytes 73736 | tf_op jit(solution)/shard_map/ppermute | solution.py:17
  12.8 5.7 %collective-permute-start.1 = (bf16[1,96,128]{2,1,0:T(8,128)(2,1)S(1)}, bf16[1,96,128]{2,1,0:T(8,128)(2,1)S(1)}, u32[]{:S(2)}, u32[]{:S(2)}) collective-permute-start(bf16[1,96,128]{2,1,0:T(8,128)(2,1)S(1)} %get-tuple-element.43), channel_id=1, source_target_pairs={{1,0},{2,1},{3,2},{5,4},{6,5},{7,6},{9,8},{10,9},{11,10},{13,12},{... | collective-permute-start | bytes 73736 | tf_op jit(solution)/shard_map/ppermute | solution.py:18
  15.2 3.3 %copy-start = (bf16[1,2,96,128]{3,2,1,0:T(8,128)(2,1)S(1)}, bf16[1,2,96,128]{3,2,1,0:T(8,128)(2,1)}, u32[]{:S(2)}) copy-start(bf16[1,2,96,128]{3,2,1,0:T(8,128)(2,1)} %param.5) | copy-start | bytes 147460
  18.7 1.1 copy-start.1
  20.0 6.9 %collective-permute-start.2 = (bf16[2,96,128]{2,1,0:T(8,128)(2,1)S(1)}, bf16[2,96,128]{2,1,0:T(8,128)(2,1)S(1)}, u32[]{:S(2)}, u32[]{:S(2)}) collective-permute-start(bf16[2,96,128]{2,1,0:T(8,128)(2,1)S(1)} %bitcast.105), channel_id=1, source_target_pairs={{0,1},{1,2},{2,3},{4,5},{5,6},{6,7},{8,9},{9,10},{10,11},{12,13},{... | collective-permute-start | bytes 147464 | tf_op jit(solution)/shard_map/ppermute | solution.py:17
  24.3 6.0 %collective-permute-start.3 = (bf16[2,96,128]{2,1,0:T(8,128)(2,1)S(1)}, bf16[2,96,128]{2,1,0:T(8,128)(2,1)S(1)}, u32[]{:S(2)}, u32[]{:S(2)}) collective-permute-start(bf16[2,96,128]{2,1,0:T(8,128)(2,1)S(1)} %bitcast.106), channel_id=1, source_target_pairs={{1,0},{2,1},{3,2},{5,4},{6,5},{7,6},{9,8},{10,9},{11,10},{13,12},{... | collective-permute-start | bytes 147464 | tf_op jit(solution)/shard_map/ppermute | solution.py:18
  25.7 0.7 copy-start.5
  30.4 0.8 copy-start.4
  32.2 5.5 %collective-permute-start.4 = (bf16[2,96,128]{2,1,0:T(8,128)(2,1)S(1)}, bf16[2,96,128]{2,1,0:T(8,128)(2,1)S(1)}, u32[]{:S(2)}, u32[]{:S(2)}) collective-permute-start(bf16[2,96,128]{2,1,0:T(8,128)(2,1)S(1)} %bitcast.101), channel_id=1, source_target_pairs={{0,1},{1,2},{2,3},{4,5},{5,6},{6,7},{8,9},{9,10},{10,11},{12,13},{... | collective-permute-start | bytes 147464 | tf_op jit(solution)/shard_map/ppermute | solution.py:17
  35.6 6.0 %collective-permute-start.5 = (bf16[2,96,128]{2,1,0:T(8,128)(2,1)S(1)}, bf16[2,96,128]{2,1,0:T(8,128)(2,1)S(1)}, u32[]{:S(2)}, u32[]{:S(2)}) collective-permute-start(bf16[2,96,128]{2,1,0:T(8,128)(2,1)S(1)} %bitcast.102), channel_id=1, source_target_pairs={{1,0},{2,1},{3,2},{5,4},{6,5},{7,6},{9,8},{10,9},{11,10},{13,12},{... | collective-permute-start | bytes 147464 | tf_op jit(solution)/shard_map/ppermute | solution.py:18
  43.0 5.1 %collective-permute-start.6 = (bf16[1,96,128]{2,1,0:T(8,128)(2,1)S(1)}, bf16[1,96,128]{2,1,0:T(8,128)(2,1)S(1)}, u32[]{:S(2)}, u32[]{:S(2)}) collective-permute-start(bf16[1,96,128]{2,1,0:T(8,128)(2,1)S(1)} %get-tuple-element.38), channel_id=1, source_target_pairs={{0,1},{1,2},{2,3},{4,5},{5,6},{6,7},{8,9},{9,10},{10,11},{12,13},{... | collective-permute-start | bytes 73736 | tf_op jit(solution)/shard_map/ppermute | solution.py:17
  45.8 5.7 %collective-permute-start.7 = (bf16[1,96,128]{2,1,0:T(8,128)(2,1)S(1)}, bf16[1,96,128]{2,1,0:T(8,128)(2,1)S(1)}, u32[]{:S(2)}, u32[]{:S(2)}) collective-permute-start(bf16[1,96,128]{2,1,0:T(8,128)(2,1)S(1)} %get-tuple-element.39), channel_id=1, source_target_pairs={{1,0},{2,1},{3,2},{5,4},{6,5},{7,6},{9,8},{10,9},{11,10},{13,12},{... | collective-permute-start | bytes 73736 | tf_op jit(solution)/shard_map/ppermute | solution.py:18
  48.0 83.2 %all-reduce.8.cloned.1.call-start = ((), (), s32[]{:S(2)}) async-start(), calls=%async_computation.1 | async-start | bytes 589824
  76.8 54.5 %copy-start.2 = (f32[2,4608]{1,0:T(2,128)S(1)}, f32[2,4608]{1,0:T(2,128)}, u32[]{:S(2)}) copy-start(f32[2,4608]{1,0:T(2,128)} %param.8) | copy-start | bytes 110596
  76.8 54.5 %copy-start.3 = (f32[2,4608]{1,0:T(2,128)S(1)}, f32[2,4608]{1,0:T(2,128)}, u32[]{:S(2)}) copy-start(f32[2,4608]{1,0:T(2,128)} %param.9) | copy-start | bytes 110596
Sparse Core Ops, SparseCore 0:
  48.1 26.8 reduce-scatter.3
  78.0 53.2 all-reduce.7
where the time goes:
time: 169 us; the launch traced here: 168 us
  waiting for transfers between devices  90.8 us (54%)
  blocking collectives  26.3 us (16%)
  starting transfers between devices  20.6 us (12%)
  between operations  14.6 us (9%)
  local copies, waits for them, and re-layouts  9.43 us (6%)
  other arithmetic  3.17 us (2%)
  matrix products  3.14 us (2%)
    unnamed x4, waiting for transfers between devices  76.8 us
    all_gather x1, blocking collectives, local(): across_samples = lax.all_gather(piece_view, 'dp', axis=1, tiled=True)  15.5 us
    ppermute x4, starting transfers between devices, with_halo(): before = lax.ppermute(last, axis, up)  15.4 us
    ppermute x4, waiting for transfers between devices, with_halo(): after = lax.ppermute(leading, axis, down)  14 us
    all_gather x1, blocking collectives, local(): gathered = lax.all_gather(across_samples, 'space', axis=2, tiled=True)  10.8 us
    ppermute x4, starting transfers between devices, with_halo(): after = lax.ppermute(leading, axis, down)  5.17 us
  transfers between devices with their start and end apart: 10, of which 6 were waited for; matrix products, arithmetic and copies ran while one was open for 3% of the time, Pallas kernels for 0%

commit v1 on v0

v1 whole, which is shorter than its diff:
```python
import jax
import jax.numpy as jnp
from jax import lax
from jax.sharding import PartitionSpec as P

momentum_rate = 0.9
learn_rate = 0.1


def taps(rows, dilation):
    height, col_count, channels = rows.shape
    padded = jnp.pad(rows, ((dilation, dilation), (dilation, dilation), (0, 0)))
    pieces = [
        padded[
            tap_row * dilation : tap_row * dilation + height,
            tap_col * dilation : tap_col * dilation + col_count,
            :,
        ]
        for tap_row in range(3)
        for tap_col in range(3)
    ]
    return jnp.concatenate(pieces, axis=-1).reshape(height * col_count, 9 * channels)


def flipped(kernel):
    channels = kernel.shape[-1]
    return (
        kernel.reshape(3, 3, channels, channels)[::-1, ::-1]
        .transpose(0, 1, 3, 2)
        .reshape(9 * channels, channels)
    )


def swish_slope(pre_act):
    sigmoid_value = jax.nn.sigmoid(pre_act)
    return sigmoid_value * (1.0 + pre_act * (1.0 - sigmoid_value))


def contract_rows(left_mat, right_mat):
    return lax.dot_general(
        left_mat, right_mat, (((0,), (0,)), ((), ())), preferred_element_type=jnp.float32
    )


def local(fields, cotangent, weights, master, momentum):
    _, strip, col_count, channels = fields.shape
    layers = weights.shape[0]
    dp_count = lax.axis_size("dp")
    space_count = lax.axis_size("space")
    height = strip * space_count
    cells = height * col_count
    where = lax.axis_index("space")
    fan_scale = (9.0 * channels) ** (-0.5)

    both = lax.all_gather(jnp.concatenate([fields, cotangent], axis=0), "space", axis=0)
    sample = both[:, 0].reshape(height, col_count, channels)
    flat_cot = both[:, 1].reshape(cells, channels).astype(jnp.float32)

    def own(flat):
        return lax.dynamic_slice_in_dim(flat, where * strip * col_count, strip * col_count, axis=0)

    inner_taps = taps(sample, 1)
    pre_one = jnp.dot(inner_taps, weights[0], preferred_element_type=jnp.float32) * fan_scale
    hidden = jax.nn.silu(pre_one).astype(jnp.bfloat16)
    outer_taps = taps(hidden.reshape(height, col_count, channels), 2)
    pre_two = jnp.dot(outer_taps, weights[1], preferred_element_type=jnp.float32) * fan_scale
    result = (jax.nn.silu(pre_two) + hidden.astype(jnp.float32)).astype(jnp.bfloat16)
    delta_two = (flat_cot * swish_slope(pre_two)).astype(jnp.bfloat16)
    back_two = taps(delta_two.reshape(height, col_count, channels), 2)
    mid_grad = (
        jnp.dot(back_two, flipped(weights[1]), preferred_element_type=jnp.float32) * fan_scale
        + flat_cot
    )
    delta_one = (mid_grad * swish_slope(pre_one)).astype(jnp.bfloat16)
    back_one = taps(delta_one.reshape(height, col_count, channels), 1)
    input_grad = (
        jnp.dot(own(back_one), flipped(weights[0]), preferred_element_type=jnp.float32) * fan_scale
    ).astype(jnp.bfloat16)
    grad_one = contract_rows(inner_taps, delta_one)
    grad_two = contract_rows(outer_taps, delta_two)

    pixel_total = dp_count * fields.shape[0] * cells
    grad_factor = fan_scale * (9.0 * channels / pixel_total) ** 0.5
    shard_len = 9 * channels * channels // (dp_count * space_count)
    blocks = (jnp.stack([grad_one, grad_two]) * grad_factor).astype(jnp.bfloat16)
    blocks = blocks.reshape(layers, dp_count, space_count, shard_len)
    quarter = lax.dynamic_index_in_dim(blocks, where, axis=2, keepdims=False)
    swapped = lax.all_to_all(quarter.transpose(1, 0, 2), "dp", 0, 0, tiled=True)
    gradient = swapped.astype(jnp.float32).sum(axis=0)
    momentum_next = momentum_rate * momentum + gradient
    master_next = master - learn_rate * momentum_next
    pieces = lax.all_gather(master_next.astype(jnp.bfloat16), ("dp", "space"), axis=0)
    weights_next = pieces.transpose(1, 0, 2).reshape(layers, 9 * channels, channels)
    return (
        own(result).reshape(1, strip, col_count, channels),
        input_grad.reshape(1, strip, col_count, channels),
        momentum_next,
        master_next,
        weights_next,
    )


def solution(mesh):
    split = P("dp", "space", None, None)
    shard = P(None, ("dp", "space"))
    return jax.shard_map(
        local,
        mesh=mesh,
        in_specs=(split, split, P(), shard, shard),
        out_specs=(split, split, shard, shard, P()),
        check_vma=False,
    )
```

time: 169 us -> 114 us (0.67)
  waiting for transfers between devices: 90.8 us -> 0.01 us
  blocking collectives: 26.3 us -> 81.9 us
  starting transfers between devices: 20.6 us -> 4.88 us
  between operations: 14.6 us -> 1.03 us
  local copies, waits for them, and re-layouts: 9.43 us -> 15.3 us
  matrix products: 3.14 us -> 6.93 us
    unnamed x4 -> x0, waiting for transfers between devices: 76.8 us -> none
    all_gather x2, blocking collectives: 26.3 us -> 81.9 us  [the longest x1 70.9 us: local(): lax.all_gather(master_next.astype(jnp.bfloat16), ('dp', 'space'), axis=0)]
    ppermute x8 -> x0, starting transfers between devices: 20.5 us -> none  [the longest x4 15.4 us: with_halo(): before = lax.ppermute(last, axis, up)]
    ppermute x8 -> x0, waiting for transfers between devices: 14 us -> none  [the longest x4 14 us: with_halo(): after = lax.ppermute(leading, axis, down)]
    unnamed x46 -> x50, local copies, waits for them, and re-layouts: 2.77 us -> 8.49 us
    all_to_all x0 -> x1, starting transfers between devices: none -> 4.88 us  [local(): swapped = lax.all_to_all(quarter.transpose(1, 0, 2), 'dp', 0, 0, tiled=True)]
    convert_element_type x1 -> x0, local copies, waits for them, and re-layouts: 1.74 us -> none  [local(): strip_summed = lax.psum_scatter(grad_blocks.astype(jnp.bfloat16), 'space'...]
  transfers between devices with their start and end apart: 10 -> 1, of which waited for: 6 -> 0; matrix products, arithmetic and copies ran while one was open for 3% -> 9% of each run, Pallas kernels for 0% -> 0%
where the time goes in v1:
time: 114 us; the launch traced here: 113 us
  blocking collectives  81.9 us (72%)
  local copies, waits for them, and re-layouts  15.3 us (13%)
  matrix products  6.93 us (6%)
  starting transfers between devices  4.88 us (4%)
  other arithmetic  3.31 us (3%)
    all_gather x1, blocking collectives, local(): lax.all_gather(master_next.astype(jnp.bfloat16), ('dp', 'space'), axis=0)  70.9 us
    all_gather x1, blocking collectives, local(): lax.all_gather(jnp.concatenate([fields, cotangent], axis=0), 'space', axi...  11 us
    unnamed x50, local copies, waits for them, and re-layouts  8.49 us
    all_to_all x1, starting transfers between devices, local(): swapped = lax.all_to_all(quarter.transpose(1, 0, 2), 'dp', 0, 0, tiled=True)  4.88 us
  transfers between devices with their start and end apart: 1, of which 0 were waited for; matrix products, arithmetic and copies ran while one was open for 9% of the time, Pallas kernels for 0%

profile of v1, /device:TPU:0, one launch (start us, length us, event | category | flops | bytes accessed | tf_op | source)
XLA Modules:
  0.0 113.4 jit_solution(15749497826332987728)
XLA Ops:
  0.6 0.0 copy-start.1
  0.6 0.9 pad_maximum_fusion
  1.5 11.0 %all-gather = bf16[8,2,96,128]{3,2,1,0:T(8,128)(2,1)S(1)} all-gather(bf16[2,2,96,128]{3,2,1,0:T(8,128)(2,1)S(1)} %pad_maximum_fusion), channel_id=2, replica_groups=mesh['dp'=8,'space'=4] {'space'}, dimensions={0}, use_global_device_ids=true | all-gather | bytes 491520 | tf_op jit(solution)/shard_map/all_gather | solution.py:55
  12.5 0.7 fusion.18
  13.2 0.0 copy-done.1
  13.3 0.9 copy.29
  14.2 0.2 pad_slice_fusion.24
  14.4 0.0 copy-start.2
  14.9 0.6 copy-done.2
  15.5 1.4 %multiply_convert_fusion = (bf16[768,128]{1,0:T(8,128)(2,1)S(1)}, f32[768,128]{1,0:T(8,128)}) fusion(bf16[768,1152]{1,0:T(8,128)(2,1)S(1)} %constant_dynamic-update-slice_fusion, bf16[2,1152,128]{2,1,0:T(8,128)(2,1)S(1)} %copy-done.2), kind=kOutput, calls=%fused_computation.30 | convolution fusion | flops 227082240 | bytes 2654208 | tf_op jit(solution)/shard_map/dot_general | solution.py:63
  16.9 0.0 copy-start
  16.9 0.2 pad_slice_fusion.8
  17.1 0.0 copy-start.4
  17.4 0.2 copy-done
  17.8 0.3 copy-done.4
  18.0 1.6 %fusion.5 = (bf16[768,128]{1,0:T(8,128)(2,1)S(1)}, f32[768,128]{1,0:T(8,128)}, f32[768,128]{1,0:T(8,128)}) fusion(bf16[4,1,2,96,128]{4,3,2,1,0:T(8,128)(2,1)S(1)} %copy-done.4, bf16[768,1152]{1,0:T(8,128)(2,1)S(1)} %constant_dynamic-update-slice_fusion.9, bf16[2,1152,128]{2,1,0:T(8,128)(2,1)S(1)} %copy-done.2), kind=kOutput, calls=%fused_computation.28 | convolution fusion | flops 227573760 | bytes 3244032 | tf_op jit(solution)/shard_map/dot_general | solution.py:66
  19.7 0.7 fusion.20
  20.3 0.2 stack.10
  20.6 0.2 copy.32
  20.8 0.2 pad_slice_fusion
  21.0 0.0 copy-start.3
  21.0 0.0 copy-start.5
  21.0 0.0 copy-start.8
  21.5 0.4 copy-done.3
  21.9 0.1 copy-done.5
  22.0 0.2 copy-done.8
  22.2 0.7 fusion.2
  22.8 0.7 fusion.19
  23.5 0.2 stack.9
  23.7 0.2 copy.31
  24.0 0.8 copy.33
  24.8 4.9 %all-to-all-start = ((bf16[8,2,4608]{2,1,0:T(2,128)(2,1)}), bf16[8,2,4608]{2,1,0:T(2,128)(2,1)S(1)}, u32[]{:S(2)}, u32[]{:S(2)}) async-start(bf16[8,2,4608]{2,1,0:T(2,128)(2,1)} %copy.33), calls=%async_computation | async-start | bytes 294912 | tf_op jit(solution)/shard_map/all_to_all | solution.py:88
  29.7 0.2 pad_slice_fusion.16
  29.9 0.7 constant_dynamic-update-slice_fusion.35
  30.6 0.7 constant_dynamic-update-slice_fusion.34
  31.3 0.7 constant_dynamic-update-slice_fusion.33
  32.0 0.7 constant_dynamic-update-slice_fusion.32
  32.7 0.7 constant_dynamic-update-slice_fusion.31
  33.4 0.0 copy-start.6
  33.4 0.0 copy-start.7
  33.4 0.7 constant_dynamic-update-slice_fusion.30
  34.1 0.7 constant_dynamic-update-slice_fusion.29
  34.9 0.7 constant_dynamic-update-slice_fusion.28
  35.6 0.7 constant_dynamic-update-slice_fusion.27
  36.3 1.6 %fusion.13 = bf16[192,128]{1,0:T(8,128)(2,1)} fusion(f32[768,128]{1,0:T(8,128)} %get-tuple-element.11, s32[]{:T(128)S(6)} %select_n.8, f32[768,128]{1,0:T(8,128)} %get-tuple-element.48, bf16[768,128]{1,0:T(8,128)(2,1)} %copy-done), kind=kLoop, calls=%fused_computation.59 | loop fusion | flops 98304 | bytes 294916 | tf_op jit(solution)/shard_map/convert_element_type | solution.py:67
  37.9 0.2 copy.30
  38.1 1.9 %fusion.3 = bf16[192,128]{1,0:T(8,128)(2,1)} fusion(bf16[1152,128]{1,0:T(8,128)(2,1)S(1)} %bitcast.86, bf16[768,1152]{1,0:T(8,128)(2,1)} %constant_dynamic-update-slice_fusion.27, s32[]{:T(128)S(6)} %select_n.8), kind=kOutput, calls=%fused_computation.9 | convolution fusion | flops 56672256 | bytes 786436 | tf_op jit(solution)/shard_map/dot_general | solution.py:77
  40.0 0.0 all-to-all-done
  40.0 0.1 convert_reduce_fusion
  40.1 0.0 copy-done.6
  40.1 0.0 copy-done.7
  40.1 0.7 convert_bitcast_fusion
  40.8 70.9 %all-gather.2 = bf16[32,2,4608]{2,1,0:T(2,128)(2,1)S(1)} all-gather(bf16[1,2,4608]{2,1,0:T(2,128)(2,1)S(1)} %get-tuple-element.5), channel_id=3, replica_groups=mesh['dp'=8,'space'=4] {'dp','space'}, dimensions={0}, use_global_device_ids=true | all-gather | bytes 608256 | tf_op jit(solution)/shard_map/all_gather | solution.py:92
  111.8 0.1 copy.34
  111.8 1.5 %reshape.92 = bf16[2,1152,128]{2,1,0:T(8,128)(2,1)} reshape(bf16[2,32,4608]{2,1,0:T(8,128)(2,1)S(1)} %copy.34) | data formatting | bytes 1179648 | tf_op jit(solution)/shard_map/reshape | solution.py:93
  (31 shorter events, 1.4 us)
Async XLA Ops:
  0.6 12.6 %copy-start.1 = (bf16[2,1152,128]{2,1,0:T(8,128)(2,1)S(1)}, bf16[2,1152,128]{2,1,0:T(8,128)(2,1)}, u32[]{:S(2)}) copy-start(bf16[2,1152,128]{2,1,0:T(8,128)(2,1)} %param.7) | copy-start | bytes 1769476
  14.4 1.1 copy-start.2
  16.9 0.7 copy-start
  17.1 0.9 copy-start.4
  21.0 1.0 copy-start.3
  21.0 1.0 copy-start.5
  21.0 1.2 %copy-start.8 = (f32[768,128]{1,0:T(8,128)S(1)}, f32[768,128]{1,0:T(8,128)}, u32[]{:S(2)}) copy-start(f32[768,128]{1,0:T(8,128)} %get-tuple-element.47) | copy-start | bytes 1179652
  24.8 15.2 %all-to-all-start = ((bf16[8,2,4608]{2,1,0:T(2,128)(2,1)}), bf16[8,2,4608]{2,1,0:T(2,128)(2,1)S(1)}, u32[]{:S(2)}, u32[]{:S(2)}) async-start(bf16[8,2,4608]{2,1,0:T(2,128)(2,1)} %copy.33), calls=%async_computation | async-start | bytes 294912 | tf_op jit(solution)/shard_map/all_to_all | solution.py:88
  33.4 6.7 %copy-start.6 = (f32[2,4608]{1,0:T(2,128)S(1)}, f32[2,4608]{1,0:T(2,128)}, u32[]{:S(2)}) copy-start(f32[2,4608]{1,0:T(2,128)} %param.8) | copy-start | bytes 110596
  33.4 6.7 %copy-start.7 = (f32[2,4608]{1,0:T(2,128)S(1)}, f32[2,4608]{1,0:T(2,128)}, u32[]{:S(2)}) copy-start(f32[2,4608]{1,0:T(2,128)} %param.9) | copy-start | bytes 110596

commit v2 on v1

v2 whole, which is shorter than its diff:
```python
import functools

import jax
import jax.numpy as jnp
from jax import lax
from jax.experimental import pallas as pl
from jax.experimental.pallas import tpu as pltpu
from jax.sharding import PartitionSpec as P

momentum_rate = 0.9
learn_rate = 0.1
lane = 128


def sigmoid(value):
    return 1.0 / (1.0 + jnp.exp(-value))


def slope_of(value, sig):
    return sig * (1.0 + value * (1.0 - sig))


def spread(rows, shift_ref, dilation, height, cols):
    channels = rows.shape[-1]
    cube = rows.reshape(height, cols, channels)
    column = lax.broadcasted_iota(jnp.int32, cube.shape, 1)
    margin = dilation * cols
    right = jnp.where(column < dilation, 0.0, pltpu.roll(cube, dilation, 1))
    left = jnp.where(column >= cols - dilation, 0.0, pltpu.roll(cube, cols - dilation, 1))
    for b, moved in enumerate((right, cube, left)):
        lanes = slice(b * channels, (b + 1) * channels)
        shift_ref[margin : margin + height * cols, lanes] = moved.reshape(
            height * cols, channels
        ).astype(jnp.bfloat16)
    edge = jnp.zeros((margin, 3 * channels), jnp.bfloat16)
    shift_ref[:margin, :] = edge
    shift_ref[margin + height * cols : 2 * margin + height * cols, :] = edge


def conv(shift_ref, kernel_ref, layer, dilation, cells, cols, channels):
    total = None
    for a in range(3):
        part = jnp.dot(
            shift_ref[a * dilation * cols : a * dilation * cols + cells, :],
            kernel_ref[layer, a * 3 * channels : (a + 1) * 3 * channels, :],
            preferred_element_type=jnp.float32,
        )
        total = part if total is None else total + part
    return total


def back_conv(shift_ref, flip_ref, dilation, cells, cols):
    total = None
    for a in range(3):
        part = lax.dot_general(
            shift_ref[a * dilation * cols : a * dilation * cols + cells, :],
            flip_ref[a],
            (((1,), (1,)), ((), ())),
            preferred_element_type=jnp.float32,
        )
        total = part if total is None else total + part
    return total


def flip_into(kernel_ref, layer, flip_ref, channels):
    for a in range(3):
        for b in range(3):
            tap = ((2 - a) * 3 + (2 - b)) * channels
            flip_ref[a, :, b * channels : (b + 1) * channels] = kernel_ref[
                layer, tap : tap + channels, :
            ]


def map_grad(shift_ref, delta, grad_ref, base, dilation, cells, cols, channels, factor):
    for a in range(3):
        part = lax.dot_general(
            shift_ref[a * dilation * cols : a * dilation * cols + cells, :],
            delta,
            (((0,), (0,)), ((), ())),
            preferred_element_type=jnp.float32,
        )
        start = base + a * 3 * channels
        grad_ref[start : start + 3 * channels, :] = part * factor


def step_kernel(plan, *refs):
    count, strip, cols, channels, fan_scale, factor, split = plan
    pieces, kernel_ref = (refs[:count], refs[count])
    if split:
        result_ref, input_ref, send_ref, keep_ref = refs[count + 1 : count + 5]
        scratch = refs[count + 5 :]
    else:
        result_ref, input_ref, grad_out = refs[count + 1 : count + 4]
        scratch = refs[count + 4 :]
    sample, cot, shift_one, shift_two, shift_back, flip, pre, grad, stage = scratch
    height, rows = (count * strip, strip * cols)
    cells = height * cols
    where = lax.axis_index("space")
    for k in range(count):
        spot = (where ^ k) if split else k
        place = pl.ds(pl.multiple_of(spot * rows, rows), rows)
        sample[place, :] = pieces[k][0].astype(jnp.float32)
        cot[place, :] = pieces[k][1].astype(jnp.float32)

    spread(sample[...], shift_one, 1, height, cols)
    pre_one = conv(shift_one, kernel_ref, 0, 1, cells, cols, channels) * fan_scale
    sig = sigmoid(pre_one)
    slope_one = slope_of(pre_one, sig)
    hidden = (pre_one * sig).astype(jnp.bfloat16).astype(jnp.float32)
    sample[...] = hidden
    spread(hidden, shift_two, 2, height, cols)
    pre_two = conv(shift_two, kernel_ref, 1, 2, cells, cols, channels) * fan_scale
    sig = sigmoid(pre_two)
    pre[...] = pre_two * sig
    own = pl.ds(pl.multiple_of(where * rows, rows), rows)
    result_ref[...] = (pre[own, :] + sample[own, :]).astype(jnp.bfloat16)
    delta_two = (cot[...] * slope_of(pre_two, sig)).astype(jnp.bfloat16)
    spread(delta_two.astype(jnp.float32), shift_back, 2, height, cols)
    flip_into(kernel_ref, 1, flip, channels)
    mid_grad = back_conv(shift_back, flip, 2, cells, cols) * fan_scale + cot[...]
    delta_one = (mid_grad * slope_one).astype(jnp.bfloat16)
    taps_len = 9 * channels
    map_grad(shift_two, delta_two, grad, taps_len, 2, cells, cols, channels, factor)
    map_grad(shift_one, delta_one, grad, 0, 1, cells, cols, channels, factor)
    if split:
        dp_count, piece = split
        side = lax.rem(lax.axis_index("dp"), 2)
        for layer in range(2):
            for z in range(dp_count // 2):
                spot = (layer * dp_count // 2 + z) * piece
                for out, core in ((stage, 1 - side), (keep_ref, side)):
                    start = layer * taps_len + ((2 * z + core) * count + where) * piece
                    out[spot : spot + piece, :] = grad[pl.ds(start, piece), :]
        send_ref[...] = stage[...].astype(jnp.bfloat16)
    else:
        grad_out[...] = grad[...].reshape(grad_out.shape).astype(grad_out.dtype)

    sample[...] = delta_one.astype(jnp.float32)
    flip_into(kernel_ref, 0, flip, channels)
    spread(sample[...], shift_one, 1, height, cols)
    total = None
    for a in range(3):
        start = pl.multiple_of(where * rows + a * cols, cols)
        part = lax.dot_general(
            shift_one[pl.ds(start, rows), :],
            flip[a],
            (((1,), (1,)), ((), ())),
            preferred_element_type=jnp.float32,
        )
        total = part if total is None else total + part
    input_ref[...] = (total * fan_scale).astype(jnp.bfloat16)


def vmem_call(body, outs, scratch=(), name=None, flops=0):
    spec = pl.BlockSpec(memory_space=pltpu.VMEM)

    def call(*args):
        return pl.pallas_call(
            body,
            out_shape=outs,
            in_specs=[spec] * len(args),
            out_specs=jax.tree.map(lambda _: spec, outs),
            scratch_shapes=list(scratch),
            name=name,
            cost_estimate=pl.CostEstimate(flops=flops, bytes_accessed=0, transcendentals=0),
        )(*args)

    return call


def sample_step(pieces, weights, strip, cols, split, pixel_total):
    channels = weights.shape[-1]
    count = len(pieces)
    height = count * strip
    cells = height * cols
    fan_scale = (9.0 * channels) ** (-0.5)
    factor = fan_scale * (9.0 * channels / pixel_total) ** 0.5
    rows = strip * cols
    outs = [jax.ShapeDtypeStruct((rows, channels), jnp.bfloat16)] * 2
    if split:
        length = split[0] * split[1]
        outs.append(jax.ShapeDtypeStruct((length, channels), jnp.bfloat16))
        outs.append(jax.ShapeDtypeStruct((length, channels), jnp.float32))
    else:
        length = 8
        outs.append(jax.ShapeDtypeStruct((2, 9 * channels, channels), jnp.bfloat16))
    scratch = [
        pltpu.VMEM((cells, channels), jnp.float32),
        pltpu.VMEM((cells, channels), jnp.float32),
        pltpu.VMEM((cells + 2 * cols, 3 * channels), jnp.bfloat16),
        pltpu.VMEM((cells + 4 * cols, 3 * channels), jnp.bfloat16),
        pltpu.VMEM((cells + 4 * cols, 3 * channels), jnp.bfloat16),
        pltpu.VMEM((3, channels, 3 * channels), jnp.bfloat16),
        pltpu.VMEM((cells, channels), jnp.float32),
        pltpu.VMEM((2 * 9 * channels, channels), jnp.float32),
        pltpu.VMEM((length, channels), jnp.float32),
    ]
    plan = (count, strip, cols, channels, fan_scale, factor, split)
    body = functools.partial(step_kernel, plan)
    return vmem_call(body, tuple(outs), scratch, "sample_step")(*pieces, weights)


def update_kernel(zs, piece, *refs):
    own_ref, far_ref = refs[:2]
    bases = refs[2 : 2 + zs]
    weight_ref, grad_ref, total, stage = refs[2 + zs :]
    here = lax.axis_index("dp") // 2
    total[...] = own_ref[...].astype(jnp.float32) + far_ref[...].astype(jnp.float32)
    for layer in range(2):
        for k in range(zs):
            z = here ^ k
            place = pl.ds((layer * zs + z) * piece, piece)
            value = total[place, :]
            if k == 0:
                grad_ref[layer] = value
            stage[place, :] = bases[k][layer] - learn_rate * value
    weight_ref[...] = stage[...].astype(jnp.bfloat16)


def place_kernel(zs, count, piece, *refs):
    parts, out_ref, stage, whole = (refs[:-3], refs[-3], refs[-2], refs[-1])
    where = lax.axis_index("space")
    side = lax.rem(lax.axis_index("dp"), 2)
    layer_len = zs * 2 * count * piece
    for core_flip in range(2):
        for k in range(count):
            stage[...] = parts[core_flip * count + k][...].astype(jnp.float32)
            for layer in range(2):
                for z in range(zs):
                    chunk = (2 * z + (side ^ core_flip)) * count + (where ^ k)
                    whole[pl.ds(layer * layer_len + chunk * piece, piece), :] = stage[
                        (layer * zs + z) * piece : (layer * zs + z + 1) * piece, :
                    ]
    out_ref[...] = whole[...].reshape(out_ref.shape).astype(jnp.bfloat16)


def swap(value, axis, bit):
    size = lax.axis_size(axis)
    return lax.ppermute(value, axis, [(i, i ^ bit) for i in range(size)])


def power(n):
    return n & (n - 1) == 0


def local(fields, cotangent, weights, master, momentum):
    _, strip, cols, channels = fields.shape
    layers = weights.shape[0]
    dp_count = lax.axis_size("dp")
    space_count = lax.axis_size("space")
    rows = strip * cols
    taps_len = 9 * channels
    shard_len = master.shape[1]
    pixel_total = dp_count * space_count * fields.shape[0] * rows
    pair = jnp.concatenate([fields, cotangent], axis=0).reshape(2, rows, channels)
    zs = dp_count // 2
    quick = (
        power(space_count)
        and power(dp_count)
        and 2 <= dp_count
        and zs <= space_count
        and shard_len % channels == 0
    )

    def maps(result, input_grad):
        shape = (1, strip, cols, channels)
        return result.reshape(shape), input_grad.reshape(shape)

    if not quick:
        both = lax.all_gather(pair, "space", axis=0)
        pieces = [both[k] for k in range(space_count)]
        result, input_grad, grads = sample_step(pieces, weights, strip, cols, None, pixel_total)
        blocks = grads.reshape(layers, dp_count, space_count, shard_len)
        quarter = lax.dynamic_index_in_dim(
            blocks, lax.axis_index("space"), axis=2, keepdims=False
        )
        swapped = lax.all_to_all(quarter.transpose(1, 0, 2), "dp", 0, 0, tiled=True)
        gradient = swapped.astype(jnp.float32).sum(axis=0)
        momentum_next = momentum_rate * momentum + gradient
        master_next = master - learn_rate * momentum_next
        gathered = lax.all_gather(master_next.astype(jnp.bfloat16), ("dp", "space"), axis=0)
        weights_next = gathered.transpose(1, 0, 2).reshape(layers, taps_len, channels)
        return *maps(result, input_grad), momentum_next, master_next, weights_next

    piece = shard_len // channels
    length = dp_count * piece
    base = (master - learn_rate * momentum_rate * momentum).reshape(layers, piece, channels)
    pieces = [pair] + [swap(pair, "space", k) for k in range(1, space_count)]
    bases = [base] + [swap(base, "dp", 2 * k) for k in range(1, zs)]
    split = (dp_count, piece)
    result, input_grad, send, keep = sample_step(
        pieces, weights, strip, cols, split, pixel_total
    )
    total = (keep + swap(send, "dp", 1).astype(jnp.float32)).astype(jnp.bfloat16)
    far = None
    bit = 2
    while bit < dp_count:
        far = swap(total, "dp", bit)
        bit *= 2
        if bit < dp_count:
            total = (total.astype(jnp.float32) + far.astype(jnp.float32)).astype(jnp.bfloat16)
    if far is None:
        far = jnp.zeros_like(total)
    update = vmem_call(
        functools.partial(update_kernel, zs, piece),
        (
            jax.ShapeDtypeStruct((length, channels), jnp.bfloat16),
            jax.ShapeDtypeStruct((layers, piece, channels), jnp.float32),
        ),
        [pltpu.VMEM((length, channels), jnp.float32)] * 2,
        "update",
    )
    new_piece, own_grad = update(total, far, *bases)
    near = [new_piece] + [swap(new_piece, "space", k) for k in range(1, space_count)]
    other = [swap(value, "dp", 1) for value in near]
    place = vmem_call(
        functools.partial(place_kernel, zs, space_count, piece),
        jax.ShapeDtypeStruct((layers, taps_len, channels), jnp.bfloat16),
        [
            pltpu.VMEM((length, channels), jnp.float32),
            pltpu.VMEM((layers * taps_len, channels), jnp.float32),
        ],
        "place",
    )
    weights_next = place(*near, *other)
    gradient = own_grad.reshape(layers, shard_len)
    momentum_next = momentum_rate * momentum + gradient
    master_next = master - learn_rate * momentum_next
    return *maps(result, input_grad), momentum_next, master_next, weights_next


def solution(mesh):
    split = P("dp", "space", None, None)
    shard = P(None, ("dp", "space"))
    return jax.shard_map(
        local,
        mesh=mesh,
        in_specs=(split, split, P(), shard, shard),
        out_specs=(split, split, shard, shard, P()),
        check_vma=False,
    )
```

time: 114 us -> 50.9 us (0.45)
  blocking collectives: 81.9 us -> 0 us
  waiting for transfers between devices: 0.01 us -> 17.3 us
  local copies, waits for them, and re-layouts: 15.3 us -> 3.19 us
  starting transfers between devices: 4.88 us -> 16.8 us
  Pallas kernels: 0 us -> 9.08 us
  matrix products: 6.93 us -> 0 us
    all_gather x2 -> x0, blocking collectives: 81.9 us -> none  [the longest x1 70.9 us: local(): lax.all_gather(master_next.astype(jnp.bfloat16), ('dp', 'space'), axis=0)]
    ppermute x0 -> x16, waiting for transfers between devices: none -> 17.3 us  [swap(): return lax.ppermute(value, axis, [(i, i ^ bit) for i in range(size)])]
    ppermute x0 -> x16, starting transfers between devices: none -> 16.8 us  [swap(): return lax.ppermute(value, axis, [(i, i ^ bit) for i in range(size)])]
    pallas_call x0 -> x3, Pallas kernels: none -> 9.08 us  [call(): pl.pallas_call(body, out_shape=outs, in_specs=[spec] * len(args), out_spe...]
    dot_general x6 -> x0, matrix products: 6.93 us -> none  [the longest x1 1.91 us: local(): jnp.dot(own(back_one), flipped(weights[0]), preferred_element_type=jnp.fl...]
    unnamed x50 -> x38, local copies, waits for them, and re-layouts: 8.49 us -> 3.16 us
    all_to_all x1 -> x0, starting transfers between devices: 4.88 us -> none  [local(): swapped = lax.all_to_all(quarter.transpose(1, 0, 2), 'dp', 0, 0, tiled=True)]
    transpose x6 -> x0, local copies, waits for them, and re-layouts: 1.98 us -> none  [the longest x4 1.15 us: flipped(): return kernel.reshape(3, 3, channels, channels)[::-1, ::-1].transpose(0,...]
  transfers between devices with their start and end apart: 1 -> 16, of which waited for: 0 -> 10; matrix products, arithmetic and copies ran while one was open for 9% -> 3% of each run, Pallas kernels for 0% -> 0%
where the time goes in v2:
time: 50.9 us; the launch traced here: 50.5 us
  waiting for transfers between devices  17.3 us (34%)
  starting transfers between devices  16.8 us (33%)
  Pallas kernels  9.08 us (18%)
  other arithmetic  3.3 us (6%)
  local copies, waits for them, and re-layouts  3.19 us (6%)
  between operations  0.82 us (2%)
    ppermute x16, waiting for transfers between devices, swap(): return lax.ppermute(value, axis, [(i, i ^ bit) for i in range(size)])  17.3 us
    ppermute x16, starting transfers between devices, swap(): return lax.ppermute(value, axis, [(i, i ^ bit) for i in range(size)])  16.8 us
    pallas_call x3, Pallas kernels, call(): pl.pallas_call(body, out_shape=outs, in_specs=[spec] * len(args), out_spe...  9.08 us
    unnamed x38, local copies, waits for them, and re-layouts  3.16 us
    sub x1, other arithmetic, local(): master_next = master - learn_rate * momentum_next  1.48 us
  transfers between devices with their start and end apart: 16, of which 10 were waited for; matrix products, arithmetic and copies ran while one was open for 3% of the time, Pallas kernels for 0%

profile of v2, /device:TPU:0, one launch (start us, length us, event | category | flops | bytes accessed | tf_op | source)
XLA Modules:
  0.0 50.5 jit_solution(4935078742548013208)
XLA Ops:
  0.6 0.8 %pad_maximum_fusion = bf16[2,2,96,128]{3,2,1,0:T(8,128)(2,1)S(1)} fusion(bf16[1,2,96,128]{3,2,1,0:T(8,128)(2,1)} %param.6, bf16[1,2,96,128]{3,2,1,0:T(8,128)(2,1)} %param.5), kind=kLoop, calls=%fused_computation.2 | loop fusion | flops 49152 | bytes 196608 | tf_op jit(solution)/shard_map/concatenate | solution.py:255
  1.5 0.0 copy-start
  1.5 3.0 %collective-permute-start = (bf16[2,192,128]{2,1,0:T(8,128)(2,1)S(1)}, bf16[2,192,128]{2,1,0:T(8,128)(2,1)S(1)}, u32[]{:S(2)}, u32[]{:S(2)}) collective-permute-start(bf16[2,192,128]{2,1,0:T(8,128)(2,1)S(1)} %bitcast.7), channel_id=1, source_target_pairs={{0,1},{1,0},{2,3},{3,2},{4,5},{5,4},{6,7},{7,6},{8,9},{9,8},{10,11... | collective-permute-start | bytes 294920 | tf_op jit(solution)/shard_map/ppermute | solution.py:239
  4.5 1.5 %collective-permute-start.1 = (bf16[2,192,128]{2,1,0:T(8,128)(2,1)S(1)}, bf16[2,192,128]{2,1,0:T(8,128)(2,1)S(1)}, u32[]{:S(2)}, u32[]{:S(2)}) collective-permute-start(bf16[2,192,128]{2,1,0:T(8,128)(2,1)S(1)} %bitcast.8), channel_id=1, source_target_pairs={{0,2},{1,3},{2,0},{3,1},{4,6},{5,7},{6,4},{7,5},{8,10},{9,11},{10,... | collective-permute-start | bytes 294920 | tf_op jit(solution)/shard_map/ppermute | solution.py:239
  6.0 0.0 collective-permute-start.2
  6.1 1.5 %collective-permute-done.refs_1_ = bf16[2,192,128]{2,1,0:T(8,128)(2,1)S(1)} collective-permute-done((bf16[2,192,128]{2,1,0:T(8,128)(2,1)S(1)}, bf16[2,192,128]{2,1,0:T(8,128)(2,1)S(1)}, u32[]{:S(2)}, u32[]{:S(2)}) %collective-permute-start) | collective-permute-done | bytes 98336 | tf_op jit(solution)/shard_map/ppermute | solution.py:239
  7.6 2.6 %collective-permute-done.1.refs_2_ = bf16[2,192,128]{2,1,0:T(8,128)(2,1)S(1)} collective-permute-done((bf16[2,192,128]{2,1,0:T(8,128)(2,1)S(1)}, bf16[2,192,128]{2,1,0:T(8,128)(2,1)S(1)}, u32[]{:S(2)}, u32[]{:S(2)}) %collective-permute-start.1) | collective-permute-done | bytes 98336 | tf_op jit(solution)/shard_map/ppermute | solution.py:239
  10.2 1.4 %collective-permute-done.2.refs_3_ = bf16[2,192,128]{2,1,0:T(8,128)(2,1)S(1)} collective-permute-done((bf16[2,192,128]{2,1,0:T(8,128)(2,1)S(1)}, bf16[2,192,128]{2,1,0:T(8,128)(2,1)S(1)}, u32[]{:S(2)}, u32[]{:S(2)}) %collective-permute-start.2) | collective-permute-done | bytes 98336 | tf_op jit(solution)/shard_map/ppermute | solution.py:239
  11.5 0.0 copy-done
  11.5 0.0 copy-done.5
  11.6 0.0 copy-done.6
  11.6 0.0 copy-start.7
  11.6 0.6 %copy-done.7 = bf16[2,192,128]{2,1,0:T(8,128)(2,1)} copy-done((bf16[2,192,128]{2,1,0:T(8,128)(2,1)}, bf16[2,192,128]{2,1,0:T(8,128)(2,1)S(1)}, u32[]{:S(2)}) %copy-start.7) | copy-done | bytes 98328
  12.2 5.3 %sample_step.1 = (bf16[192,128]{1,0:T(8,128)(2,1)}, bf16[192,128]{1,0:T(8,128)(2,1)}, bf16[288,128]{1,0:T(8,128)(2,1)}, f32[288,128]{1,0:T(8,128)}) custom-call(bf16[2,192,128]{2,1,0:T(8,128)(2,1)} %bitcast.10, bf16[2,192,128]{2,1,0:T(8,128)(2,1)} %copy-done.5, bf16[2,192,128]{2,1,0:T(8,128)(2,1)} %copy-done.6, bf16[2,192,128]{2,1,0:T(8,128)(2,1)} %copy-done.7, ...), custom_call_target="tpu_custom_call" | custom-call | tf_op jit(solution)/shard_map/sample_step/pallas_call | solution.py:158
  17.5 0.0 collective-permute-start.3
  17.5 1.5 %collective-permute-done.3 = bf16[288,128]{1,0:T(8,128)(2,1)S(1)} collective-permute-done((bf16[288,128]{1,0:T(8,128)(2,1)}, bf16[288,128]{1,0:T(8,128)(2,1)S(1)}, u32[]{:S(2)}, u32[]{:S(2)}) %collective-permute-start.3) | collective-permute-done | bytes 73760 | tf_op jit(solution)/shard_map/ppermute | solution.py:239
  18.9 0.9 %add_convert_fusion.1 = bf16[288,128]{1,0:T(8,128)(2,1)S(1)} fusion(f32[288,128]{1,0:T(8,128)} %get-tuple-element.13, bf16[288,128]{1,0:T(8,128)(2,1)S(1)} %collective-permute-done.3), kind=kLoop, calls=%fused_computation.1 | loop fusion | flops 110592 | bytes 294912 | tf_op jit(solution)/shard_map/convert_element_type | solution.py:294
  19.9 0.0 copy-start.3
  19.9 0.0 copy-start.4
  19.9 1.6 %collective-permute-start.4 = (bf16[288,128]{1,0:T(8,128)(2,1)S(1)}, bf16[288,128]{1,0:T(8,128)(2,1)S(1)}, u32[]{:S(2)}, u32[]{:S(2)}) collective-permute-start(bf16[288,128]{1,0:T(8,128)(2,1)S(1)} %add_convert_fusion.1), channel_id=1, source_target_pairs={{0,8},{4,12},{8,0},{12,4},{16,24},{20,28},{24,16},{28,20},{1,9},{5... | collective-permute-start | bytes 221192 | tf_op jit(solution)/shard_map/ppermute | solution.py:239
  21.5 2.8 %collective-permute-done.4 = bf16[288,128]{1,0:T(8,128)(2,1)S(1)} collective-permute-done((bf16[288,128]{1,0:T(8,128)(2,1)S(1)}, bf16[288,128]{1,0:T(8,128)(2,1)S(1)}, u32[]{:S(2)}, u32[]{:S(2)}) %collective-permute-start.4) | collective-permute-done | bytes 73760 | tf_op jit(solution)/shard_map/ppermute | solution.py:239
  24.3 0.0 copy-start.1
  24.4 2.6 %collective-permute-start.5 = (bf16[288,128]{1,0:T(8,128)(2,1)S(1)}, bf16[288,128]{1,0:T(8,128)(2,1)S(1)}, u32[]{:S(2)}, u32[]{:S(2)}) collective-permute-start(bf16[288,128]{1,0:T(8,128)(2,1)S(1)} %add_convert_fusion.refs_0_), channel_id=1, source_target_pairs={{0,16},{4,20},{8,24},{12,28},{16,0},{20,4},{24,8},{28,12},{1,17},{... | collective-permute-start | bytes 221192 | tf_op jit(solution)/shard_map/ppermute | solution.py:239
  27.0 0.0 copy-done.3
  27.0 0.0 copy-done.4
  27.1 0.0 copy-done.1
  27.1 0.0 copy-start.2
  27.1 1.6 %collective-permute-start.6 = (f32[2,36,128]{2,1,0:T(8,128)S(1)}, f32[2,36,128]{2,1,0:T(8,128)S(1)}, u32[]{:S(2)}, u32[]{:S(2)}) collective-permute-start(f32[2,36,128]{2,1,0:T(8,128)S(1)} %reshape.28.refs_2_), channel_id=1, source_target_pairs={{0,8},{4,12},{8,0},{12,4},{16,24},{20,28},{24,16},{28,20},{1,9},{5... | collective-permute-start | bytes 110600 | tf_op jit(solution)/shard_map/ppermute | solution.py:239
  28.7 0.4 collective-permute-start.7
  29.1 2.4 %collective-permute-start.8 = (f32[2,36,128]{2,1,0:T(8,128)S(1)}, f32[2,36,128]{2,1,0:T(8,128)S(1)}, u32[]{:S(2)}, u32[]{:S(2)}) collective-permute-start(f32[2,36,128]{2,1,0:T(8,128)S(1)} %reshape.28.refs_2_), channel_id=1, source_target_pairs={{0,24},{4,28},{8,16},{12,20},{16,8},{20,12},{24,0},{28,4},{1,25},{... | collective-permute-start | bytes 110600 | tf_op jit(solution)/shard_map/ppermute | solution.py:239
  31.5 0.0 collective-permute-done.6.refs_3_
  31.6 2.4 %collective-permute-done.7.refs_4_ = f32[2,36,128]{2,1,0:T(8,128)S(1)} collective-permute-done((f32[2,36,128]{2,1,0:T(8,128)S(1)}, f32[2,36,128]{2,1,0:T(8,128)S(1)}, u32[]{:S(2)}, u32[]{:S(2)}) %collective-permute-start.7) | collective-permute-done | bytes 36896 | tf_op jit(solution)/shard_map/ppermute | solution.py:239
  34.0 1.0 %collective-permute-done.8.refs_5_ = f32[2,36,128]{2,1,0:T(8,128)S(1)} collective-permute-done((f32[2,36,128]{2,1,0:T(8,128)S(1)}, f32[2,36,128]{2,1,0:T(8,128)S(1)}, u32[]{:S(2)}, u32[]{:S(2)}) %collective-permute-start.8) | collective-permute-done | bytes 36896 | tf_op jit(solution)/shard_map/ppermute | solution.py:239
  34.9 0.0 collective-permute-done.5.refs_1_
  34.9 0.0 copy-done.2
  34.9 0.0 copy-done.16
  35.0 0.0 copy-done.17
  35.0 0.6 %copy-done.18 = f32[2,36,128]{2,1,0:T(8,128)} copy-done((f32[2,36,128]{2,1,0:T(8,128)}, f32[2,36,128]{2,1,0:T(8,128)S(1)}, u32[]{:S(2)}) %copy-start.18) | copy-done | bytes 36888
  35.6 0.6 %copy-done.15 = bf16[288,128]{1,0:T(8,128)(2,1)} copy-done((bf16[288,128]{1,0:T(8,128)(2,1)}, bf16[288,128]{1,0:T(8,128)(2,1)S(1)}, u32[]{:S(2)}) %copy-start.15) | copy-done | bytes 73752
  36.2 1.6 %update.1 = (bf16[288,128]{1,0:T(8,128)(2,1)}, f32[2,36,128]{2,1,0:T(8,128)}) custom-call(bf16[288,128]{1,0:T(8,128)(2,1)} %copy-done.1, bf16[288,128]{1,0:T(8,128)(2,1)} %copy-done.15, f32[2,36,128]{2,1,0:T(8,128)} %copy-done.2, f32[2,36,128]{2,1,0:T(8,128)} %copy-done.16, f32[2,36,128]{2,1,0:T(8,128)} %copy-done.17, f32[2,36,128]{2,1,0:T(8,128)} %copy-done.18), custom_call_target="tpu_custom_call" | custom-call | tf_op jit(solution)/shard_map/update/pallas_call | solution.py:158
  37.8 0.7 %collective-permute-start.9 = (bf16[288,128]{1,0:T(8,128)(2,1)}, bf16[288,128]{1,0:T(8,128)(2,1)S(1)}, u32[]{:S(2)}, u32[]{:S(2)}) collective-permute-start(bf16[288,128]{1,0:T(8,128)(2,1)} %get-tuple-element.16.refs_0_), channel_id=1, source_target_pairs={{0,1},{1,0},{2,3},{3,2},{4,5},{5,4},{6,7},{7,6},{8,9},{9,8},{10,11... | collective-permute-start | bytes 221192 | tf_op jit(solution)/shard_map/ppermute | solution.py:239
  38.5 1.6 %collective-permute-start.10 = (bf16[288,128]{1,0:T(8,128)(2,1)}, bf16[288,128]{1,0:T(8,128)(2,1)S(1)}, u32[]{:S(2)}, u32[]{:S(2)}) collective-permute-start(bf16[288,128]{1,0:T(8,128)(2,1)} %get-tuple-element.16.refs_0_), channel_id=1, source_target_pairs={{0,2},{1,3},{2,0},{3,1},{4,6},{5,7},{6,4},{7,5},{8,10},{9,11},{10,... | collective-permute-start | bytes 221192 | tf_op jit(solution)/shard_map/ppermute | solution.py:239
  40.1 1.3 %collective-permute-start.11 = (bf16[288,128]{1,0:T(8,128)(2,1)}, bf16[288,128]{1,0:T(8,128)(2,1)S(1)}, u32[]{:S(2)}, u32[]{:S(2)}) collective-permute-start(bf16[288,128]{1,0:T(8,128)(2,1)} %get-tuple-element.16.refs_0_), channel_id=1, source_target_pairs={{0,3},{1,2},{2,1},{3,0},{4,7},{5,6},{6,5},{7,4},{8,11},{9,10},{10,... | collective-permute-start | bytes 221192 | tf_op jit(solution)/shard_map/ppermute | solution.py:239
  41.3 0.0 collective-permute-start.12
  41.3 1.1 %collective-permute-done.9.refs_1_ = bf16[288,128]{1,0:T(8,128)(2,1)S(1)} collective-permute-done((bf16[288,128]{1,0:T(8,128)(2,1)}, bf16[288,128]{1,0:T(8,128)(2,1)S(1)}, u32[]{:S(2)}, u32[]{:S(2)}) %collective-permute-start.9) | collective-permute-done | bytes 73760 | tf_op jit(solution)/shard_map/ppermute | solution.py:239
  42.4 0.0 collective-permute-start.13
  42.4 0.7 %collective-permute-done.10.refs_2_ = bf16[288,128]{1,0:T(8,128)(2,1)S(1)} collective-permute-done((bf16[288,128]{1,0:T(8,128)(2,1)}, bf16[288,128]{1,0:T(8,128)(2,1)S(1)}, u32[]{:S(2)}, u32[]{:S(2)}) %collective-permute-start.10) | collective-permute-done | bytes 73760 | tf_op jit(solution)/shard_map/ppermute | solution.py:239
  43.1 0.0 collective-permute-start.14
  43.1 2.5 %collective-permute-done.11.refs_3_ = bf16[288,128]{1,0:T(8,128)(2,1)S(1)} collective-permute-done((bf16[288,128]{1,0:T(8,128)(2,1)}, bf16[288,128]{1,0:T(8,128)(2,1)S(1)}, u32[]{:S(2)}, u32[]{:S(2)}) %collective-permute-start.11) | collective-permute-done | bytes 73760 | tf_op jit(solution)/shard_map/ppermute | solution.py:239
  45.5 0.0 collective-permute-start.15
  45.5 1.5 %multiply_subtract_fusion = (f32[2,4608]{1,0:T(2,128)}, f32[2,4608]{1,0:T(2,128)}) fusion(f32[2,4608]{1,0:T(2,128)S(1)} %copy-done.3, f32[1,2,36,128]{3,2,1,0:T(8,128)} %bitcast.11, f32[2,4608]{1,0:T(2,128)S(1)} %copy-done.4), kind=kLoop, calls=%fused_computation.4 | loop fusion | flops 36864 | bytes 184320 | tf_op jit(solution)/shard_map/sub | solution.py:328
  47.0 0.0 copy-done.8
  47.0 0.0 copy-done.9
  47.0 0.0 collective-permute-done.12.refs_4_
  47.0 0.0 copy-start.11
  47.0 0.0 collective-permute-done.13.refs_5_
  47.1 0.0 collective-permute-done.14.refs_6_
  47.1 0.0 collective-permute-done.15.refs_7_
  47.1 0.0 copy-done.10
  47.1 0.6 %copy-done.11 = bf16[288,128]{1,0:T(8,128)(2,1)} copy-done((bf16[288,128]{1,0:T(8,128)(2,1)}, bf16[288,128]{1,0:T(8,128)(2,1)S(1)}, u32[]{:S(2)}) %copy-start.11) | copy-done | bytes 73752
  47.7 0.0 copy-done.12
  47.7 0.0 copy-done.13
  47.7 0.6 %copy-done.14 = bf16[288,128]{1,0:T(8,128)(2,1)} copy-done((bf16[288,128]{1,0:T(8,128)(2,1)}, bf16[288,128]{1,0:T(8,128)(2,1)S(1)}, u32[]{:S(2)}) %copy-start.14) | copy-done | bytes 73752
  48.3 2.2 %place.1 = bf16[2,1152,128]{2,1,0:T(8,128)(2,1)} custom-call(bf16[288,128]{1,0:T(8,128)(2,1)} %get-tuple-element.16.refs_0_, bf16[288,128]{1,0:T(8,128)(2,1)} %copy-done.8, bf16[288,128]{1,0:T(8,128)(2,1)} %copy-done.9, bf16[288,128]{1,0:T(8,128)(2,1)} %copy-done.10, bf16[288,128]{1,0:T(8,128)(2,1)} %copy-done.11, bf16[288,128]{1,0:T(8,128)(2,1)} %copy-done.12, ...), custom_call_target="tpu_custom_call" | custom-call | tf_op jit(solution)/shard_map/place/pallas_call | solution.py:158
  (15 shorter events, 0.1 us)
Async XLA Ops:
  1.5 10.1 %copy-start = (bf16[2,2,96,128]{3,2,1,0:T(8,128)(2,1)}, bf16[2,2,96,128]{3,2,1,0:T(8,128)(2,1)S(1)}, u32[]{:S(2)}) copy-start(bf16[2,2,96,128]{3,2,1,0:T(8,128)(2,1)S(1)} %pad_maximum_fusion) | copy-start | bytes 294916
  1.5 6.1 %collective-permute-start = (bf16[2,192,128]{2,1,0:T(8,128)(2,1)S(1)}, bf16[2,192,128]{2,1,0:T(8,128)(2,1)S(1)}, u32[]{:S(2)}, u32[]{:S(2)}) collective-permute-start(bf16[2,192,128]{2,1,0:T(8,128)(2,1)S(1)} %bitcast.7), channel_id=1, source_target_pairs={{0,1},{1,0},{2,3},{3,2},{4,5},{5,4},{6,7},{7,6},{8,9},{9,8},{10,11... | collective-permute-start | bytes 294920 | tf_op jit(solution)/shard_map/ppermute | solution.py:239
  4.5 5.7 %collective-permute-start.1 = (bf16[2,192,128]{2,1,0:T(8,128)(2,1)S(1)}, bf16[2,192,128]{2,1,0:T(8,128)(2,1)S(1)}, u32[]{:S(2)}, u32[]{:S(2)}) collective-permute-start(bf16[2,192,128]{2,1,0:T(8,128)(2,1)S(1)} %bitcast.8), channel_id=1, source_target_pairs={{0,2},{1,3},{2,0},{3,1},{4,6},{5,7},{6,4},{7,5},{8,10},{9,11},{10,... | collective-permute-start | bytes 294920 | tf_op jit(solution)/shard_map/ppermute | solution.py:239
  6.0 5.5 %collective-permute-start.2 = (bf16[2,192,128]{2,1,0:T(8,128)(2,1)S(1)}, bf16[2,192,128]{2,1,0:T(8,128)(2,1)S(1)}, u32[]{:S(2)}, u32[]{:S(2)}) collective-permute-start(bf16[2,192,128]{2,1,0:T(8,128)(2,1)S(1)} %bitcast.9), channel_id=1, source_target_pairs={{0,3},{1,2},{2,1},{3,0},{4,7},{5,6},{6,5},{7,4},{8,11},{9,10},{10,... | collective-permute-start | bytes 294920 | tf_op jit(solution)/shard_map/ppermute | solution.py:239
  7.6 4.0 %copy-start.5 = (bf16[2,192,128]{2,1,0:T(8,128)(2,1)}, bf16[2,192,128]{2,1,0:T(8,128)(2,1)S(1)}, u32[]{:S(2)}) copy-start(bf16[2,192,128]{2,1,0:T(8,128)(2,1)S(1)} %collective-permute-done.refs_1_) | copy-start | bytes 294916
  10.2 1.4 %copy-start.6 = (bf16[2,192,128]{2,1,0:T(8,128)(2,1)}, bf16[2,192,128]{2,1,0:T(8,128)(2,1)S(1)}, u32[]{:S(2)}) copy-start(bf16[2,192,128]{2,1,0:T(8,128)(2,1)S(1)} %collective-permute-done.1.refs_2_) | copy-start | bytes 294916
  11.6 0.6 %copy-start.7 = (bf16[2,192,128]{2,1,0:T(8,128)(2,1)}, bf16[2,192,128]{2,1,0:T(8,128)(2,1)S(1)}, u32[]{:S(2)}) copy-start(bf16[2,192,128]{2,1,0:T(8,128)(2,1)S(1)} %collective-permute-done.2.refs_3_) | copy-start | bytes 294916
  17.5 1.5 %collective-permute-start.3 = (bf16[288,128]{1,0:T(8,128)(2,1)}, bf16[288,128]{1,0:T(8,128)(2,1)S(1)}, u32[]{:S(2)}, u32[]{:S(2)}) collective-permute-start(bf16[288,128]{1,0:T(8,128)(2,1)} %get-tuple-element.14), channel_id=1, source_target_pairs={{0,4},{4,0},{8,12},{12,8},{16,20},{20,16},{24,28},{28,24},{1,5},{5... | collective-permute-start | bytes 221192 | tf_op jit(solution)/shard_map/ppermute | solution.py:239
  19.9 7.1 %copy-start.3 = (f32[2,4608]{1,0:T(2,128)S(1)}, f32[2,4608]{1,0:T(2,128)}, u32[]{:S(2)}) copy-start(f32[2,4608]{1,0:T(2,128)} %param.8) | copy-start | bytes 110596
  19.9 7.1 %copy-start.4 = (f32[2,4608]{1,0:T(2,128)S(1)}, f32[2,4608]{1,0:T(2,128)}, u32[]{:S(2)}) copy-start(f32[2,4608]{1,0:T(2,128)} %param.9) | copy-start | bytes 110596
  19.9 4.4 %collective-permute-start.4 = (bf16[288,128]{1,0:T(8,128)(2,1)S(1)}, bf16[288,128]{1,0:T(8,128)(2,1)S(1)}, u32[]{:S(2)}, u32[]{:S(2)}) collective-permute-start(bf16[288,128]{1,0:T(8,128)(2,1)S(1)} %add_convert_fusion.1), channel_id=1, source_target_pairs={{0,8},{4,12},{8,0},{12,4},{16,24},{20,28},{24,16},{28,20},{1,9},{5... | collective-permute-start | bytes 221192 | tf_op jit(solution)/shard_map/ppermute | solution.py:239
  24.3 2.7 %copy-start.1 = (bf16[288,128]{1,0:T(8,128)(2,1)}, bf16[288,128]{1,0:T(8,128)(2,1)S(1)}, u32[]{:S(2)}) copy-start(bf16[288,128]{1,0:T(8,128)(2,1)S(1)} %add_convert_fusion.refs_0_) | copy-start | bytes 221188
  24.4 10.6 %collective-permute-start.5 = (bf16[288,128]{1,0:T(8,128)(2,1)S(1)}, bf16[288,128]{1,0:T(8,128)(2,1)S(1)}, u32[]{:S(2)}, u32[]{:S(2)}) collective-permute-start(bf16[288,128]{1,0:T(8,128)(2,1)S(1)} %add_convert_fusion.refs_0_), channel_id=1, source_target_pairs={{0,16},{4,20},{8,24},{12,28},{16,0},{20,4},{24,8},{28,12},{1,17},{... | collective-permute-start | bytes 221192 | tf_op jit(solution)/shard_map/ppermute | solution.py:239
  27.1 7.9 %copy-start.2 = (f32[2,36,128]{2,1,0:T(8,128)}, f32[2,36,128]{2,1,0:T(8,128)S(1)}, u32[]{:S(2)}) copy-start(f32[2,36,128]{2,1,0:T(8,128)S(1)} %reshape.28.refs_2_) | copy-start | bytes 110596
  27.1 4.5 %collective-permute-start.6 = (f32[2,36,128]{2,1,0:T(8,128)S(1)}, f32[2,36,128]{2,1,0:T(8,128)S(1)}, u32[]{:S(2)}, u32[]{:S(2)}) collective-permute-start(f32[2,36,128]{2,1,0:T(8,128)S(1)} %reshape.28.refs_2_), channel_id=1, source_target_pairs={{0,8},{4,12},{8,0},{12,4},{16,24},{20,28},{24,16},{28,20},{1,9},{5... | collective-permute-start | bytes 110600 | tf_op jit(solution)/shard_map/ppermute | solution.py:239
  28.7 5.2 %collective-permute-start.7 = (f32[2,36,128]{2,1,0:T(8,128)S(1)}, f32[2,36,128]{2,1,0:T(8,128)S(1)}, u32[]{:S(2)}, u32[]{:S(2)}) collective-permute-start(f32[2,36,128]{2,1,0:T(8,128)S(1)} %reshape.28.refs_2_), channel_id=1, source_target_pairs={{0,16},{4,20},{8,24},{12,28},{16,0},{20,4},{24,8},{28,12},{1,17},{... | collective-permute-start | bytes 110600 | tf_op jit(solution)/shard_map/ppermute | solution.py:239
  29.1 5.8 %collective-permute-start.8 = (f32[2,36,128]{2,1,0:T(8,128)S(1)}, f32[2,36,128]{2,1,0:T(8,128)S(1)}, u32[]{:S(2)}, u32[]{:S(2)}) collective-permute-start(f32[2,36,128]{2,1,0:T(8,128)S(1)} %reshape.28.refs_2_), channel_id=1, source_target_pairs={{0,24},{4,28},{8,16},{12,20},{16,8},{20,12},{24,0},{28,4},{1,25},{... | collective-permute-start | bytes 110600 | tf_op jit(solution)/shard_map/ppermute | solution.py:239
  31.6 3.4 %copy-start.16 = (f32[2,36,128]{2,1,0:T(8,128)}, f32[2,36,128]{2,1,0:T(8,128)S(1)}, u32[]{:S(2)}) copy-start(f32[2,36,128]{2,1,0:T(8,128)S(1)} %collective-permute-done.6.refs_3_) | copy-start | bytes 110596
  34.0 1.0 %copy-start.17 = (f32[2,36,128]{2,1,0:T(8,128)}, f32[2,36,128]{2,1,0:T(8,128)S(1)}, u32[]{:S(2)}) copy-start(f32[2,36,128]{2,1,0:T(8,128)S(1)} %collective-permute-done.7.refs_4_) | copy-start | bytes 110596
  34.9 0.6 %copy-start.18 = (f32[2,36,128]{2,1,0:T(8,128)}, f32[2,36,128]{2,1,0:T(8,128)S(1)}, u32[]{:S(2)}) copy-start(f32[2,36,128]{2,1,0:T(8,128)S(1)} %collective-permute-done.8.refs_5_) | copy-start | bytes 110596
  35.6 0.6 %copy-start.15 = (bf16[288,128]{1,0:T(8,128)(2,1)}, bf16[288,128]{1,0:T(8,128)(2,1)S(1)}, u32[]{:S(2)}) copy-start(bf16[288,128]{1,0:T(8,128)(2,1)S(1)} %collective-permute-done.5.refs_1_) | copy-start | bytes 221188
  37.8 4.6 %collective-permute-start.9 = (bf16[288,128]{1,0:T(8,128)(2,1)}, bf16[288,128]{1,0:T(8,128)(2,1)S(1)}, u32[]{:S(2)}, u32[]{:S(2)}) collective-permute-start(bf16[288,128]{1,0:T(8,128)(2,1)} %get-tuple-element.16.refs_0_), channel_id=1, source_target_pairs={{0,1},{1,0},{2,3},{3,2},{4,5},{5,4},{6,7},{7,6},{8,9},{9,8},{10,11... | collective-permute-start | bytes 221192 | tf_op jit(solution)/shard_map/ppermute | solution.py:239
  38.5 4.6 %collective-permute-start.10 = (bf16[288,128]{1,0:T(8,128)(2,1)}, bf16[288,128]{1,0:T(8,128)(2,1)S(1)}, u32[]{:S(2)}, u32[]{:S(2)}) collective-permute-start(bf16[288,128]{1,0:T(8,128)(2,1)} %get-tuple-element.16.refs_0_), channel_id=1, source_target_pairs={{0,2},{1,3},{2,0},{3,1},{4,6},{5,7},{6,4},{7,5},{8,10},{9,11},{10,... | collective-permute-start | bytes 221192 | tf_op jit(solution)/shard_map/ppermute | solution.py:239
  40.1 5.5 %collective-permute-start.11 = (bf16[288,128]{1,0:T(8,128)(2,1)}, bf16[288,128]{1,0:T(8,128)(2,1)S(1)}, u32[]{:S(2)}, u32[]{:S(2)}) collective-permute-start(bf16[288,128]{1,0:T(8,128)(2,1)} %get-tuple-element.16.refs_0_), channel_id=1, source_target_pairs={{0,3},{1,2},{2,1},{3,0},{4,7},{5,6},{6,5},{7,4},{8,11},{9,10},{10,... | collective-permute-start | bytes 221192 | tf_op jit(solution)/shard_map/ppermute | solution.py:239
  41.3 5.7 %collective-permute-start.12 = (bf16[288,128]{1,0:T(8,128)(2,1)}, bf16[288,128]{1,0:T(8,128)(2,1)S(1)}, u32[]{:S(2)}, u32[]{:S(2)}) collective-permute-start(bf16[288,128]{1,0:T(8,128)(2,1)} %get-tuple-element.16.refs_0_), channel_id=1, source_target_pairs={{0,4},{4,0},{8,12},{12,8},{16,20},{20,16},{24,28},{28,24},{1,5},{5... | collective-permute-start | bytes 221192 | tf_op jit(solution)/shard_map/ppermute | solution.py:239
  42.4 4.6 %copy-start.8 = (bf16[288,128]{1,0:T(8,128)(2,1)}, bf16[288,128]{1,0:T(8,128)(2,1)S(1)}, u32[]{:S(2)}) copy-start(bf16[288,128]{1,0:T(8,128)(2,1)S(1)} %collective-permute-done.9.refs_1_) | copy-start | bytes 221188
  42.4 4.6 %collective-permute-start.13 = (bf16[288,128]{1,0:T(8,128)(2,1)S(1)}, bf16[288,128]{1,0:T(8,128)(2,1)S(1)}, u32[]{:S(2)}, u32[]{:S(2)}) collective-permute-start(bf16[288,128]{1,0:T(8,128)(2,1)S(1)} %collective-permute-done.9.refs_1_), channel_id=1, source_target_pairs={{0,4},{4,0},{8,12},{12,8},{16,20},{20,16},{24,28},{28,24},{1,5},{5... | collective-permute-start | bytes 221192 | tf_op jit(solution)/shard_map/ppermute | solution.py:239
  43.1 4.0 %copy-start.9 = (bf16[288,128]{1,0:T(8,128)(2,1)}, bf16[288,128]{1,0:T(8,128)(2,1)S(1)}, u32[]{:S(2)}) copy-start(bf16[288,128]{1,0:T(8,128)(2,1)S(1)} %collective-permute-done.10.refs_2_) | copy-start | bytes 221188
  43.1 4.0 %collective-permute-start.14 = (bf16[288,128]{1,0:T(8,128)(2,1)S(1)}, bf16[288,128]{1,0:T(8,128)(2,1)S(1)}, u32[]{:S(2)}, u32[]{:S(2)}) collective-permute-start(bf16[288,128]{1,0:T(8,128)(2,1)S(1)} %collective-permute-done.10.refs_2_), channel_id=1, source_target_pairs={{0,4},{4,0},{8,12},{12,8},{16,20},{20,16},{24,28},{28,24},{1,5},{5... | collective-permute-start | bytes 221192 | tf_op jit(solution)/shard_map/ppermute | solution.py:239
  45.5 1.6 %copy-start.10 = (bf16[288,128]{1,0:T(8,128)(2,1)}, bf16[288,128]{1,0:T(8,128)(2,1)S(1)}, u32[]{:S(2)}) copy-start(bf16[288,128]{1,0:T(8,128)(2,1)S(1)} %collective-permute-done.11.refs_3_) | copy-start | bytes 221188
  45.5 1.6 %collective-permute-start.15 = (bf16[288,128]{1,0:T(8,128)(2,1)S(1)}, bf16[288,128]{1,0:T(8,128)(2,1)S(1)}, u32[]{:S(2)}, u32[]{:S(2)}) collective-permute-start(bf16[288,128]{1,0:T(8,128)(2,1)S(1)} %collective-permute-done.11.refs_3_), channel_id=1, source_target_pairs={{0,4},{4,0},{8,12},{12,8},{16,20},{20,16},{24,28},{28,24},{1,5},{5... | collective-permute-start | bytes 221192 | tf_op jit(solution)/shard_map/ppermute | solution.py:239
  47.0 0.6 %copy-start.11 = (bf16[288,128]{1,0:T(8,128)(2,1)}, bf16[288,128]{1,0:T(8,128)(2,1)S(1)}, u32[]{:S(2)}) copy-start(bf16[288,128]{1,0:T(8,128)(2,1)S(1)} %collective-permute-done.12.refs_4_) | copy-start | bytes 221188
  47.0 0.6 %copy-start.12 = (bf16[288,128]{1,0:T(8,128)(2,1)}, bf16[288,128]{1,0:T(8,128)(2,1)S(1)}, u32[]{:S(2)}) copy-start(bf16[288,128]{1,0:T(8,128)(2,1)S(1)} %collective-permute-done.13.refs_5_) | copy-start | bytes 221188
  47.1 0.6 %copy-start.13 = (bf16[288,128]{1,0:T(8,128)(2,1)}, bf16[288,128]{1,0:T(8,128)(2,1)S(1)}, u32[]{:S(2)}) copy-start(bf16[288,128]{1,0:T(8,128)(2,1)S(1)} %collective-permute-done.14.refs_6_) | copy-start | bytes 221188
  47.7 0.6 %copy-start.14 = (bf16[288,128]{1,0:T(8,128)(2,1)}, bf16[288,128]{1,0:T(8,128)(2,1)S(1)}, u32[]{:S(2)}) copy-start(bf16[288,128]{1,0:T(8,128)(2,1)S(1)} %collective-permute-done.15.refs_7_) | copy-start | bytes 221188

commit v3 on v2

--- a/solution.py
+++ b/solution.py
@@ -7,9 +7,9 @@
 from jax.experimental.pallas import tpu as pltpu
 from jax.sharding import PartitionSpec as P
 
+
 momentum_rate = 0.9
 learn_rate = 0.1
-lane = 128
 
 
 def sigmoid(value):
@@ -151,7 +151,7 @@
     input_ref[...] = (total * fan_scale).astype(jnp.bfloat16)
 
 
-def vmem_call(body, outs, scratch=(), name=None, flops=0):
+def vmem_call(body, outs, scratch=(), limit=8):
     spec = pl.BlockSpec(memory_space=pltpu.VMEM)
 
     def call(*args):
@@ -161,8 +161,7 @@
             in_specs=[spec] * len(args),
             out_specs=jax.tree.map(lambda _: spec, outs),
             scratch_shapes=list(scratch),
-            name=name,
-            cost_estimate=pl.CostEstimate(flops=flops, bytes_accessed=0, transcendentals=0),
+            compiler_params=pltpu.CompilerParams(vmem_limit_bytes=limit << 20),
         )(*args)
 
     return call
@@ -197,7 +196,7 @@
     ]
     plan = (count, strip, cols, channels, fan_scale, factor, split)
     body = functools.partial(step_kernel, plan)
-    return vmem_call(body, tuple(outs), scratch, "sample_step")(*pieces, weights)
+    return vmem_call(body, tuple(outs), scratch, 20)(*pieces, weights)
 
 
 def update_kernel(zs, piece, *refs):
@@ -243,7 +242,7 @@
     return n & (n - 1) == 0
 
 
-def local(fields, cotangent, weights, master, momentum):
+def block(fields, cotangent, weights, master, momentum):
     _, strip, cols, channels = fields.shape
     layers = weights.shape[0]
     dp_count = lax.axis_size("dp")
@@ -288,9 +287,7 @@
     pieces = [pair] + [swap(pair, "space", k) for k in range(1, space_count)]
     bases = [base] + [swap(base, "dp", 2 * k) for k in range(1, zs)]
     split = (dp_count, piece)
-    result, input_grad, send, keep = sample_step(
-        pieces, weights, strip, cols, split, pixel_total
-    )
+    result, input_grad, send, keep = sample_step(pieces, weights, strip, cols, split, pixel_total)
     total = (keep + swap(send, "dp", 1).astype(jnp.float32)).astype(jnp.bfloat16)
     far = None
     bit = 2
@@ -308,7 +305,6 @@
             jax.ShapeDtypeStruct((layers, piece, channels), jnp.float32),
         ),
         [pltpu.VMEM((length, channels), jnp.float32)] * 2,
-        "update",
     )
     new_piece, own_grad = update(total, far, *bases)
     near = [new_piece] + [swap(new_piece, "space", k) for k in range(1, space_count)]
@@ -320,7 +316,6 @@
             pltpu.VMEM((length, channels), jnp.float32),
             pltpu.VMEM((layers * taps_len, channels), jnp.float32),
         ],
-        "place",
     )
     weights_next = place(*near, *other)
     gradient = own_grad.reshape(layers, shard_len)
@@ -333,7 +328,7 @@
     split = P("dp", "space", None, None)
     shard = P(None, ("dp", "space"))
     return jax.shard_map(
-        local,
+        block,
         mesh=mesh,
         in_specs=(split, split, P(), shard, shard),
         out_specs=(split, split, shard, shard, P()),

time: 50.9 us -> 42.4 us (0.83)
  Pallas kernels: 9.08 us -> 5.07 us
  local copies, waits for them, and re-layouts: 3.19 us -> 1.11 us
  other arithmetic: 3.3 us -> 1.59 us
    pallas_call x3, Pallas kernels: 9.08 us -> 5.07 us  [call(): pl.pallas_call(body, out_shape=outs, in_specs=[spec] * len(args), out_spe...]
    unnamed x38 -> x6, local copies, waits for them, and re-layouts: 3.16 us -> 1.08 us
    convert_element_type x2, other arithmetic: 0.95 us -> 0.04 us  [the longest x1 0.02 us: block(): (total.astype(jnp.float32) + far.astype(jnp.float32)).astype(jnp.bfloat16)]
    sub x2, other arithmetic: 1.51 us -> 0.71 us  [the longest x1 0.68 us: block(): master_next = master - learn_rate * momentum_next]
    ppermute x16, waiting for transfers between devices: 17.3 us -> 16.8 us  [swap(): return lax.ppermute(value, axis, [(i, i ^ bit) for i in range(size)])]
  transfers between devices with their start and end apart: 16 -> 16, of which waited for: 10 -> 11; matrix products, arithmetic and copies ran while one was open for 3% -> 2% of each run, Pallas kernels for 0% -> 0%
where the time goes in v3:
time: 42.4 us; the launch traced here: 42.1 us
  starting transfers between devices  16.9 us (40%)
  waiting for transfers between devices  16.8 us (40%)
  Pallas kernels  5.07 us (12%)
  other arithmetic  1.59 us (4%)
  local copies, waits for them, and re-layouts  1.11 us (3%)
  between operations  0.7 us (2%)
    ppermute x16, starting transfers between devices, swap(): return lax.ppermute(value, axis, [(i, i ^ bit) for i in range(size)])  16.9 us
    ppermute x16, waiting for transfers between devices, swap(): return lax.ppermute(value, axis, [(i, i ^ bit) for i in range(size)])  16.8 us
    pallas_call x3, Pallas kernels, call(): pl.pallas_call(body, out_shape=outs, in_specs=[spec] * len(args), out_spe...  5.07 us
    unnamed x6, local copies, waits for them, and re-layouts  1.08 us
  transfers between devices with their start and end apart: 16, of which 11 were waited for; matrix products, arithmetic and copies ran while one was open for 2% of the time, Pallas kernels for 0%

profile of v3, /device:TPU:0, one launch (start us, length us, event | category | flops | bytes accessed | tf_op | source)
XLA Modules:
  0.0 42.1 jit_solution(8016096798234835772)
XLA Ops:
  0.6 0.8 %pad_maximum_fusion = bf16[2,2,96,128]{3,2,1,0:T(8,128)(2,1)S(1)} fusion(bf16[1,2,96,128]{3,2,1,0:T(8,128)(2,1)} %param.6, bf16[1,2,96,128]{3,2,1,0:T(8,128)(2,1)} %param.5), kind=kLoop, calls=%fused_computation.2 | loop fusion | flops 49152 | bytes 196608 | tf_op jit(solution)/shard_map/concatenate | solution.py:254
  1.5 3.0 %collective-permute-start = (bf16[2,192,128]{2,1,0:T(8,128)(2,1)S(1)}, bf16[2,192,128]{2,1,0:T(8,128)(2,1)S(1)}, u32[]{:S(2)}, u32[]{:S(2)}) collective-permute-start(bf16[2,192,128]{2,1,0:T(8,128)(2,1)S(1)} %bitcast.7), channel_id=1, source_target_pairs={{0,1},{1,0},{2,3},{3,2},{4,5},{5,4},{6,7},{7,6},{8,9},{9,8},{10,11... | collective-permute-start | bytes 294920 | tf_op jit(solution)/shard_map/ppermute | solution.py:238
  4.5 1.5 %collective-permute-start.1 = (bf16[2,192,128]{2,1,0:T(8,128)(2,1)S(1)}, bf16[2,192,128]{2,1,0:T(8,128)(2,1)S(1)}, u32[]{:S(2)}, u32[]{:S(2)}) collective-permute-start(bf16[2,192,128]{2,1,0:T(8,128)(2,1)S(1)} %bitcast.8), channel_id=1, source_target_pairs={{0,2},{1,3},{2,0},{3,1},{4,6},{5,7},{6,4},{7,5},{8,10},{9,11},{10,... | collective-permute-start | bytes 294920 | tf_op jit(solution)/shard_map/ppermute | solution.py:238
  6.0 0.0 collective-permute-start.2
  6.0 1.5 %collective-permute-done.refs_1_ = bf16[2,192,128]{2,1,0:T(8,128)(2,1)S(1)} collective-permute-done((bf16[2,192,128]{2,1,0:T(8,128)(2,1)S(1)}, bf16[2,192,128]{2,1,0:T(8,128)(2,1)S(1)}, u32[]{:S(2)}, u32[]{:S(2)}) %collective-permute-start) | collective-permute-done | bytes 98336 | tf_op jit(solution)/shard_map/ppermute | solution.py:238
  7.6 2.6 %collective-permute-done.1.refs_2_ = bf16[2,192,128]{2,1,0:T(8,128)(2,1)S(1)} collective-permute-done((bf16[2,192,128]{2,1,0:T(8,128)(2,1)S(1)}, bf16[2,192,128]{2,1,0:T(8,128)(2,1)S(1)}, u32[]{:S(2)}, u32[]{:S(2)}) %collective-permute-start.1) | collective-permute-done | bytes 98336 | tf_op jit(solution)/shard_map/ppermute | solution.py:238
  10.2 1.4 %collective-permute-done.2.refs_3_ = bf16[2,192,128]{2,1,0:T(8,128)(2,1)S(1)} collective-permute-done((bf16[2,192,128]{2,1,0:T(8,128)(2,1)S(1)}, bf16[2,192,128]{2,1,0:T(8,128)(2,1)S(1)}, u32[]{:S(2)}, u32[]{:S(2)}) %collective-permute-start.2) | collective-permute-done | bytes 98336 | tf_op jit(solution)/shard_map/ppermute | solution.py:238
  11.5 0.0 copy-start
  11.5 1.1 %copy-done = bf16[2,1152,128]{2,1,0:T(8,128)(2,1)S(1)} copy-done((bf16[2,1152,128]{2,1,0:T(8,128)(2,1)S(1)}, bf16[2,1152,128]{2,1,0:T(8,128)(2,1)}, u32[]{:S(2)}) %copy-start) | copy-done | bytes 589848
  12.6 4.0 %shard_map.92 = (bf16[192,128]{1,0:T(8,128)(2,1)}, bf16[192,128]{1,0:T(8,128)(2,1)}, bf16[288,128]{1,0:T(8,128)(2,1)S(1)}, f32[288,128]{1,0:T(8,128)S(1)}) custom-call(bf16[2,192,128]{2,1,0:T(8,128)(2,1)S(1)} %bitcast.10, bf16[2,192,128]{2,1,0:T(8,128)(2,1)S(1)} %collective-permute-done.refs_1_, bf16[2,192,128]{2,1,0:T(8,128)(2,1)S(1)} %collective-permute-done.1.refs_2_, ...), custom_call_target="tpu_custom_call" | custom-call | tf_op jit(solution)/shard_map/pallas_call | solution.py:158
  16.6 0.0 collective-permute-start.3
  16.6 1.3 %collective-permute-done.3 = bf16[288,128]{1,0:T(8,128)(2,1)S(1)} collective-permute-done((bf16[288,128]{1,0:T(8,128)(2,1)S(1)}, bf16[288,128]{1,0:T(8,128)(2,1)S(1)}, u32[]{:S(2)}, u32[]{:S(2)}) %collective-permute-start.3) | collective-permute-done | bytes 73760 | tf_op jit(solution)/shard_map/ppermute | solution.py:238
  17.9 0.0 copy-start.1
  17.9 0.0 copy-start.2
  17.9 1.6 %collective-permute-start.4 = (bf16[288,128]{1,0:T(8,128)(2,1)S(1)}, bf16[288,128]{1,0:T(8,128)(2,1)S(1)}, u32[]{:S(2)}, u32[]{:S(2)}) collective-permute-start(bf16[288,128]{1,0:T(8,128)(2,1)S(1)} %add_convert_fusion.1), channel_id=1, source_target_pairs={{0,8},{4,12},{8,0},{12,4},{16,24},{20,28},{24,16},{28,20},{1,9},{5... | collective-permute-start | bytes 221192 | tf_op jit(solution)/shard_map/ppermute | solution.py:238
  19.5 2.8 %collective-permute-done.4 = bf16[288,128]{1,0:T(8,128)(2,1)S(1)} collective-permute-done((bf16[288,128]{1,0:T(8,128)(2,1)S(1)}, bf16[288,128]{1,0:T(8,128)(2,1)S(1)}, u32[]{:S(2)}, u32[]{:S(2)}) %collective-permute-start.4) | collective-permute-done | bytes 73760 | tf_op jit(solution)/shard_map/ppermute | solution.py:238
  22.3 2.7 %collective-permute-start.5 = (bf16[288,128]{1,0:T(8,128)(2,1)S(1)}, bf16[288,128]{1,0:T(8,128)(2,1)S(1)}, u32[]{:S(2)}, u32[]{:S(2)}) collective-permute-start(bf16[288,128]{1,0:T(8,128)(2,1)S(1)} %add_convert_fusion.refs_0_), channel_id=1, source_target_pairs={{0,16},{4,20},{8,24},{12,28},{16,0},{20,4},{24,8},{28,12},{1,17},{... | collective-permute-start | bytes 221192 | tf_op jit(solution)/shard_map/ppermute | solution.py:238
  25.0 0.0 copy-done.1
  25.0 0.0 copy-done.2
  25.1 1.6 %collective-permute-start.6 = (f32[2,36,128]{2,1,0:T(8,128)S(1)}, f32[2,36,128]{2,1,0:T(8,128)S(1)}, u32[]{:S(2)}, u32[]{:S(2)}) collective-permute-start(f32[2,36,128]{2,1,0:T(8,128)S(1)} %reshape.28.refs_2_), channel_id=1, source_target_pairs={{0,8},{4,12},{8,0},{12,4},{16,24},{20,28},{24,16},{28,20},{1,9},{5... | collective-permute-start | bytes 110600 | tf_op jit(solution)/shard_map/ppermute | solution.py:238
  26.7 0.3 collective-permute-start.7
  27.0 2.5 %collective-permute-start.8 = (f32[2,36,128]{2,1,0:T(8,128)S(1)}, f32[2,36,128]{2,1,0:T(8,128)S(1)}, u32[]{:S(2)}, u32[]{:S(2)}) collective-permute-start(f32[2,36,128]{2,1,0:T(8,128)S(1)} %reshape.28.refs_2_), channel_id=1, source_target_pairs={{0,24},{4,28},{8,16},{12,20},{16,8},{20,12},{24,0},{28,4},{1,25},{... | collective-permute-start | bytes 110600 | tf_op jit(solution)/shard_map/ppermute | solution.py:238
  29.5 0.0 collective-permute-done.6.refs_3_
  29.5 2.4 %collective-permute-done.7.refs_4_ = f32[2,36,128]{2,1,0:T(8,128)S(1)} collective-permute-done((f32[2,36,128]{2,1,0:T(8,128)S(1)}, f32[2,36,128]{2,1,0:T(8,128)S(1)}, u32[]{:S(2)}, u32[]{:S(2)}) %collective-permute-start.7) | collective-permute-done | bytes 36896 | tf_op jit(solution)/shard_map/ppermute | solution.py:238
  31.9 0.9 %collective-permute-done.8.refs_5_ = f32[2,36,128]{2,1,0:T(8,128)S(1)} collective-permute-done((f32[2,36,128]{2,1,0:T(8,128)S(1)}, f32[2,36,128]{2,1,0:T(8,128)S(1)}, u32[]{:S(2)}, u32[]{:S(2)}) %collective-permute-start.8) | collective-permute-done | bytes 36896 | tf_op jit(solution)/shard_map/ppermute | solution.py:238
  32.8 0.0 collective-permute-done.5.refs_1_
  32.9 0.7 %collective-permute-start.9 = (bf16[288,128]{1,0:T(8,128)(2,1)S(1)}, bf16[288,128]{1,0:T(8,128)(2,1)S(1)}, u32[]{:S(2)}, u32[]{:S(2)}) collective-permute-start(bf16[288,128]{1,0:T(8,128)(2,1)S(1)} %get-tuple-element.16.refs_0_), channel_id=1, source_target_pairs={{0,1},{1,0},{2,3},{3,2},{4,5},{5,4},{6,7},{7,6},{8,9},{9,8},{10,11... | collective-permute-start | bytes 221192 | tf_op jit(solution)/shard_map/ppermute | solution.py:238
  33.6 1.0 %collective-permute-start.10 = (bf16[288,128]{1,0:T(8,128)(2,1)S(1)}, bf16[288,128]{1,0:T(8,128)(2,1)S(1)}, u32[]{:S(2)}, u32[]{:S(2)}) collective-permute-start(bf16[288,128]{1,0:T(8,128)(2,1)S(1)} %get-tuple-element.16.refs_0_), channel_id=1, source_target_pairs={{0,2},{1,3},{2,0},{3,1},{4,6},{5,7},{6,4},{7,5},{8,10},{9,11},{10,... | collective-permute-start | bytes 221192 | tf_op jit(solution)/shard_map/ppermute | solution.py:238
  34.6 1.9 %collective-permute-start.11 = (bf16[288,128]{1,0:T(8,128)(2,1)S(1)}, bf16[288,128]{1,0:T(8,128)(2,1)S(1)}, u32[]{:S(2)}, u32[]{:S(2)}) collective-permute-start(bf16[288,128]{1,0:T(8,128)(2,1)S(1)} %get-tuple-element.16.refs_0_), channel_id=1, source_target_pairs={{0,3},{1,2},{2,1},{3,0},{4,7},{5,6},{6,5},{7,4},{8,11},{9,10},{10,... | collective-permute-start | bytes 221192 | tf_op jit(solution)/shard_map/ppermute | solution.py:238
  36.4 0.0 collective-permute-start.12
  36.5 0.9 %collective-permute-done.9.refs_1_ = bf16[288,128]{1,0:T(8,128)(2,1)S(1)} collective-permute-done((bf16[288,128]{1,0:T(8,128)(2,1)S(1)}, bf16[288,128]{1,0:T(8,128)(2,1)S(1)}, u32[]{:S(2)}, u32[]{:S(2)}) %collective-permute-start.9) | collective-permute-done | bytes 73760 | tf_op jit(solution)/shard_map/ppermute | solution.py:238
  37.3 0.0 collective-permute-start.13
  37.3 0.6 %collective-permute-done.10.refs_2_ = bf16[288,128]{1,0:T(8,128)(2,1)S(1)} collective-permute-done((bf16[288,128]{1,0:T(8,128)(2,1)S(1)}, bf16[288,128]{1,0:T(8,128)(2,1)S(1)}, u32[]{:S(2)}, u32[]{:S(2)}) %collective-permute-start.10) | collective-permute-done | bytes 73760 | tf_op jit(solution)/shard_map/ppermute | solution.py:238
  38.0 0.0 collective-permute-start.14
  38.0 1.9 %collective-permute-done.11.refs_3_ = bf16[288,128]{1,0:T(8,128)(2,1)S(1)} collective-permute-done((bf16[288,128]{1,0:T(8,128)(2,1)S(1)}, bf16[288,128]{1,0:T(8,128)(2,1)S(1)}, u32[]{:S(2)}, u32[]{:S(2)}) %collective-permute-start.11) | collective-permute-done | bytes 73760 | tf_op jit(solution)/shard_map/ppermute | solution.py:238
  39.8 0.0 collective-permute-start.15
  39.8 0.7 %multiply_subtract_fusion = (f32[2,4608]{1,0:T(2,128)}, f32[2,4608]{1,0:T(2,128)}) fusion(f32[2,4608]{1,0:T(2,128)S(1)} %copy-done.1, f32[1,2,36,128]{3,2,1,0:T(8,128)S(1)} %bitcast.11, f32[2,4608]{1,0:T(2,128)S(1)} %copy-done.2), kind=kLoop, calls=%fused_computation.4 | loop fusion | flops 36864 | bytes 184320 | tf_op jit(solution)/shard_map/sub | solution.py:323
  40.5 0.0 collective-permute-done.12.refs_4_
  40.5 0.0 collective-permute-done.13.refs_5_
  40.5 0.0 collective-permute-done.14.refs_6_
  40.5 0.6 %collective-permute-done.15.refs_7_ = bf16[288,128]{1,0:T(8,128)(2,1)S(1)} collective-permute-done((bf16[288,128]{1,0:T(8,128)(2,1)S(1)}, bf16[288,128]{1,0:T(8,128)(2,1)S(1)}, u32[]{:S(2)}, u32[]{:S(2)}) %collective-permute-start.15) | collective-permute-done | bytes 73760 | tf_op jit(solution)/shard_map/ppermute | solution.py:238
  41.1 1.1 %shard_map.94 = bf16[2,1152,128]{2,1,0:T(8,128)(2,1)} custom-call(bf16[288,128]{1,0:T(8,128)(2,1)S(1)} %get-tuple-element.16.refs_0_, bf16[288,128]{1,0:T(8,128)(2,1)S(1)} %collective-permute-done.9.refs_1_, bf16[288,128]{1,0:T(8,128)(2,1)S(1)} %collective-permute-done.10.refs_2_, bf16[288,128]{1,0:T(8,128)(2,1)S(1)} %collective-permute-done.11.refs_3_, ...), custom_call_target="tpu_custom_call" | custom-call | tf_op jit(solution)/shard_map/pallas_call | solution.py:158
  (5 shorter events, 0.2 us)
Async XLA Ops:
  1.5 6.1 %collective-permute-start = (bf16[2,192,128]{2,1,0:T(8,128)(2,1)S(1)}, bf16[2,192,128]{2,1,0:T(8,128)(2,1)S(1)}, u32[]{:S(2)}, u32[]{:S(2)}) collective-permute-start(bf16[2,192,128]{2,1,0:T(8,128)(2,1)S(1)} %bitcast.7), channel_id=1, source_target_pairs={{0,1},{1,0},{2,3},{3,2},{4,5},{5,4},{6,7},{7,6},{8,9},{9,8},{10,11... | collective-permute-start | bytes 294920 | tf_op jit(solution)/shard_map/ppermute | solution.py:238
  4.5 5.7 %collective-permute-start.1 = (bf16[2,192,128]{2,1,0:T(8,128)(2,1)S(1)}, bf16[2,192,128]{2,1,0:T(8,128)(2,1)S(1)}, u32[]{:S(2)}, u32[]{:S(2)}) collective-permute-start(bf16[2,192,128]{2,1,0:T(8,128)(2,1)S(1)} %bitcast.8), channel_id=1, source_target_pairs={{0,2},{1,3},{2,0},{3,1},{4,6},{5,7},{6,4},{7,5},{8,10},{9,11},{10,... | collective-permute-start | bytes 294920 | tf_op jit(solution)/shard_map/ppermute | solution.py:238
  6.0 5.5 %collective-permute-start.2 = (bf16[2,192,128]{2,1,0:T(8,128)(2,1)S(1)}, bf16[2,192,128]{2,1,0:T(8,128)(2,1)S(1)}, u32[]{:S(2)}, u32[]{:S(2)}) collective-permute-start(bf16[2,192,128]{2,1,0:T(8,128)(2,1)S(1)} %bitcast.9), channel_id=1, source_target_pairs={{0,3},{1,2},{2,1},{3,0},{4,7},{5,6},{6,5},{7,4},{8,11},{9,10},{10,... | collective-permute-start | bytes 294920 | tf_op jit(solution)/shard_map/ppermute | solution.py:238
  11.5 1.1 %copy-start = (bf16[2,1152,128]{2,1,0:T(8,128)(2,1)S(1)}, bf16[2,1152,128]{2,1,0:T(8,128)(2,1)}, u32[]{:S(2)}) copy-start(bf16[2,1152,128]{2,1,0:T(8,128)(2,1)} %refs_4_.1) | copy-start | bytes 1769476
  16.6 1.3 %collective-permute-start.3 = (bf16[288,128]{1,0:T(8,128)(2,1)S(1)}, bf16[288,128]{1,0:T(8,128)(2,1)S(1)}, u32[]{:S(2)}, u32[]{:S(2)}) collective-permute-start(bf16[288,128]{1,0:T(8,128)(2,1)S(1)} %get-tuple-element.14), channel_id=1, source_target_pairs={{0,4},{4,0},{8,12},{12,8},{16,20},{20,16},{24,28},{28,24},{1,5},{5... | collective-permute-start | bytes 221192 | tf_op jit(solution)/shard_map/ppermute | solution.py:238
  17.9 7.1 %copy-start.1 = (f32[2,4608]{1,0:T(2,128)S(1)}, f32[2,4608]{1,0:T(2,128)}, u32[]{:S(2)}) copy-start(f32[2,4608]{1,0:T(2,128)} %param.8) | copy-start | bytes 110596
  17.9 7.1 %copy-start.2 = (f32[2,4608]{1,0:T(2,128)S(1)}, f32[2,4608]{1,0:T(2,128)}, u32[]{:S(2)}) copy-start(f32[2,4608]{1,0:T(2,128)} %param.9) | copy-start | bytes 110596
  17.9 4.4 %collective-permute-start.4 = (bf16[288,128]{1,0:T(8,128)(2,1)S(1)}, bf16[288,128]{1,0:T(8,128)(2,1)S(1)}, u32[]{:S(2)}, u32[]{:S(2)}) collective-permute-start(bf16[288,128]{1,0:T(8,128)(2,1)S(1)} %add_convert_fusion.1), channel_id=1, source_target_pairs={{0,8},{4,12},{8,0},{12,4},{16,24},{20,28},{24,16},{28,20},{1,9},{5... | collective-permute-start | bytes 221192 | tf_op jit(solution)/shard_map/ppermute | solution.py:238
  22.3 10.5 %collective-permute-start.5 = (bf16[288,128]{1,0:T(8,128)(2,1)S(1)}, bf16[288,128]{1,0:T(8,128)(2,1)S(1)}, u32[]{:S(2)}, u32[]{:S(2)}) collective-permute-start(bf16[288,128]{1,0:T(8,128)(2,1)S(1)} %add_convert_fusion.refs_0_), channel_id=1, source_target_pairs={{0,16},{4,20},{8,24},{12,28},{16,0},{20,4},{24,8},{28,12},{1,17},{... | collective-permute-start | bytes 221192 | tf_op jit(solution)/shard_map/ppermute | solution.py:238
  25.1 4.5 %collective-permute-start.6 = (f32[2,36,128]{2,1,0:T(8,128)S(1)}, f32[2,36,128]{2,1,0:T(8,128)S(1)}, u32[]{:S(2)}, u32[]{:S(2)}) collective-permute-start(f32[2,36,128]{2,1,0:T(8,128)S(1)} %reshape.28.refs_2_), channel_id=1, source_target_pairs={{0,8},{4,12},{8,0},{12,4},{16,24},{20,28},{24,16},{28,20},{1,9},{5... | collective-permute-start | bytes 110600 | tf_op jit(solution)/shard_map/ppermute | solution.py:238
  26.7 5.2 %collective-permute-start.7 = (f32[2,36,128]{2,1,0:T(8,128)S(1)}, f32[2,36,128]{2,1,0:T(8,128)S(1)}, u32[]{:S(2)}, u32[]{:S(2)}) collective-permute-start(f32[2,36,128]{2,1,0:T(8,128)S(1)} %reshape.28.refs_2_), channel_id=1, source_target_pairs={{0,16},{4,20},{8,24},{12,28},{16,0},{20,4},{24,8},{28,12},{1,17},{... | collective-permute-start | bytes 110600 | tf_op jit(solution)/shard_map/ppermute | solution.py:238
  27.0 5.8 %collective-permute-start.8 = (f32[2,36,128]{2,1,0:T(8,128)S(1)}, f32[2,36,128]{2,1,0:T(8,128)S(1)}, u32[]{:S(2)}, u32[]{:S(2)}) collective-permute-start(f32[2,36,128]{2,1,0:T(8,128)S(1)} %reshape.28.refs_2_), channel_id=1, source_target_pairs={{0,24},{4,28},{8,16},{12,20},{16,8},{20,12},{24,0},{28,4},{1,25},{... | collective-permute-start | bytes 110600 | tf_op jit(solution)/shard_map/ppermute | solution.py:238
  32.9 4.4 %collective-permute-start.9 = (bf16[288,128]{1,0:T(8,128)(2,1)S(1)}, bf16[288,128]{1,0:T(8,128)(2,1)S(1)}, u32[]{:S(2)}, u32[]{:S(2)}) collective-permute-start(bf16[288,128]{1,0:T(8,128)(2,1)S(1)} %get-tuple-element.16.refs_0_), channel_id=1, source_target_pairs={{0,1},{1,0},{2,3},{3,2},{4,5},{5,4},{6,7},{7,6},{8,9},{9,8},{10,11... | collective-permute-start | bytes 221192 | tf_op jit(solution)/shard_map/ppermute | solution.py:238
  33.6 4.4 %collective-permute-start.10 = (bf16[288,128]{1,0:T(8,128)(2,1)S(1)}, bf16[288,128]{1,0:T(8,128)(2,1)S(1)}, u32[]{:S(2)}, u32[]{:S(2)}) collective-permute-start(bf16[288,128]{1,0:T(8,128)(2,1)S(1)} %get-tuple-element.16.refs_0_), channel_id=1, source_target_pairs={{0,2},{1,3},{2,0},{3,1},{4,6},{5,7},{6,4},{7,5},{8,10},{9,11},{10,... | collective-permute-start | bytes 221192 | tf_op jit(solution)/shard_map/ppermute | solution.py:238
  34.6 5.3 %collective-permute-start.11 = (bf16[288,128]{1,0:T(8,128)(2,1)S(1)}, bf16[288,128]{1,0:T(8,128)(2,1)S(1)}, u32[]{:S(2)}, u32[]{:S(2)}) collective-permute-start(bf16[288,128]{1,0:T(8,128)(2,1)S(1)} %get-tuple-element.16.refs_0_), channel_id=1, source_target_pairs={{0,3},{1,2},{2,1},{3,0},{4,7},{5,6},{6,5},{7,4},{8,11},{9,10},{10,... | collective-permute-start | bytes 221192 | tf_op jit(solution)/shard_map/ppermute | solution.py:238
  36.4 4.1 %collective-permute-start.12 = (bf16[288,128]{1,0:T(8,128)(2,1)S(1)}, bf16[288,128]{1,0:T(8,128)(2,1)S(1)}, u32[]{:S(2)}, u32[]{:S(2)}) collective-permute-start(bf16[288,128]{1,0:T(8,128)(2,1)S(1)} %get-tuple-element.16.refs_0_), channel_id=1, source_target_pairs={{0,4},{4,0},{8,12},{12,8},{16,20},{20,16},{24,28},{28,24},{1,5},{5... | collective-permute-start | bytes 221192 | tf_op jit(solution)/shard_map/ppermute | solution.py:238
  37.3 3.2 %collective-permute-start.13 = (bf16[288,128]{1,0:T(8,128)(2,1)S(1)}, bf16[288,128]{1,0:T(8,128)(2,1)S(1)}, u32[]{:S(2)}, u32[]{:S(2)}) collective-permute-start(bf16[288,128]{1,0:T(8,128)(2,1)S(1)} %collective-permute-done.9.refs_1_), channel_id=1, source_target_pairs={{0,4},{4,0},{8,12},{12,8},{16,20},{20,16},{24,28},{28,24},{1,5},{5... | collective-permute-start | bytes 221192 | tf_op jit(solution)/shard_map/ppermute | solution.py:238
  38.0 2.6 %collective-permute-start.14 = (bf16[288,128]{1,0:T(8,128)(2,1)S(1)}, bf16[288,128]{1,0:T(8,128)(2,1)S(1)}, u32[]{:S(2)}, u32[]{:S(2)}) collective-permute-start(bf16[288,128]{1,0:T(8,128)(2,1)S(1)} %collective-permute-done.10.refs_2_), channel_id=1, source_target_pairs={{0,4},{4,0},{8,12},{12,8},{16,20},{20,16},{24,28},{28,24},{1,5},{5... | collective-permute-start | bytes 221192 | tf_op jit(solution)/shard_map/ppermute | solution.py:238
  39.8 1.3 %collective-permute-start.15 = (bf16[288,128]{1,0:T(8,128)(2,1)S(1)}, bf16[288,128]{1,0:T(8,128)(2,1)S(1)}, u32[]{:S(2)}, u32[]{:S(2)}) collective-permute-start(bf16[288,128]{1,0:T(8,128)(2,1)S(1)} %collective-permute-done.11.refs_3_), channel_id=1, source_target_pairs={{0,4},{4,0},{8,12},{12,8},{16,20},{20,16},{24,28},{28,24},{1,5},{5... | collective-permute-start | bytes 221192 | tf_op jit(solution)/shard_map/ppermute | solution.py:238

commit v4 on v3

v4 whole, which is shorter than its diff:
```python
import functools

import jax
import jax.numpy as jnp
from jax import lax
from jax.experimental import pallas as pl
from jax.experimental.pallas import tpu as pltpu
from jax.sharding import PartitionSpec as P


momentum_rate = 0.9
learn_rate = 0.1
spare = 8


def sigmoid(value):
    return 1.0 / (1.0 + jnp.exp(-value))


def slope_of(value, sig):
    return sig * (1.0 + value * (1.0 - sig))


def moved(rows, steps):
    if steps == 0:
        return rows
    edge = jnp.zeros((abs(steps), rows.shape[1]), rows.dtype)
    if steps > 0:
        return jnp.concatenate([edge, rows[:-steps]], axis=0)
    return jnp.concatenate([rows[-steps:], edge], axis=0)


def spread(rows, dilation, cols):
    count, channels = rows.shape
    cube = rows.reshape(count // cols, cols, channels)
    column = lax.broadcasted_iota(jnp.int32, cube.shape, 1)
    right = jnp.where(column < dilation, 0.0, pltpu.roll(cube, dilation, 1))
    left = jnp.where(column >= cols - dilation, 0.0, pltpu.roll(cube, cols - dilation, 1))
    parts = [part.reshape(rows.shape).astype(jnp.bfloat16) for part in (right, cube, left)]
    return jnp.concatenate(parts, axis=1)


def fold(wide, dilation, cols, channels):
    total = wide[:, channels : 2 * channels]
    step = dilation * cols
    total = total + moved(wide[:, :channels], step)
    return total + moved(wide[:, 2 * channels :], -step)


def conv(shifted, kernel, dilation, cols, channels):
    wide = jnp.dot(shifted, kernel, preferred_element_type=jnp.float32)
    return fold(wide, dilation, cols, channels)


def back_conv(shifted, kernel, dilation, cols, channels):
    wide = lax.dot_general(
        shifted, kernel, (((1,), (1,)), ((), ())), preferred_element_type=jnp.float32
    )
    return fold(wide, dilation, cols, channels)


def map_grad(shifted, delta, grad_ref, base, dilation, cols, channels, factor):
    step = dilation * cols
    turned = jnp.concatenate([moved(delta, (1 - a) * -step) for a in range(3)], axis=1)
    wide = lax.dot_general(
        shifted, turned, (((0,), (0,)), ((), ())), preferred_element_type=jnp.float32
    )
    for a in range(3):
        for b in range(3):
            start = base + (a * 3 + b) * channels
            grad_ref[start : start + channels, :] = (
                wide[b * channels : (b + 1) * channels, a * channels : (a + 1) * channels]
                * factor
            )


def ahead_matrix(weight_ref, layer):
    channels = weight_ref.shape[-1]

    def tap(a, b):
        start = (a * 3 + b) * channels
        return weight_ref[layer, start : start + channels, :]

    return jnp.concatenate(
        [jnp.concatenate([tap(a, b) for a in range(3)], axis=1) for b in range(3)], axis=0
    )


def back_matrix(weight_ref, layer):
    channels = weight_ref.shape[-1]

    def tap(a, b):
        start = ((2 - a) * 3 + 2 - b) * channels
        return weight_ref[layer, start : start + channels, :]

    return jnp.concatenate(
        [jnp.concatenate([tap(a, b) for b in range(3)], axis=1) for a in range(3)], axis=0
    )


def touch_kernel(weight_ref, mark_ref):
    mark_ref[...] = jnp.zeros(mark_ref.shape, mark_ref.dtype)


def step_kernel(plan, *refs):
    count, strip, cols, channels, fan_scale, factor, split = plan
    pieces, weight_ref = (refs[:count], refs[count])
    outs, scratch = (refs[count + 2 : -6], refs[-6:])
    sample, cot, smooth, edge, grad, stage = scratch
    rows = strip * cols
    cells = count * rows
    where = lax.axis_index("space")
    for k in range(count):
        spot = (where ^ k) if split else k
        place = pl.ds(pl.multiple_of(spot * rows, rows), rows)
        sample[place, :] = pieces[k][0].reshape(rows, channels).astype(jnp.float32)
        cot[place, :] = pieces[k][1].reshape(rows, channels).astype(jnp.float32)

    one = spread(sample[...], 1, cols)
    pre_one = conv(one, ahead_matrix(weight_ref, 0), 1, cols, channels) * fan_scale
    sig = sigmoid(pre_one)
    slope_one = slope_of(pre_one, sig)
    hidden = (pre_one * sig).astype(jnp.bfloat16).astype(jnp.float32)
    two = spread(hidden, 2, cols)
    pre_two = conv(two, ahead_matrix(weight_ref, 1), 2, cols, channels) * fan_scale
    sig = sigmoid(pre_two)
    smooth[...] = pre_two * sig + hidden
    delta_two = (cot[...] * slope_of(pre_two, sig)).astype(jnp.bfloat16)
    back = spread(delta_two.astype(jnp.float32), 2, cols)
    mid_grad = back_conv(back, back_matrix(weight_ref, 1), 2, cols, channels) * fan_scale + cot[...]
    delta_one = (mid_grad * slope_one).astype(jnp.bfloat16)
    taps_len = 9 * channels
    map_grad(two, delta_two, grad, taps_len, 2, cols, channels, factor)
    map_grad(one, delta_one, grad, 0, 1, cols, channels, factor)

    edge[:cols, :] = jnp.zeros((cols, channels), jnp.bfloat16)
    edge[cols : cols + cells, :] = delta_one
    edge[cols + cells :, :] = jnp.zeros((cols, channels), jnp.bfloat16)
    start = pl.multiple_of(where * rows, rows)
    outs[0][...] = smooth[pl.ds(start, rows), :].astype(jnp.bfloat16)
    outs[1][...] = edge[pl.ds(start, rows + 2 * cols), :]
    if split:
        dp_count, piece = split
        side = lax.rem(lax.axis_index("dp"), 2)
        length = dp_count * piece
        for core in range(2):
            chosen = side if core else 1 - side
            for layer in range(2):
                for z in range(dp_count // 2):
                    spot = core * length + (layer * dp_count // 2 + z) * piece
                    start = layer * taps_len + ((2 * z + chosen) * count + where) * piece
                    stage[spot : spot + piece, :] = grad[pl.ds(start, piece), :]
        outs[2][...] = stage[:length, :].astype(jnp.bfloat16)
        outs[3][...] = stage[length : 2 * length, :]
    else:
        outs[2][...] = (
            grad[: 2 * taps_len, :].reshape(outs[2].shape).astype(outs[2].dtype)
        )


def finish_kernel(plan, smooth_ref, edge_ref, weight_ref, result_ref, input_ref):
    cols, channels, fan_scale = plan
    rows = result_ref.shape[0]
    result_ref[...] = smooth_ref[...]
    shifted = spread(edge_ref[...].astype(jnp.float32), 1, cols)
    wide = back_conv(shifted, back_matrix(weight_ref, 0), 1, cols, channels)
    input_ref[...] = (wide[cols : cols + rows, :] * fan_scale).astype(jnp.bfloat16)


def update_kernel(zs, piece, *refs):
    own_ref, far_ref = refs[:2]
    bases = refs[2 : 2 + zs]
    weight_ref, grad_ref, total, stage = refs[2 + zs :]
    here = lax.axis_index("dp") // 2
    length = own_ref.shape[0]
    total[:length, :] = own_ref[...].astype(jnp.float32) + far_ref[...].astype(jnp.float32)
    for layer in range(2):
        for k in range(zs):
            place = pl.ds((layer * zs + (here ^ k)) * piece, piece)
            value = total[place, :]
            if k == 0:
                grad_ref[layer] = value
            stage[place, :] = bases[k][layer] - learn_rate * value
    weight_ref[...] = stage[:length, :].astype(jnp.bfloat16)


def place_kernel(zs, count, piece, far, *refs):
    parts = refs[:count]
    out_ref, stage, whole, half, sems = refs[-5:]
    where = lax.axis_index("space")
    side = lax.rem(lax.axis_index("dp"), 2)
    side = 1 - side if far else side
    run = count * piece
    copies = []
    for layer in range(2):
        for k in range(count):
            rows = slice(layer * zs * piece, (layer + 1) * zs * piece)
            stage[rows, :] = parts[k][rows, :].astype(jnp.float32)
            for z in range(zs):
                spot = (layer * zs + z) * piece
                whole[pl.ds((layer * zs + z) * run + (where ^ k) * piece, piece), :] = stage[
                    spot : spot + piece, :
                ]
        for z in range(zs):
            rows = slice((layer * zs + z) * run, (layer * zs + z + 1) * run)
            half[rows, :] = whole[rows, :].astype(jnp.bfloat16)
            start = pl.multiple_of((2 * z + side) * run, run)
            copies.append(
                pltpu.make_async_copy(
                    half.at[rows],
                    out_ref.at[layer, pl.ds(start, run)],
                    sems.at[layer * zs + z],
                )
            )
            copies[-1].start()
    for copy in copies:
        copy.wait()


def place(parts, held, zs, piece, dims):
    count = len(parts)
    length = 2 * zs * piece
    channels = dims[-1]
    spec = pl.BlockSpec(memory_space=pltpu.VMEM)
    anywhere = pl.BlockSpec(memory_space=pl.ANY)
    extra = [] if held is None else [held]
    return pl.pallas_call(
        functools.partial(place_kernel, zs, count, piece, held is not None),
        out_shape=shape(dims),
        in_specs=[spec] * count + [anywhere] * len(extra),
        out_specs=anywhere,
        input_output_aliases={count: 0} if extra else {},
        scratch_shapes=[
            pltpu.VMEM((length + spare, channels), jnp.float32),
            pltpu.VMEM((count * length + spare, channels), jnp.float32),
            pltpu.VMEM((count * length, channels), jnp.bfloat16),
            pltpu.SemaphoreType.DMA((2 * zs,)),
        ],
        name="place_far" if extra else "place_near",
        compiler_params=pltpu.CompilerParams(vmem_limit_bytes=8 << 20),
    )(*parts, *extra)


def vmem_call(body, outs, scratch=(), limit=8):
    spec = pl.BlockSpec(memory_space=pltpu.VMEM)

    def call(*args):
        return pl.pallas_call(
            body,
            out_shape=outs,
            in_specs=[spec] * len(args),
            out_specs=jax.tree.map(lambda _: spec, outs),
            scratch_shapes=list(scratch),
            compiler_params=pltpu.CompilerParams(vmem_limit_bytes=limit << 20),
        )(*args)

    return call


def shape(dims, dtype=jnp.bfloat16):
    return jax.ShapeDtypeStruct(dims, dtype)


def touch(weights):
    return pl.pallas_call(
        touch_kernel,
        out_shape=shape((16, weights.shape[-1])),
        in_specs=[pl.BlockSpec(memory_space=pl.ANY)],
        out_specs=pl.BlockSpec(memory_space=pltpu.VMEM),
        name="touch",
        compiler_params=pltpu.CompilerParams(vmem_limit_bytes=54784 << 10),
    )(weights)


def sample_step(pieces, weights, mark, strip, cols, split, pixel_total):
    channels = weights.shape[-1]
    count = len(pieces)
    rows = strip * cols
    cells = count * rows
    fan_scale = (9.0 * channels) ** (-0.5)
    factor = fan_scale * (9.0 * channels / pixel_total) ** 0.5
    outs = [shape((rows, channels)), shape((rows + 2 * cols, channels))]
    length = spare
    if split:
        length = split[0] * split[1]
        outs += [shape((length, channels)), shape((length, channels), jnp.float32)]
    else:
        outs.append(shape((2, 9 * channels, channels)))
    scratch = [
        pltpu.VMEM((cells, channels), jnp.float32),
        pltpu.VMEM((cells, channels), jnp.float32),
        pltpu.VMEM((cells, channels), jnp.float32),
        pltpu.VMEM((cells + 2 * cols, channels), jnp.bfloat16),
        pltpu.VMEM((18 * channels + spare, channels), jnp.float32),
        pltpu.VMEM((2 * length + spare, channels), jnp.float32),
    ]
    plan = (count, strip, cols, channels, fan_scale, factor, split)
    body = functools.partial(step_kernel, plan)
    return vmem_call(body, tuple(outs), scratch, 24)(*pieces, weights, mark)


def finish(smooth, edge, weights, cols):
    channels = smooth.shape[-1]
    body = functools.partial(finish_kernel, (cols, channels, (9.0 * channels) ** (-0.5)))
    outs = (shape(smooth.shape), shape(smooth.shape))
    return vmem_call(body, outs, ())(smooth, edge, weights)


def swap(value, axis, bit):
    size = lax.axis_size(axis)
    return lax.ppermute(value, axis, [(i, i ^ bit) for i in range(size)])


def power(n):
    return n & (n - 1) == 0


def block(fields, cotangent, weights, master, momentum):
    _, strip, cols, channels = fields.shape
    layers = weights.shape[0]
    dp_count = lax.axis_size("dp")
    space_count = lax.axis_size("space")
    rows = strip * cols
    taps_len = 9 * channels
    shard_len = master.shape[1]
    pixel_total = dp_count * space_count * fields.shape[0] * rows
    pair = jnp.concatenate([fields, cotangent], axis=0)
    mark = touch(weights)
    zs = dp_count // 2
    quick = (
        power(space_count)
        and power(dp_count)
        and 4 <= dp_count
        and zs <= space_count
        and shard_len % channels == 0
    )

    def maps(*values):
        return [value.reshape(1, strip, cols, channels) for value in values]

    if not quick:
        both = lax.all_gather(pair, "space", axis=0)
        pieces = [both[k] for k in range(space_count)]
        smooth, edge, grads = sample_step(pieces, weights, mark, strip, cols, None, pixel_total)
        result, input_grad = finish(smooth, edge, weights, cols)
        blocks = grads.reshape(layers, dp_count, space_count, shard_len)
        quarter = lax.dynamic_index_in_dim(
            blocks, lax.axis_index("space"), axis=2, keepdims=False
        )
        swapped = lax.all_to_all(quarter.transpose(1, 0, 2), "dp", 0, 0, tiled=True)
        gradient = swapped.astype(jnp.float32).sum(axis=0)
        momentum_next = momentum_rate * momentum + gradient
        master_next = master - learn_rate * momentum_next
        gathered = lax.all_gather(master_next.astype(jnp.bfloat16), ("dp", "space"), axis=0)
        weights_next = gathered.transpose(1, 0, 2).reshape(layers, taps_len, channels)
        return *maps(result, input_grad), momentum_next, master_next, weights_next

    piece = shard_len // channels
    length = dp_count * piece
    base = (master - learn_rate * momentum_rate * momentum).reshape(layers, piece, channels)
    pieces = [pair] + [swap(pair, "space", k) for k in range(1, space_count)]
    bases = [base] + [swap(base, "dp", 2 * k) for k in range(1, zs)]
    smooth, edge, send, keep = sample_step(
        pieces, weights, mark, strip, cols, (dp_count, piece), pixel_total
    )
    total = (keep + swap(send, "dp", 1).astype(jnp.float32)).astype(jnp.bfloat16)
    bit = 2
    while bit < dp_count:
        far = swap(total, "dp", bit)
        bit *= 2
        if bit < dp_count:
            total = (total.astype(jnp.float32) + far.astype(jnp.float32)).astype(jnp.bfloat16)
    result, input_grad = finish(smooth, edge, weights, cols)
    update = vmem_call(
        functools.partial(update_kernel, zs, piece),
        (shape((length, channels)), shape((layers, piece, channels), jnp.float32)),
        [pltpu.VMEM((length + spare, channels), jnp.float32)] * 2,
    )
    new_piece, own_grad = update(total, far, *bases)
    near = [new_piece] + [swap(new_piece, "space", k) for k in range(1, space_count)]
    other = [swap(value, "dp", 1) for value in near]
    held = place(near, None, zs, piece, (layers, taps_len, channels))
    weights_next = place(other, held, zs, piece, (layers, taps_len, channels))
    gradient = own_grad.reshape(layers, shard_len)
    momentum_next = momentum_rate * momentum + gradient
    master_next = master - learn_rate * momentum_next
    return *maps(result, input_grad), momentum_next, master_next, weights_next


def solution(mesh):
    split = P("dp", "space", None, None)
    shard = P(None, ("dp", "space"))
    return jax.shard_map(
        block,
        mesh=mesh,
        in_specs=(split, split, P(), shard, shard),
        out_specs=(split, split, shard, shard, P()),
        check_vma=False,
    )
```

time: 42.4 us -> 38.8 us (0.915)
  waiting for transfers between devices: 16.8 us -> 14.3 us
  other arithmetic: 1.59 us -> 0.75 us
    ppermute x16, waiting for transfers between devices: 16.8 us -> 14.3 us  [swap(): return lax.ppermute(value, axis, [(i, i ^ bit) for i in range(size)])]
    pallas_call x3, Pallas kernels: 5.07 us -> 3.25 us  [call(): pl.pallas_call(body, out_shape=outs, in_specs=[spec] * len(args), out_spe...]
    pallas_call x0 -> x3, Pallas kernels: none -> 1.68 us  [the longest x2 1.68 us: place(): pl.pallas_call(functools.partial(place_kernel, zs, count, piece, held is...]
    concatenate x1 -> x0, other arithmetic: 0.83 us -> none  [block(): jnp.concatenate([fields, cotangent], axis=0).reshape(2, rows, channels)]
    unnamed x6 -> x9, local copies, waits for them, and re-layouts: 1.08 us -> 0.89 us
  transfers between devices with their start and end apart: 16 -> 16, of which waited for: 11 -> 11; matrix products, arithmetic and copies ran while one was open for 2% -> 2% of each run, Pallas kernels for 0% -> 5%
where the time goes in v4:
time: 38.8 us; the launch traced here: 38.7 us
  starting transfers between devices  17 us (44%)
  waiting for transfers between devices  14.3 us (37%)
  Pallas kernels  4.93 us (13%)
  local copies, waits for them, and re-layouts  0.93 us (2%)
  between operations  0.76 us (2%)
  other arithmetic  0.75 us (2%)
    ppermute x16, starting transfers between devices, swap(): return lax.ppermute(value, axis, [(i, i ^ bit) for i in range(size)])  17 us
    ppermute x16, waiting for transfers between devices, swap(): return lax.ppermute(value, axis, [(i, i ^ bit) for i in range(size)])  14.3 us
    pallas_call x3, Pallas kernels, call(): pl.pallas_call(body, out_shape=outs, in_specs=[spec] * len(args), out_spe...  3.25 us
    pallas_call x2, Pallas kernels, place(): pl.pallas_call(functools.partial(place_kernel, zs, count, piece, held is...  1.68 us
    unnamed x9, local copies, waits for them, and re-layouts  0.89 us
  transfers between devices with their start and end apart: 16, of which 11 were waited for; matrix products, arithmetic and copies ran while one was open for 2% of the time, Pallas kernels for 5%

profile of v4, /device:TPU:0, one launch (start us, length us, event | category | flops | bytes accessed | tf_op | source)
XLA Modules:
  0.0 38.7 jit_solution(3481860732844177524)
XLA Ops:
  0.6 0.0 copy-start.3
  0.6 0.0 copy-start
  0.7 0.9 %constant_dynamic-update-slice_fusion.1 = bf16[2,2,96,128]{3,2,1,0:T(8,128)(2,1)S(1)} fusion(bf16[1,2,96,128]{3,2,1,0:T(8,128)(2,1)} %param.5), kind=kLoop, calls=%fused_computation.6 | loop fusion | bytes 98304
  1.5 0.0 copy-done.3
  1.5 4.0 %collective-permute-start.2 = (bf16[2,2,96,128]{3,2,1,0:T(8,128)(2,1)S(1)}, bf16[2,2,96,128]{3,2,1,0:T(8,128)(2,1)S(1)}, u32[]{:S(2)}, u32[]{:S(2)}) collective-permute-start(bf16[2,2,96,128]{3,2,1,0:T(8,128)(2,1)S(1)} %constant_dynamic-update-slice_fusion.refs_0_), channel_id=1, source_target_pairs={{0,3},{1,2},{2,1},{3,0},{4,7},{5,6},{6,5},{7,4},{8,11},{9,10},{10,... | collective-permute-start | bytes 294920 | tf_op jit(solution)/shard_map/ppermute | solution.py:311
  5.5 0.5 %collective-permute-start.1 = (bf16[2,2,96,128]{3,2,1,0:T(8,128)(2,1)S(1)}, bf16[2,2,96,128]{3,2,1,0:T(8,128)(2,1)S(1)}, u32[]{:S(2)}, u32[]{:S(2)}) collective-permute-start(bf16[2,2,96,128]{3,2,1,0:T(8,128)(2,1)S(1)} %constant_dynamic-update-slice_fusion.refs_0_), channel_id=1, source_target_pairs={{0,2},{1,3},{2,0},{3,1},{4,6},{5,7},{6,4},{7,5},{8,10},{9,11},{10,... | collective-permute-start | bytes 294920 | tf_op jit(solution)/shard_map/ppermute | solution.py:311
  6.0 0.1 collective-permute-start
  6.2 2.5 %collective-permute-done.2.refs_3_ = bf16[2,2,96,128]{3,2,1,0:T(8,128)(2,1)S(1)} collective-permute-done((bf16[2,2,96,128]{3,2,1,0:T(8,128)(2,1)S(1)}, bf16[2,2,96,128]{3,2,1,0:T(8,128)(2,1)S(1)}, u32[]{:S(2)}, u32[]{:S(2)}) %collective-permute-start.2) | collective-permute-done | bytes 98336 | tf_op jit(solution)/shard_map/ppermute | solution.py:311
  8.7 1.7 %collective-permute-done.1.refs_2_ = bf16[2,2,96,128]{3,2,1,0:T(8,128)(2,1)S(1)} collective-permute-done((bf16[2,2,96,128]{3,2,1,0:T(8,128)(2,1)S(1)}, bf16[2,2,96,128]{3,2,1,0:T(8,128)(2,1)S(1)}, u32[]{:S(2)}, u32[]{:S(2)}) %collective-permute-start.1) | collective-permute-done | bytes 98336 | tf_op jit(solution)/shard_map/ppermute | solution.py:311
  10.4 0.3 collective-permute-done.refs_1_
  10.8 0.0 copy-done
  10.8 2.2 %shard_map.92 = (bf16[192,128]{1,0:T(8,128)(2,1)S(1)}, bf16[384,128]{1,0:T(8,128)(2,1)S(1)}, bf16[288,128]{1,0:T(8,128)(2,1)S(1)}, f32[288,128]{1,0:T(8,128)S(1)}) custom-call(bf16[2,2,96,128]{3,2,1,0:T(8,128)(2,1)S(1)} %constant_dynamic-update-slice_fusion.refs_0_, bf16[2,2,96,128]{3,2,1,0:T(8,128)(2,1)S(1)} %collective-permute-done.refs_1_, ...), custom_call_target="tpu_custom_call" | custom-call | tf_op jit(solution)/shard_map/pallas_call | solution.py:248
  13.0 0.1 collective-permute-start.3
  13.1 1.3 %collective-permute-done.3 = bf16[288,128]{1,0:T(8,128)(2,1)S(1)} collective-permute-done((bf16[288,128]{1,0:T(8,128)(2,1)S(1)}, bf16[288,128]{1,0:T(8,128)(2,1)S(1)}, u32[]{:S(2)}, u32[]{:S(2)}) %collective-permute-start.3) | collective-permute-done | bytes 73760 | tf_op jit(solution)/shard_map/ppermute | solution.py:311
  14.3 0.0 copy-start.1
  14.3 0.0 copy-start.2
  14.4 1.6 %collective-permute-start.4 = (bf16[288,128]{1,0:T(8,128)(2,1)S(1)}, bf16[288,128]{1,0:T(8,128)(2,1)S(1)}, u32[]{:S(2)}, u32[]{:S(2)}) collective-permute-start(bf16[288,128]{1,0:T(8,128)(2,1)S(1)} %add_convert_fusion.1), channel_id=1, source_target_pairs={{0,8},{4,12},{8,0},{12,4},{16,24},{20,28},{24,16},{28,20},{1,9},{5... | collective-permute-start | bytes 221192 | tf_op jit(solution)/shard_map/ppermute | solution.py:311
  16.0 2.8 %collective-permute-done.4 = bf16[288,128]{1,0:T(8,128)(2,1)S(1)} collective-permute-done((bf16[288,128]{1,0:T(8,128)(2,1)S(1)}, bf16[288,128]{1,0:T(8,128)(2,1)S(1)}, u32[]{:S(2)}, u32[]{:S(2)}) %collective-permute-start.4) | collective-permute-done | bytes 73760 | tf_op jit(solution)/shard_map/ppermute | solution.py:311
  18.8 2.6 %collective-permute-start.5 = (bf16[288,128]{1,0:T(8,128)(2,1)S(1)}, bf16[288,128]{1,0:T(8,128)(2,1)S(1)}, u32[]{:S(2)}, u32[]{:S(2)}) collective-permute-start(bf16[288,128]{1,0:T(8,128)(2,1)S(1)} %add_convert_fusion.refs_0_), channel_id=1, source_target_pairs={{0,16},{4,20},{8,24},{12,28},{16,0},{20,4},{24,8},{28,12},{1,17},{... | collective-permute-start | bytes 221192 | tf_op jit(solution)/shard_map/ppermute | solution.py:311
  21.5 0.0 copy-done.1
  21.5 0.0 copy-done.2
  21.5 1.4 %collective-permute-start.8 = (f32[2,36,128]{2,1,0:T(8,128)S(1)}, f32[2,36,128]{2,1,0:T(8,128)S(1)}, u32[]{:S(2)}, u32[]{:S(2)}) collective-permute-start(f32[2,36,128]{2,1,0:T(8,128)S(1)} %reshape.24.refs_2_), channel_id=1, source_target_pairs={{0,24},{4,28},{8,16},{12,20},{16,8},{20,12},{24,0},{28,4},{1,25},{... | collective-permute-start | bytes 110600 | tf_op jit(solution)/shard_map/ppermute | solution.py:311
  22.9 1.7 %collective-permute-start.7 = (f32[2,36,128]{2,1,0:T(8,128)S(1)}, f32[2,36,128]{2,1,0:T(8,128)S(1)}, u32[]{:S(2)}, u32[]{:S(2)}) collective-permute-start(f32[2,36,128]{2,1,0:T(8,128)S(1)} %reshape.24.refs_2_), channel_id=1, source_target_pairs={{0,16},{4,20},{8,24},{12,28},{16,0},{20,4},{24,8},{28,12},{1,17},{... | collective-permute-start | bytes 110600 | tf_op jit(solution)/shard_map/ppermute | solution.py:311
  24.6 1.3 %collective-permute-start.6 = (f32[2,36,128]{2,1,0:T(8,128)S(1)}, f32[2,36,128]{2,1,0:T(8,128)S(1)}, u32[]{:S(2)}, u32[]{:S(2)}) collective-permute-start(f32[2,36,128]{2,1,0:T(8,128)S(1)} %reshape.24.refs_2_), channel_id=1, source_target_pairs={{0,8},{4,12},{8,0},{12,4},{16,24},{20,28},{24,16},{28,20},{1,9},{5... | collective-permute-start | bytes 110600 | tf_op jit(solution)/shard_map/ppermute | solution.py:311
  26.0 1.5 %collective-permute-done.8.refs_5_ = f32[2,36,128]{2,1,0:T(8,128)S(1)} collective-permute-done((f32[2,36,128]{2,1,0:T(8,128)S(1)}, f32[2,36,128]{2,1,0:T(8,128)S(1)}, u32[]{:S(2)}, u32[]{:S(2)}) %collective-permute-start.8) | collective-permute-done | bytes 36896 | tf_op jit(solution)/shard_map/ppermute | solution.py:311
  27.5 0.9 %collective-permute-done.7.refs_4_ = f32[2,36,128]{2,1,0:T(8,128)S(1)} collective-permute-done((f32[2,36,128]{2,1,0:T(8,128)S(1)}, f32[2,36,128]{2,1,0:T(8,128)S(1)}, u32[]{:S(2)}, u32[]{:S(2)}) %collective-permute-start.7) | collective-permute-done | bytes 36896 | tf_op jit(solution)/shard_map/ppermute | solution.py:311
  28.4 0.4 %collective-permute-done.6.refs_3_ = f32[2,36,128]{2,1,0:T(8,128)S(1)} collective-permute-done((f32[2,36,128]{2,1,0:T(8,128)S(1)}, f32[2,36,128]{2,1,0:T(8,128)S(1)}, u32[]{:S(2)}, u32[]{:S(2)}) %collective-permute-start.6) | collective-permute-done | bytes 36896 | tf_op jit(solution)/shard_map/ppermute | solution.py:311
  28.9 0.0 collective-permute-done.5.refs_1_
  28.9 0.1 shard_map.94
  28.9 1.6 %collective-permute-start.14 = (bf16[288,128]{1,0:T(8,128)(2,1)S(1)}, bf16[288,128]{1,0:T(8,128)(2,1)S(1)}, u32[]{:S(2)}, u32[]{:S(2)}) collective-permute-start(bf16[288,128]{1,0:T(8,128)(2,1)S(1)} %get-tuple-element.20.refs_0_), channel_id=1, source_target_pairs={{0,3},{1,2},{2,1},{3,0},{4,7},{5,6},{6,5},{7,4},{8,11},{9,10},{10,... | collective-permute-start | bytes 221192 | tf_op jit(solution)/shard_map/ppermute | solution.py:311
  30.5 1.4 %collective-permute-start.12 = (bf16[288,128]{1,0:T(8,128)(2,1)S(1)}, bf16[288,128]{1,0:T(8,128)(2,1)S(1)}, u32[]{:S(2)}, u32[]{:S(2)}) collective-permute-start(bf16[288,128]{1,0:T(8,128)(2,1)S(1)} %get-tuple-element.20.refs_0_), channel_id=1, source_target_pairs={{0,2},{1,3},{2,0},{3,1},{4,6},{5,7},{6,4},{7,5},{8,10},{9,11},{10,... | collective-permute-start | bytes 221192 | tf_op jit(solution)/shard_map/ppermute | solution.py:311
  31.9 0.6 %collective-permute-start.10 = (bf16[288,128]{1,0:T(8,128)(2,1)S(1)}, bf16[288,128]{1,0:T(8,128)(2,1)S(1)}, u32[]{:S(2)}, u32[]{:S(2)}) collective-permute-start(bf16[288,128]{1,0:T(8,128)(2,1)S(1)} %get-tuple-element.20.refs_0_), channel_id=1, source_target_pairs={{0,1},{1,0},{2,3},{3,2},{4,5},{5,4},{6,7},{7,6},{8,9},{9,8},{10,11... | collective-permute-start | bytes 221192 | tf_op jit(solution)/shard_map/ppermute | solution.py:311
  32.5 1.0 %shard_map.93 = (bf16[192,128]{1,0:T(8,128)(2,1)}, bf16[192,128]{1,0:T(8,128)(2,1)}) custom-call(bf16[192,128]{1,0:T(8,128)(2,1)S(1)} %get-tuple-element.13.smooth_ref, bf16[384,128]{1,0:T(8,128)(2,1)S(1)} %get-tuple-element.14.edge_ref, bf16[2,1152,128]{2,1,0:T(8,128)(2,1)S(1)} %copy-done), custom_call_target="tpu_custom_call" | custom-call | tf_op jit(solution)/shard_map/pallas_call | solution.py:248
  33.5 0.0 collective-permute-start.9
  33.5 1.1 %collective-permute-done.14.refs_3_ = bf16[288,128]{1,0:T(8,128)(2,1)S(1)} collective-permute-done((bf16[288,128]{1,0:T(8,128)(2,1)S(1)}, bf16[288,128]{1,0:T(8,128)(2,1)S(1)}, u32[]{:S(2)}, u32[]{:S(2)}) %collective-permute-start.14) | collective-permute-done | bytes 73760 | tf_op jit(solution)/shard_map/ppermute | solution.py:311
  34.6 0.0 collective-permute-start.15
  34.6 0.7 %collective-permute-done.12.refs_2_ = bf16[288,128]{1,0:T(8,128)(2,1)S(1)} collective-permute-done((bf16[288,128]{1,0:T(8,128)(2,1)S(1)}, bf16[288,128]{1,0:T(8,128)(2,1)S(1)}, u32[]{:S(2)}, u32[]{:S(2)}) %collective-permute-start.12) | collective-permute-done | bytes 73760 | tf_op jit(solution)/shard_map/ppermute | solution.py:311
  35.3 0.0 collective-permute-start.13
  35.3 0.9 %collective-permute-done.10.refs_1_ = bf16[288,128]{1,0:T(8,128)(2,1)S(1)} collective-permute-done((bf16[288,128]{1,0:T(8,128)(2,1)S(1)}, bf16[288,128]{1,0:T(8,128)(2,1)S(1)}, u32[]{:S(2)}, u32[]{:S(2)}) %collective-permute-start.10) | collective-permute-done | bytes 73760 | tf_op jit(solution)/shard_map/ppermute | solution.py:311
  36.3 0.0 collective-permute-start.11
  36.3 0.7 %multiply_subtract_fusion = (f32[2,4608]{1,0:T(2,128)}, f32[2,4608]{1,0:T(2,128)}) fusion(f32[2,4608]{1,0:T(2,128)S(1)} %copy-done.1, f32[1,2,36,128]{3,2,1,0:T(8,128)S(1)} %bitcast.6, f32[2,4608]{1,0:T(2,128)S(1)} %copy-done.2), kind=kLoop, calls=%fused_computation.3 | loop fusion | flops 36864 | bytes 184320 | tf_op jit(solution)/shard_map/sub | solution.py:386
  36.9 0.8 %place_near.1.refs_4_ = bf16[2,1152,128]{2,1,0:T(8,128)(2,1)} custom-call(bf16[288,128]{1,0:T(8,128)(2,1)S(1)} %get-tuple-element.20.refs_0_, bf16[288,128]{1,0:T(8,128)(2,1)S(1)} %collective-permute-done.10.refs_1_, bf16[288,128]{1,0:T(8,128)(2,1)S(1)} %collective-permute-done.12.refs_2_, bf16[288,128]{1,0:T(8,128)(2,1)S(1)} %collective-permute-done.14.refs_3_), custom_call_target="tpu_custom_call" | custom-call | tf_op jit(solution)/shard_map/place_near/pallas_call | solution.py:227
  37.8 0.0 collective-permute-done.9.refs_0_
  37.8 0.0 collective-permute-done.15.refs_3_
  37.8 0.0 collective-permute-done.13.refs_2_
  37.8 0.0 collective-permute-done.11.refs_1_
  37.8 0.8 %place_far.1 = bf16[2,1152,128]{2,1,0:T(8,128)(2,1)} custom-call(bf16[288,128]{1,0:T(8,128)(2,1)S(1)} %collective-permute-done.9.refs_0_, bf16[288,128]{1,0:T(8,128)(2,1)S(1)} %collective-permute-done.11.refs_1_, bf16[288,128]{1,0:T(8,128)(2,1)S(1)} %collective-permute-done.13.refs_2_, ...), custom_call_target="tpu_custom_call", output_to_operand_aliasing={{}: (4, {})} | custom-call | tf_op jit(solution)/shard_map/place_far/pallas_call | solution.py:227
  (6 shorter events, 0.1 us)
Async XLA Ops:
  0.6 0.9 %copy-start.3 = (bf16[1,2,96,128]{3,2,1,0:T(8,128)(2,1)S(1)}, bf16[1,2,96,128]{3,2,1,0:T(8,128)(2,1)}, u32[]{:S(2)}) copy-start(bf16[1,2,96,128]{3,2,1,0:T(8,128)(2,1)} %param.6) | copy-start | bytes 147460
  0.6 10.1 %copy-start = (bf16[2,1152,128]{2,1,0:T(8,128)(2,1)S(1)}, bf16[2,1152,128]{2,1,0:T(8,128)(2,1)}, u32[]{:S(2)}) copy-start(bf16[2,1152,128]{2,1,0:T(8,128)(2,1)} %weight_ref.3) | copy-start | bytes 1769476
  1.5 7.2 %collective-permute-start.2 = (bf16[2,2,96,128]{3,2,1,0:T(8,128)(2,1)S(1)}, bf16[2,2,96,128]{3,2,1,0:T(8,128)(2,1)S(1)}, u32[]{:S(2)}, u32[]{:S(2)}) collective-permute-start(bf16[2,2,96,128]{3,2,1,0:T(8,128)(2,1)S(1)} %constant_dynamic-update-slice_fusion.refs_0_), channel_id=1, source_target_pairs={{0,3},{1,2},{2,1},{3,0},{4,7},{5,6},{6,5},{7,4},{8,11},{9,10},{10,... | collective-permute-start | bytes 294920 | tf_op jit(solution)/shard_map/ppermute | solution.py:311
  5.5 4.9 %collective-permute-start.1 = (bf16[2,2,96,128]{3,2,1,0:T(8,128)(2,1)S(1)}, bf16[2,2,96,128]{3,2,1,0:T(8,128)(2,1)S(1)}, u32[]{:S(2)}, u32[]{:S(2)}) collective-permute-start(bf16[2,2,96,128]{3,2,1,0:T(8,128)(2,1)S(1)} %constant_dynamic-update-slice_fusion.refs_0_), channel_id=1, source_target_pairs={{0,2},{1,3},{2,0},{3,1},{4,6},{5,7},{6,4},{7,5},{8,10},{9,11},{10,... | collective-permute-start | bytes 294920 | tf_op jit(solution)/shard_map/ppermute | solution.py:311
  6.0 4.7 %collective-permute-start = (bf16[2,2,96,128]{3,2,1,0:T(8,128)(2,1)S(1)}, bf16[2,2,96,128]{3,2,1,0:T(8,128)(2,1)S(1)}, u32[]{:S(2)}, u32[]{:S(2)}) collective-permute-start(bf16[2,2,96,128]{3,2,1,0:T(8,128)(2,1)S(1)} %constant_dynamic-update-slice_fusion.refs_0_), channel_id=1, source_target_pairs={{0,1},{1,0},{2,3},{3,2},{4,5},{5,4},{6,7},{7,6},{8,9},{9,8},{10,11... | collective-permute-start | bytes 294920 | tf_op jit(solution)/shard_map/ppermute | solution.py:311
  13.0 1.3 %collective-permute-start.3 = (bf16[288,128]{1,0:T(8,128)(2,1)S(1)}, bf16[288,128]{1,0:T(8,128)(2,1)S(1)}, u32[]{:S(2)}, u32[]{:S(2)}) collective-permute-start(bf16[288,128]{1,0:T(8,128)(2,1)S(1)} %get-tuple-element.18), channel_id=1, source_target_pairs={{0,4},{4,0},{8,12},{12,8},{16,20},{20,16},{24,28},{28,24},{1,5},{5... | collective-permute-start | bytes 221192 | tf_op jit(solution)/shard_map/ppermute | solution.py:311
  14.3 7.1 %copy-start.1 = (f32[2,4608]{1,0:T(2,128)S(1)}, f32[2,4608]{1,0:T(2,128)}, u32[]{:S(2)}) copy-start(f32[2,4608]{1,0:T(2,128)} %param.8) | copy-start | bytes 110596
  14.3 7.1 %copy-start.2 = (f32[2,4608]{1,0:T(2,128)S(1)}, f32[2,4608]{1,0:T(2,128)}, u32[]{:S(2)}) copy-start(f32[2,4608]{1,0:T(2,128)} %param.9) | copy-start | bytes 110596
  14.4 4.4 %collective-permute-start.4 = (bf16[288,128]{1,0:T(8,128)(2,1)S(1)}, bf16[288,128]{1,0:T(8,128)(2,1)S(1)}, u32[]{:S(2)}, u32[]{:S(2)}) collective-permute-start(bf16[288,128]{1,0:T(8,128)(2,1)S(1)} %add_convert_fusion.1), channel_id=1, source_target_pairs={{0,8},{4,12},{8,0},{12,4},{16,24},{20,28},{24,16},{28,20},{1,9},{5... | collective-permute-start | bytes 221192 | tf_op jit(solution)/shard_map/ppermute | solution.py:311
  18.8 10.1 %collective-permute-start.5 = (bf16[288,128]{1,0:T(8,128)(2,1)S(1)}, bf16[288,128]{1,0:T(8,128)(2,1)S(1)}, u32[]{:S(2)}, u32[]{:S(2)}) collective-permute-start(bf16[288,128]{1,0:T(8,128)(2,1)S(1)} %add_convert_fusion.refs_0_), channel_id=1, source_target_pairs={{0,16},{4,20},{8,24},{12,28},{16,0},{20,4},{24,8},{28,12},{1,17},{... | collective-permute-start | bytes 221192 | tf_op jit(solution)/shard_map/ppermute | solution.py:311
  21.5 6.0 %collective-permute-start.8 = (f32[2,36,128]{2,1,0:T(8,128)S(1)}, f32[2,36,128]{2,1,0:T(8,128)S(1)}, u32[]{:S(2)}, u32[]{:S(2)}) collective-permute-start(f32[2,36,128]{2,1,0:T(8,128)S(1)} %reshape.24.refs_2_), channel_id=1, source_target_pairs={{0,24},{4,28},{8,16},{12,20},{16,8},{20,12},{24,0},{28,4},{1,25},{... | collective-permute-start | bytes 110600 | tf_op jit(solution)/shard_map/ppermute | solution.py:311
  22.9 5.5 %collective-permute-start.7 = (f32[2,36,128]{2,1,0:T(8,128)S(1)}, f32[2,36,128]{2,1,0:T(8,128)S(1)}, u32[]{:S(2)}, u32[]{:S(2)}) collective-permute-start(f32[2,36,128]{2,1,0:T(8,128)S(1)} %reshape.24.refs_2_), channel_id=1, source_target_pairs={{0,16},{4,20},{8,24},{12,28},{16,0},{20,4},{24,8},{28,12},{1,17},{... | collective-permute-start | bytes 110600 | tf_op jit(solution)/shard_map/ppermute | solution.py:311
  24.6 4.2 %collective-permute-start.6 = (f32[2,36,128]{2,1,0:T(8,128)S(1)}, f32[2,36,128]{2,1,0:T(8,128)S(1)}, u32[]{:S(2)}, u32[]{:S(2)}) collective-permute-start(f32[2,36,128]{2,1,0:T(8,128)S(1)} %reshape.24.refs_2_), channel_id=1, source_target_pairs={{0,8},{4,12},{8,0},{12,4},{16,24},{20,28},{24,16},{28,20},{1,9},{5... | collective-permute-start | bytes 110600 | tf_op jit(solution)/shard_map/ppermute | solution.py:311
  28.9 5.6 %collective-permute-start.14 = (bf16[288,128]{1,0:T(8,128)(2,1)S(1)}, bf16[288,128]{1,0:T(8,128)(2,1)S(1)}, u32[]{:S(2)}, u32[]{:S(2)}) collective-permute-start(bf16[288,128]{1,0:T(8,128)(2,1)S(1)} %get-tuple-element.20.refs_0_), channel_id=1, source_target_pairs={{0,3},{1,2},{2,1},{3,0},{4,7},{5,6},{6,5},{7,4},{8,11},{9,10},{10,... | collective-permute-start | bytes 221192 | tf_op jit(solution)/shard_map/ppermute | solution.py:311
  30.5 4.8 %collective-permute-start.12 = (bf16[288,128]{1,0:T(8,128)(2,1)S(1)}, bf16[288,128]{1,0:T(8,128)(2,1)S(1)}, u32[]{:S(2)}, u32[]{:S(2)}) collective-permute-start(bf16[288,128]{1,0:T(8,128)(2,1)S(1)} %get-tuple-element.20.refs_0_), channel_id=1, source_target_pairs={{0,2},{1,3},{2,0},{3,1},{4,6},{5,7},{6,4},{7,5},{8,10},{9,11},{10,... | collective-permute-start | bytes 221192 | tf_op jit(solution)/shard_map/ppermute | solution.py:311
  31.9 4.4 %collective-permute-start.10 = (bf16[288,128]{1,0:T(8,128)(2,1)S(1)}, bf16[288,128]{1,0:T(8,128)(2,1)S(1)}, u32[]{:S(2)}, u32[]{:S(2)}) collective-permute-start(bf16[288,128]{1,0:T(8,128)(2,1)S(1)} %get-tuple-element.20.refs_0_), channel_id=1, source_target_pairs={{0,1},{1,0},{2,3},{3,2},{4,5},{5,4},{6,7},{7,6},{8,9},{9,8},{10,11... | collective-permute-start | bytes 221192 | tf_op jit(solution)/shard_map/ppermute | solution.py:311
  33.5 4.3 %collective-permute-start.9 = (bf16[288,128]{1,0:T(8,128)(2,1)S(1)}, bf16[288,128]{1,0:T(8,128)(2,1)S(1)}, u32[]{:S(2)}, u32[]{:S(2)}) collective-permute-start(bf16[288,128]{1,0:T(8,128)(2,1)S(1)} %get-tuple-element.20.refs_0_), channel_id=1, source_target_pairs={{0,4},{4,0},{8,12},{12,8},{16,20},{20,16},{24,28},{28,24},{1,5},{5... | collective-permute-start | bytes 221192 | tf_op jit(solution)/shard_map/ppermute | solution.py:311
  34.6 3.2 %collective-permute-start.15 = (bf16[288,128]{1,0:T(8,128)(2,1)S(1)}, bf16[288,128]{1,0:T(8,128)(2,1)S(1)}, u32[]{:S(2)}, u32[]{:S(2)}) collective-permute-start(bf16[288,128]{1,0:T(8,128)(2,1)S(1)} %collective-permute-done.14.refs_3_), channel_id=1, source_target_pairs={{0,4},{4,0},{8,12},{12,8},{16,20},{20,16},{24,28},{28,24},{1,5},{5... | collective-permute-start | bytes 221192 | tf_op jit(solution)/shard_map/ppermute | solution.py:311
  35.3 2.5 %collective-permute-start.13 = (bf16[288,128]{1,0:T(8,128)(2,1)S(1)}, bf16[288,128]{1,0:T(8,128)(2,1)S(1)}, u32[]{:S(2)}, u32[]{:S(2)}) collective-permute-start(bf16[288,128]{1,0:T(8,128)(2,1)S(1)} %collective-permute-done.12.refs_2_), channel_id=1, source_target_pairs={{0,4},{4,0},{8,12},{12,8},{16,20},{20,16},{24,28},{28,24},{1,5},{5... | collective-permute-start | bytes 221192 | tf_op jit(solution)/shard_map/ppermute | solution.py:311
  36.3 1.6 %collective-permute-start.11 = (bf16[288,128]{1,0:T(8,128)(2,1)S(1)}, bf16[288,128]{1,0:T(8,128)(2,1)S(1)}, u32[]{:S(2)}, u32[]{:S(2)}) collective-permute-start(bf16[288,128]{1,0:T(8,128)(2,1)S(1)} %collective-permute-done.10.refs_1_), channel_id=1, source_target_pairs={{0,4},{4,0},{8,12},{12,8},{16,20},{20,16},{24,28},{28,24},{1,5},{5... | collective-permute-start | bytes 221192 | tf_op jit(solution)/shard_map/ppermute | solution.py:311

commit v5 on v4

--- a/solution.py
+++ b/solution.py
@@ -40,23 +40,28 @@
     return jnp.concatenate(parts, axis=1)
 
 
-def fold(wide, dilation, cols, channels):
-    total = wide[:, channels : 2 * channels]
+def conv(maps, taps, dilation, cols, channels, back=False):
     step = dilation * cols
+    blank = jnp.zeros((channels, channels), jnp.bfloat16)
+    first = [[taps(a, b) for a in range(3)] for b in range(2)]
+    second = [[taps(0, 2), blank], [taps(1, 2), taps(2, 2)]]
+    right = maps[:, 2 * channels :]
+    wide = mixed(maps[:, : 2 * channels], first, back)
+    side = mixed(jnp.concatenate([moved(right, step), right], axis=1), second, back)
+    total = wide[:, channels : 2 * channels] + side[:, :channels]
     total = total + moved(wide[:, :channels], step)
-    return total + moved(wide[:, 2 * channels :], -step)
-
-
-def conv(shifted, kernel, dilation, cols, channels):
-    wide = jnp.dot(shifted, kernel, preferred_element_type=jnp.float32)
-    return fold(wide, dilation, cols, channels)
-
-
-def back_conv(shifted, kernel, dilation, cols, channels):
-    wide = lax.dot_general(
-        shifted, kernel, (((1,), (1,)), ((), ())), preferred_element_type=jnp.float32
-    )
-    return fold(wide, dilation, cols, channels)
+    return total + moved(wide[:, 2 * channels :] + side[:, channels:], -step)
+
+
+def mixed(maps, blocks, back):
+    if back:
+        rows = [jnp.concatenate(column, axis=1) for column in zip(*blocks)]
+        kernel = jnp.concatenate(rows, axis=0)
+        dims = (((1,), (1,)), ((), ()))
+    else:
+        kernel = jnp.concatenate([jnp.concatenate(row, axis=1) for row in blocks], axis=0)
+        dims = (((1,), (0,)), ((), ()))
+    return lax.dot_general(maps, kernel, dims, preferred_element_type=jnp.float32)
 
 
 def map_grad(shifted, delta, grad_ref, base, dilation, cols, channels, factor):
@@ -74,28 +79,19 @@
             )
 
 
-def ahead_matrix(weight_ref, layer):
+def ahead_taps(weight_ref, layer):
     channels = weight_ref.shape[-1]
 
     def tap(a, b):
         start = (a * 3 + b) * channels
         return weight_ref[layer, start : start + channels, :]
 
-    return jnp.concatenate(
-        [jnp.concatenate([tap(a, b) for a in range(3)], axis=1) for b in range(3)], axis=0
-    )
-
-
-def back_matrix(weight_ref, layer):
-    channels = weight_ref.shape[-1]
-
-    def tap(a, b):
-        start = ((2 - a) * 3 + 2 - b) * channels
-        return weight_ref[layer, start : start + channels, :]
-
-    return jnp.concatenate(
-        [jnp.concatenate([tap(a, b) for b in range(3)], axis=1) for a in range(3)], axis=0
-    )
+    return tap
+
+
+def back_taps(weight_ref, layer):
+    tap = ahead_taps(weight_ref, layer)
+    return lambda a, b: tap(2 - a, 2 - b)
 
 
 def touch_kernel(weight_ref, mark_ref):
@@ -117,17 +113,17 @@
         cot[place, :] = pieces[k][1].reshape(rows, channels).astype(jnp.float32)
 
     one = spread(sample[...], 1, cols)
-    pre_one = conv(one, ahead_matrix(weight_ref, 0), 1, cols, channels) * fan_scale
+    pre_one = conv(one, ahead_taps(weight_ref, 0), 1, cols, channels) * fan_scale
     sig = sigmoid(pre_one)
     slope_one = slope_of(pre_one, sig)
     hidden = (pre_one * sig).astype(jnp.bfloat16).astype(jnp.float32)
     two = spread(hidden, 2, cols)
-    pre_two = conv(two, ahead_matrix(weight_ref, 1), 2, cols, channels) * fan_scale
+    pre_two = conv(two, ahead_taps(weight_ref, 1), 2, cols, channels) * fan_scale
     sig = sigmoid(pre_two)
     smooth[...] = pre_two * sig + hidden
     delta_two = (cot[...] * slope_of(pre_two, sig)).astype(jnp.bfloat16)
     back = spread(delta_two.astype(jnp.float32), 2, cols)
-    mid_grad = back_conv(back, back_matrix(weight_ref, 1), 2, cols, channels) * fan_scale + cot[...]
+    mid_grad = conv(back, back_taps(weight_ref, 1), 2, cols, channels, True) * fan_scale + cot[...]
     delta_one = (mid_grad * slope_one).astype(jnp.bfloat16)
     taps_len = 9 * channels
     map_grad(two, delta_two, grad, taps_len, 2, cols, channels, factor)
@@ -163,17 +159,21 @@
     rows = result_ref.shape[0]
     result_ref[...] = smooth_ref[...]
     shifted = spread(edge_ref[...].astype(jnp.float32), 1, cols)
-    wide = back_conv(shifted, back_matrix(weight_ref, 0), 1, cols, channels)
+    wide = conv(shifted, back_taps(weight_ref, 0), 1, cols, channels, True)
     input_ref[...] = (wide[cols : cols + rows, :] * fan_scale).astype(jnp.bfloat16)
 
 
 def update_kernel(zs, piece, *refs):
-    own_ref, far_ref = refs[:2]
-    bases = refs[2 : 2 + zs]
-    weight_ref, grad_ref, total, stage = refs[2 + zs :]
+    parts, bases = (refs[:zs], refs[zs : 2 * zs])
+    weight_ref, grad_ref, pile, total, stage = refs[2 * zs :]
     here = lax.axis_index("dp") // 2
-    length = own_ref.shape[0]
-    total[:length, :] = own_ref[...].astype(jnp.float32) + far_ref[...].astype(jnp.float32)
+    length = parts[0].shape[0]
+    for k in range(zs):
+        pile[here ^ k] = parts[k][...].astype(jnp.float32)
+    added = pile[0]
+    for z in range(1, zs):
+        added = added + pile[z]
+    total[:length, :] = added
     for layer in range(2):
         for k in range(zs):
             place = pl.ds((layer * zs + (here ^ k)) * piece, piece)
@@ -364,19 +364,15 @@
         pieces, weights, mark, strip, cols, (dp_count, piece), pixel_total
     )
     total = (keep + swap(send, "dp", 1).astype(jnp.float32)).astype(jnp.bfloat16)
-    bit = 2
-    while bit < dp_count:
-        far = swap(total, "dp", bit)
-        bit *= 2
-        if bit < dp_count:
-            total = (total.astype(jnp.float32) + far.astype(jnp.float32)).astype(jnp.bfloat16)
+    totals = [total] + [swap(total, "dp", 2 * k) for k in range(1, zs)]
     result, input_grad = finish(smooth, edge, weights, cols)
     update = vmem_call(
         functools.partial(update_kernel, zs, piece),
         (shape((length, channels)), shape((layers, piece, channels), jnp.float32)),
-        [pltpu.VMEM((length + spare, channels), jnp.float32)] * 2,
-    )
-    new_piece, own_grad = update(total, far, *bases)
+        [pltpu.VMEM((zs, length, channels), jnp.float32)]
+        + [pltpu.VMEM((length + spare, channels), jnp.float32)] * 2,
+    )
+    new_piece, own_grad = update(*totals, *bases)
     near = [new_piece] + [swap(new_piece, "space", k) for k in range(1, space_count)]
     other = [swap(value, "dp", 1) for value in near]
     held = place(near, None, zs, piece, (layers, taps_len, channels))

time: 38.8 us -> 37.8 us (0.974)
  waiting for transfers between devices: 14.3 us -> 12.3 us
  starting transfers between devices: 17 us -> 18.1 us
    ppermute x16 -> x17, waiting for transfers between devices: 14.3 us -> 12.3 us  [swap(): return lax.ppermute(value, axis, [(i, i ^ bit) for i in range(size)])]
    ppermute x16 -> x17, starting transfers between devices: 17 us -> 18.1 us  [swap(): return lax.ppermute(value, axis, [(i, i ^ bit) for i in range(size)])]
  transfers between devices with their start and end apart: 16 -> 17, of which waited for: 11 -> 7; matrix products, arithmetic and copies ran while one was open for 2% -> 2% of each run, Pallas kernels for 5% -> 5%
where the time goes in v5:
time: 37.8 us; the launch traced here: 37.7 us
  starting transfers between devices  18.1 us (48%)
  waiting for transfers between devices  12.3 us (33%)
  Pallas kernels  4.88 us (13%)
  local copies, waits for them, and re-layouts  0.92 us (2%)
  between operations  0.77 us (2%)
  other arithmetic  0.73 us (2%)
    ppermute x17, starting transfers between devices, swap(): return lax.ppermute(value, axis, [(i, i ^ bit) for i in range(size)])  18.1 us
    ppermute x17, waiting for transfers between devices, swap(): return lax.ppermute(value, axis, [(i, i ^ bit) for i in range(size)])  12.3 us
    pallas_call x3, Pallas kernels, call(): pl.pallas_call(body, out_shape=outs, in_specs=[spec] * len(args), out_spe...  3.2 us
    pallas_call x2, Pallas kernels, place(): pl.pallas_call(functools.partial(place_kernel, zs, count, piece, held is...  1.67 us
    unnamed x9, local copies, waits for them, and re-layouts  0.88 us
  transfers between devices with their start and end apart: 17, of which 7 were waited for; matrix products, arithmetic and copies ran while one was open for 2% of the time, Pallas kernels for 5%

profile of v5, /device:TPU:0, one launch (start us, length us, event | category | flops | bytes accessed | tf_op | source)
XLA Modules:
  0.0 37.7 jit_solution(15543381426582287512)
XLA Ops:
  0.6 0.0 copy-start.3
  0.6 0.0 copy-start
  0.7 0.9 %constant_dynamic-update-slice_fusion.1 = bf16[2,2,96,128]{3,2,1,0:T(8,128)(2,1)S(1)} fusion(bf16[1,2,96,128]{3,2,1,0:T(8,128)(2,1)} %param.5), kind=kLoop, calls=%fused_computation.5 | loop fusion | bytes 98304
  1.5 0.0 copy-done.3
  1.5 4.0 %collective-permute-start.2 = (bf16[2,2,96,128]{3,2,1,0:T(8,128)(2,1)S(1)}, bf16[2,2,96,128]{3,2,1,0:T(8,128)(2,1)S(1)}, u32[]{:S(2)}, u32[]{:S(2)}) collective-permute-start(bf16[2,2,96,128]{3,2,1,0:T(8,128)(2,1)S(1)} %constant_dynamic-update-slice_fusion.refs_0_), channel_id=1, source_target_pairs={{0,3},{1,2},{2,1},{3,0},{4,7},{5,6},{6,5},{7,4},{8,11},{9,10},{10,... | collective-permute-start | bytes 294920 | tf_op jit(solution)/shard_map/ppermute | solution.py:311
  5.5 0.5 %collective-permute-start.1 = (bf16[2,2,96,128]{3,2,1,0:T(8,128)(2,1)S(1)}, bf16[2,2,96,128]{3,2,1,0:T(8,128)(2,1)S(1)}, u32[]{:S(2)}, u32[]{:S(2)}) collective-permute-start(bf16[2,2,96,128]{3,2,1,0:T(8,128)(2,1)S(1)} %constant_dynamic-update-slice_fusion.refs_0_), channel_id=1, source_target_pairs={{0,2},{1,3},{2,0},{3,1},{4,6},{5,7},{6,4},{7,5},{8,10},{9,11},{10,... | collective-permute-start | bytes 294920 | tf_op jit(solution)/shard_map/ppermute | solution.py:311
  6.0 0.1 collective-permute-start
  6.2 0.0 copy-start.1
  6.2 0.0 copy-start.2
  6.2 2.5 %collective-permute-done.2.refs_3_ = bf16[2,2,96,128]{3,2,1,0:T(8,128)(2,1)S(1)} collective-permute-done((bf16[2,2,96,128]{3,2,1,0:T(8,128)(2,1)S(1)}, bf16[2,2,96,128]{3,2,1,0:T(8,128)(2,1)S(1)}, u32[]{:S(2)}, u32[]{:S(2)}) %collective-permute-start.2) | collective-permute-done | bytes 98336 | tf_op jit(solution)/shard_map/ppermute | solution.py:311
  8.7 1.7 %collective-permute-done.1.refs_2_ = bf16[2,2,96,128]{3,2,1,0:T(8,128)(2,1)S(1)} collective-permute-done((bf16[2,2,96,128]{3,2,1,0:T(8,128)(2,1)S(1)}, bf16[2,2,96,128]{3,2,1,0:T(8,128)(2,1)S(1)}, u32[]{:S(2)}, u32[]{:S(2)}) %collective-permute-start.1) | collective-permute-done | bytes 98336 | tf_op jit(solution)/shard_map/ppermute | solution.py:311
  10.4 0.3 collective-permute-done.refs_1_
  10.8 0.0 copy-done
  10.8 2.1 %shard_map.92 = (bf16[192,128]{1,0:T(8,128)(2,1)S(1)}, bf16[384,128]{1,0:T(8,128)(2,1)S(1)}, bf16[288,128]{1,0:T(8,128)(2,1)S(1)}, f32[288,128]{1,0:T(8,128)S(1)}) custom-call(bf16[2,2,96,128]{3,2,1,0:T(8,128)(2,1)S(1)} %constant_dynamic-update-slice_fusion.refs_0_, bf16[2,2,96,128]{3,2,1,0:T(8,128)(2,1)S(1)} %collective-permute-done.refs_1_, ...), custom_call_target="tpu_custom_call" | custom-call | tf_op jit(solution)/shard_map/pallas_call | solution.py:248
  12.9 0.1 collective-permute-start.3
  13.0 0.0 copy-done.1
  13.0 0.0 copy-done.2
  13.1 3.7 %collective-permute-start.9 = (f32[2,36,128]{2,1,0:T(8,128)S(1)}, f32[2,36,128]{2,1,0:T(8,128)S(1)}, u32[]{:S(2)}, u32[]{:S(2)}) collective-permute-start(f32[2,36,128]{2,1,0:T(8,128)S(1)} %reshape.24.refs_4_), channel_id=1, source_target_pairs={{0,24},{4,28},{8,16},{12,20},{16,8},{20,12},{24,0},{28,4},{1,25},{... | collective-permute-start | bytes 110600 | tf_op jit(solution)/shard_map/ppermute | solution.py:311
  16.8 0.0 collective-permute-done.3
  16.8 1.2 %collective-permute-start.6 = (bf16[288,128]{1,0:T(8,128)(2,1)S(1)}, bf16[288,128]{1,0:T(8,128)(2,1)S(1)}, u32[]{:S(2)}, u32[]{:S(2)}) collective-permute-start(bf16[288,128]{1,0:T(8,128)(2,1)S(1)} %add_convert_fusion.refs_0_), channel_id=1, source_target_pairs={{0,24},{4,28},{8,16},{12,20},{16,8},{20,12},{24,0},{28,4},{1,25},{... | collective-permute-start | bytes 221192 | tf_op jit(solution)/shard_map/ppermute | solution.py:311
  17.9 0.0 collective-permute-start.5
  17.9 3.3 %collective-permute-start.4 = (bf16[288,128]{1,0:T(8,128)(2,1)S(1)}, bf16[288,128]{1,0:T(8,128)(2,1)S(1)}, u32[]{:S(2)}, u32[]{:S(2)}) collective-permute-start(bf16[288,128]{1,0:T(8,128)(2,1)S(1)} %add_convert_fusion.refs_0_), channel_id=1, source_target_pairs={{0,8},{4,12},{8,0},{12,4},{16,24},{20,28},{24,16},{28,20},{1,9},{5... | collective-permute-start | bytes 221192 | tf_op jit(solution)/shard_map/ppermute | solution.py:311
  21.2 0.0 collective-permute-start.8
  21.2 0.0 collective-permute-done.9.refs_7_
  21.2 1.6 %collective-permute-start.7 = (f32[2,36,128]{2,1,0:T(8,128)S(1)}, f32[2,36,128]{2,1,0:T(8,128)S(1)}, u32[]{:S(2)}, u32[]{:S(2)}) collective-permute-start(f32[2,36,128]{2,1,0:T(8,128)S(1)} %reshape.24.refs_4_), channel_id=1, source_target_pairs={{0,8},{4,12},{8,0},{12,4},{16,24},{20,28},{24,16},{28,20},{1,9},{5... | collective-permute-start | bytes 110600 | tf_op jit(solution)/shard_map/ppermute | solution.py:311
  22.9 4.9 %collective-permute-done.8.refs_6_ = f32[2,36,128]{2,1,0:T(8,128)S(1)} collective-permute-done((f32[2,36,128]{2,1,0:T(8,128)S(1)}, f32[2,36,128]{2,1,0:T(8,128)S(1)}, u32[]{:S(2)}, u32[]{:S(2)}) %collective-permute-start.8) | collective-permute-done | bytes 36896 | tf_op jit(solution)/shard_map/ppermute | solution.py:311
  27.8 0.0 collective-permute-done.7.refs_5_
  27.8 0.0 collective-permute-done.6.refs_3_
  27.8 0.0 collective-permute-done.5.refs_2_
  27.8 0.0 collective-permute-done.4.refs_1_
  27.8 0.1 shard_map.94
  27.9 1.7 %collective-permute-start.15 = (bf16[288,128]{1,0:T(8,128)(2,1)S(1)}, bf16[288,128]{1,0:T(8,128)(2,1)S(1)}, u32[]{:S(2)}, u32[]{:S(2)}) collective-permute-start(bf16[288,128]{1,0:T(8,128)(2,1)S(1)} %get-tuple-element.20.refs_0_), channel_id=1, source_target_pairs={{0,3},{1,2},{2,1},{3,0},{4,7},{5,6},{6,5},{7,4},{8,11},{9,10},{10,... | collective-permute-start | bytes 221192 | tf_op jit(solution)/shard_map/ppermute | solution.py:311
  29.6 1.3 %collective-permute-start.13 = (bf16[288,128]{1,0:T(8,128)(2,1)S(1)}, bf16[288,128]{1,0:T(8,128)(2,1)S(1)}, u32[]{:S(2)}, u32[]{:S(2)}) collective-permute-start(bf16[288,128]{1,0:T(8,128)(2,1)S(1)} %get-tuple-element.20.refs_0_), channel_id=1, source_target_pairs={{0,2},{1,3},{2,0},{3,1},{4,6},{5,7},{6,4},{7,5},{8,10},{9,11},{10,... | collective-permute-start | bytes 221192 | tf_op jit(solution)/shard_map/ppermute | solution.py:311
  30.9 0.6 %collective-permute-start.11 = (bf16[288,128]{1,0:T(8,128)(2,1)S(1)}, bf16[288,128]{1,0:T(8,128)(2,1)S(1)}, u32[]{:S(2)}, u32[]{:S(2)}) collective-permute-start(bf16[288,128]{1,0:T(8,128)(2,1)S(1)} %get-tuple-element.20.refs_0_), channel_id=1, source_target_pairs={{0,1},{1,0},{2,3},{3,2},{4,5},{5,4},{6,7},{7,6},{8,9},{9,8},{10,11... | collective-permute-start | bytes 221192 | tf_op jit(solution)/shard_map/ppermute | solution.py:311
  31.5 0.9 %shard_map.93 = (bf16[192,128]{1,0:T(8,128)(2,1)}, bf16[192,128]{1,0:T(8,128)(2,1)}) custom-call(bf16[192,128]{1,0:T(8,128)(2,1)S(1)} %get-tuple-element.13.smooth_ref, bf16[384,128]{1,0:T(8,128)(2,1)S(1)} %get-tuple-element.14.edge_ref, bf16[2,1152,128]{2,1,0:T(8,128)(2,1)S(1)} %copy-done), custom_call_target="tpu_custom_call" | custom-call | tf_op jit(solution)/shard_map/pallas_call | solution.py:248
  32.5 0.0 collective-permute-start.10
  32.5 1.2 %collective-permute-done.15.refs_3_ = bf16[288,128]{1,0:T(8,128)(2,1)S(1)} collective-permute-done((bf16[288,128]{1,0:T(8,128)(2,1)S(1)}, bf16[288,128]{1,0:T(8,128)(2,1)S(1)}, u32[]{:S(2)}, u32[]{:S(2)}) %collective-permute-start.15) | collective-permute-done | bytes 73760 | tf_op jit(solution)/shard_map/ppermute | solution.py:311
  33.7 0.0 collective-permute-start.16
  33.7 0.7 %collective-permute-done.13.refs_2_ = bf16[288,128]{1,0:T(8,128)(2,1)S(1)} collective-permute-done((bf16[288,128]{1,0:T(8,128)(2,1)S(1)}, bf16[288,128]{1,0:T(8,128)(2,1)S(1)}, u32[]{:S(2)}, u32[]{:S(2)}) %collective-permute-start.13) | collective-permute-done | bytes 73760 | tf_op jit(solution)/shard_map/ppermute | solution.py:311
  34.4 0.0 collective-permute-start.14
  34.4 0.9 %collective-permute-done.11.refs_1_ = bf16[288,128]{1,0:T(8,128)(2,1)S(1)} collective-permute-done((bf16[288,128]{1,0:T(8,128)(2,1)S(1)}, bf16[288,128]{1,0:T(8,128)(2,1)S(1)}, u32[]{:S(2)}, u32[]{:S(2)}) %collective-permute-start.11) | collective-permute-done | bytes 73760 | tf_op jit(solution)/shard_map/ppermute | solution.py:311
  35.3 0.0 collective-permute-start.12
  35.3 0.7 %multiply_subtract_fusion = (f32[2,4608]{1,0:T(2,128)}, f32[2,4608]{1,0:T(2,128)}) fusion(f32[2,4608]{1,0:T(2,128)S(1)} %copy-done.1, f32[1,2,36,128]{3,2,1,0:T(8,128)S(1)} %bitcast.6, f32[2,4608]{1,0:T(2,128)S(1)} %copy-done.2), kind=kLoop, calls=%fused_computation.2 | loop fusion | flops 36864 | bytes 184320 | tf_op jit(solution)/shard_map/sub | solution.py:382
  36.0 0.8 %place_near.1.refs_4_ = bf16[2,1152,128]{2,1,0:T(8,128)(2,1)} custom-call(bf16[288,128]{1,0:T(8,128)(2,1)S(1)} %get-tuple-element.20.refs_0_, bf16[288,128]{1,0:T(8,128)(2,1)S(1)} %collective-permute-done.11.refs_1_, bf16[288,128]{1,0:T(8,128)(2,1)S(1)} %collective-permute-done.13.refs_2_, bf16[288,128]{1,0:T(8,128)(2,1)S(1)} %collective-permute-done.15.refs_3_), custom_call_target="tpu_custom_call" | custom-call | tf_op jit(solution)/shard_map/place_near/pallas_call | solution.py:227
  36.8 0.0 collective-permute-done.10.refs_0_
  36.8 0.0 collective-permute-done.16.refs_3_
  36.8 0.0 collective-permute-done.14.refs_2_
  36.8 0.0 collective-permute-done.12.refs_1_
  36.8 0.8 %place_far.1 = bf16[2,1152,128]{2,1,0:T(8,128)(2,1)} custom-call(bf16[288,128]{1,0:T(8,128)(2,1)S(1)} %collective-permute-done.10.refs_0_, bf16[288,128]{1,0:T(8,128)(2,1)S(1)} %collective-permute-done.12.refs_1_, bf16[288,128]{1,0:T(8,128)(2,1)S(1)} %collective-permute-done.14.refs_2_, ...), custom_call_target="tpu_custom_call", output_to_operand_aliasing={{}: (4, {})} | custom-call | tf_op jit(solution)/shard_map/place_far/pallas_call | solution.py:227
  (5 shorter events, 0.1 us)
Async XLA Ops:
  0.6 0.9 %copy-start.3 = (bf16[1,2,96,128]{3,2,1,0:T(8,128)(2,1)S(1)}, bf16[1,2,96,128]{3,2,1,0:T(8,128)(2,1)}, u32[]{:S(2)}) copy-start(bf16[1,2,96,128]{3,2,1,0:T(8,128)(2,1)} %param.6) | copy-start | bytes 147460
  0.6 10.1 %copy-start = (bf16[2,1152,128]{2,1,0:T(8,128)(2,1)S(1)}, bf16[2,1152,128]{2,1,0:T(8,128)(2,1)}, u32[]{:S(2)}) copy-start(bf16[2,1152,128]{2,1,0:T(8,128)(2,1)} %weight_ref.3) | copy-start | bytes 1769476
  1.5 7.2 %collective-permute-start.2 = (bf16[2,2,96,128]{3,2,1,0:T(8,128)(2,1)S(1)}, bf16[2,2,96,128]{3,2,1,0:T(8,128)(2,1)S(1)}, u32[]{:S(2)}, u32[]{:S(2)}) collective-permute-start(bf16[2,2,96,128]{3,2,1,0:T(8,128)(2,1)S(1)} %constant_dynamic-update-slice_fusion.refs_0_), channel_id=1, source_target_pairs={{0,3},{1,2},{2,1},{3,0},{4,7},{5,6},{6,5},{7,4},{8,11},{9,10},{10,... | collective-permute-start | bytes 294920 | tf_op jit(solution)/shard_map/ppermute | solution.py:311
  5.5 4.9 %collective-permute-start.1 = (bf16[2,2,96,128]{3,2,1,0:T(8,128)(2,1)S(1)}, bf16[2,2,96,128]{3,2,1,0:T(8,128)(2,1)S(1)}, u32[]{:S(2)}, u32[]{:S(2)}) collective-permute-start(bf16[2,2,96,128]{3,2,1,0:T(8,128)(2,1)S(1)} %constant_dynamic-update-slice_fusion.refs_0_), channel_id=1, source_target_pairs={{0,2},{1,3},{2,0},{3,1},{4,6},{5,7},{6,4},{7,5},{8,10},{9,11},{10,... | collective-permute-start | bytes 294920 | tf_op jit(solution)/shard_map/ppermute | solution.py:311
  6.0 4.7 %collective-permute-start = (bf16[2,2,96,128]{3,2,1,0:T(8,128)(2,1)S(1)}, bf16[2,2,96,128]{3,2,1,0:T(8,128)(2,1)S(1)}, u32[]{:S(2)}, u32[]{:S(2)}) collective-permute-start(bf16[2,2,96,128]{3,2,1,0:T(8,128)(2,1)S(1)} %constant_dynamic-update-slice_fusion.refs_0_), channel_id=1, source_target_pairs={{0,1},{1,0},{2,3},{3,2},{4,5},{5,4},{6,7},{7,6},{8,9},{9,8},{10,11... | collective-permute-start | bytes 294920 | tf_op jit(solution)/shard_map/ppermute | solution.py:311
  6.2 6.8 %copy-start.1 = (f32[2,4608]{1,0:T(2,128)S(1)}, f32[2,4608]{1,0:T(2,128)}, u32[]{:S(2)}) copy-start(f32[2,4608]{1,0:T(2,128)} %param.8) | copy-start | bytes 110596
  6.2 6.8 %copy-start.2 = (f32[2,4608]{1,0:T(2,128)S(1)}, f32[2,4608]{1,0:T(2,128)}, u32[]{:S(2)}) copy-start(f32[2,4608]{1,0:T(2,128)} %param.9) | copy-start | bytes 110596
  12.9 3.9 %collective-permute-start.3 = (bf16[288,128]{1,0:T(8,128)(2,1)S(1)}, bf16[288,128]{1,0:T(8,128)(2,1)S(1)}, u32[]{:S(2)}, u32[]{:S(2)}) collective-permute-start(bf16[288,128]{1,0:T(8,128)(2,1)S(1)} %get-tuple-element.18), channel_id=1, source_target_pairs={{0,4},{4,0},{8,12},{12,8},{16,20},{20,16},{24,28},{28,24},{1,5},{5... | collective-permute-start | bytes 221192 | tf_op jit(solution)/shard_map/ppermute | solution.py:311
  13.1 8.2 %collective-permute-start.9 = (f32[2,36,128]{2,1,0:T(8,128)S(1)}, f32[2,36,128]{2,1,0:T(8,128)S(1)}, u32[]{:S(2)}, u32[]{:S(2)}) collective-permute-start(f32[2,36,128]{2,1,0:T(8,128)S(1)} %reshape.24.refs_4_), channel_id=1, source_target_pairs={{0,24},{4,28},{8,16},{12,20},{16,8},{20,12},{24,0},{28,4},{1,25},{... | collective-permute-start | bytes 110600 | tf_op jit(solution)/shard_map/ppermute | solution.py:311
  16.8 11.0 %collective-permute-start.6 = (bf16[288,128]{1,0:T(8,128)(2,1)S(1)}, bf16[288,128]{1,0:T(8,128)(2,1)S(1)}, u32[]{:S(2)}, u32[]{:S(2)}) collective-permute-start(bf16[288,128]{1,0:T(8,128)(2,1)S(1)} %add_convert_fusion.refs_0_), channel_id=1, source_target_pairs={{0,24},{4,28},{8,16},{12,20},{16,8},{20,12},{24,0},{28,4},{1,25},{... | collective-permute-start | bytes 221192 | tf_op jit(solution)/shard_map/ppermute | solution.py:311
  17.9 9.9 %collective-permute-start.5 = (bf16[288,128]{1,0:T(8,128)(2,1)S(1)}, bf16[288,128]{1,0:T(8,128)(2,1)S(1)}, u32[]{:S(2)}, u32[]{:S(2)}) collective-permute-start(bf16[288,128]{1,0:T(8,128)(2,1)S(1)} %add_convert_fusion.refs_0_), channel_id=1, source_target_pairs={{0,16},{4,20},{8,24},{12,28},{16,0},{20,4},{24,8},{28,12},{1,17},{... | collective-permute-start | bytes 221192 | tf_op jit(solution)/shard_map/ppermute | solution.py:311
  17.9 9.9 %collective-permute-start.4 = (bf16[288,128]{1,0:T(8,128)(2,1)S(1)}, bf16[288,128]{1,0:T(8,128)(2,1)S(1)}, u32[]{:S(2)}, u32[]{:S(2)}) collective-permute-start(bf16[288,128]{1,0:T(8,128)(2,1)S(1)} %add_convert_fusion.refs_0_), channel_id=1, source_target_pairs={{0,8},{4,12},{8,0},{12,4},{16,24},{20,28},{24,16},{28,20},{1,9},{5... | collective-permute-start | bytes 221192 | tf_op jit(solution)/shard_map/ppermute | solution.py:311
  21.2 6.6 %collective-permute-start.8 = (f32[2,36,128]{2,1,0:T(8,128)S(1)}, f32[2,36,128]{2,1,0:T(8,128)S(1)}, u32[]{:S(2)}, u32[]{:S(2)}) collective-permute-start(f32[2,36,128]{2,1,0:T(8,128)S(1)} %reshape.24.refs_4_), channel_id=1, source_target_pairs={{0,16},{4,20},{8,24},{12,28},{16,0},{20,4},{24,8},{28,12},{1,17},{... | collective-permute-start | bytes 110600 | tf_op jit(solution)/shard_map/ppermute | solution.py:311
  21.2 6.6 %collective-permute-start.7 = (f32[2,36,128]{2,1,0:T(8,128)S(1)}, f32[2,36,128]{2,1,0:T(8,128)S(1)}, u32[]{:S(2)}, u32[]{:S(2)}) collective-permute-start(f32[2,36,128]{2,1,0:T(8,128)S(1)} %reshape.24.refs_4_), channel_id=1, source_target_pairs={{0,8},{4,12},{8,0},{12,4},{16,24},{20,28},{24,16},{28,20},{1,9},{5... | collective-permute-start | bytes 110600 | tf_op jit(solution)/shard_map/ppermute | solution.py:311
  27.9 5.7 %collective-permute-start.15 = (bf16[288,128]{1,0:T(8,128)(2,1)S(1)}, bf16[288,128]{1,0:T(8,128)(2,1)S(1)}, u32[]{:S(2)}, u32[]{:S(2)}) collective-permute-start(bf16[288,128]{1,0:T(8,128)(2,1)S(1)} %get-tuple-element.20.refs_0_), channel_id=1, source_target_pairs={{0,3},{1,2},{2,1},{3,0},{4,7},{5,6},{6,5},{7,4},{8,11},{9,10},{10,... | collective-permute-start | bytes 221192 | tf_op jit(solution)/shard_map/ppermute | solution.py:311
  29.6 4.8 %collective-permute-start.13 = (bf16[288,128]{1,0:T(8,128)(2,1)S(1)}, bf16[288,128]{1,0:T(8,128)(2,1)S(1)}, u32[]{:S(2)}, u32[]{:S(2)}) collective-permute-start(bf16[288,128]{1,0:T(8,128)(2,1)S(1)} %get-tuple-element.20.refs_0_), channel_id=1, source_target_pairs={{0,2},{1,3},{2,0},{3,1},{4,6},{5,7},{6,4},{7,5},{8,10},{9,11},{10,... | collective-permute-start | bytes 221192 | tf_op jit(solution)/shard_map/ppermute | solution.py:311
  30.9 4.4 %collective-permute-start.11 = (bf16[288,128]{1,0:T(8,128)(2,1)S(1)}, bf16[288,128]{1,0:T(8,128)(2,1)S(1)}, u32[]{:S(2)}, u32[]{:S(2)}) collective-permute-start(bf16[288,128]{1,0:T(8,128)(2,1)S(1)} %get-tuple-element.20.refs_0_), channel_id=1, source_target_pairs={{0,1},{1,0},{2,3},{3,2},{4,5},{5,4},{6,7},{7,6},{8,9},{9,8},{10,11... | collective-permute-start | bytes 221192 | tf_op jit(solution)/shard_map/ppermute | solution.py:311
  32.5 4.4 %collective-permute-start.10 = (bf16[288,128]{1,0:T(8,128)(2,1)S(1)}, bf16[288,128]{1,0:T(8,128)(2,1)S(1)}, u32[]{:S(2)}, u32[]{:S(2)}) collective-permute-start(bf16[288,128]{1,0:T(8,128)(2,1)S(1)} %get-tuple-element.20.refs_0_), channel_id=1, source_target_pairs={{0,4},{4,0},{8,12},{12,8},{16,20},{20,16},{24,28},{28,24},{1,5},{5... | collective-permute-start | bytes 221192 | tf_op jit(solution)/shard_map/ppermute | solution.py:311
  33.7 3.1 %collective-permute-start.16 = (bf16[288,128]{1,0:T(8,128)(2,1)S(1)}, bf16[288,128]{1,0:T(8,128)(2,1)S(1)}, u32[]{:S(2)}, u32[]{:S(2)}) collective-permute-start(bf16[288,128]{1,0:T(8,128)(2,1)S(1)} %collective-permute-done.15.refs_3_), channel_id=1, source_target_pairs={{0,4},{4,0},{8,12},{12,8},{16,20},{20,16},{24,28},{28,24},{1,5},{5... | collective-permute-start | bytes 221192 | tf_op jit(solution)/shard_map/ppermute | solution.py:311
  34.4 2.4 %collective-permute-start.14 = (bf16[288,128]{1,0:T(8,128)(2,1)S(1)}, bf16[288,128]{1,0:T(8,128)(2,1)S(1)}, u32[]{:S(2)}, u32[]{:S(2)}) collective-permute-start(bf16[288,128]{1,0:T(8,128)(2,1)S(1)} %collective-permute-done.13.refs_2_), channel_id=1, source_target_pairs={{0,4},{4,0},{8,12},{12,8},{16,20},{20,16},{24,28},{28,24},{1,5},{5... | collective-permute-start | bytes 221192 | tf_op jit(solution)/shard_map/ppermute | solution.py:311
  35.3 1.6 %collective-permute-start.12 = (bf16[288,128]{1,0:T(8,128)(2,1)S(1)}, bf16[288,128]{1,0:T(8,128)(2,1)S(1)}, u32[]{:S(2)}, u32[]{:S(2)}) collective-permute-start(bf16[288,128]{1,0:T(8,128)(2,1)S(1)} %collective-permute-done.11.refs_1_), channel_id=1, source_target_pairs={{0,4},{4,0},{8,12},{12,8},{16,20},{20,16},{24,28},{28,24},{1,5},{5... | collective-permute-start | bytes 221192 | tf_op jit(solution)/shard_map/ppermute | solution.py:311

commit v6 on v5

--- a/solution.py
+++ b/solution.py
@@ -184,57 +184,65 @@
     weight_ref[...] = stage[:length, :].astype(jnp.bfloat16)
 
 
-def place_kernel(zs, count, piece, far, *refs):
-    parts = refs[:count]
+def place_kernel(zs, count, piece, near, far, *refs):
+    parts = refs[: len(near) + len(far)]
     out_ref, stage, whole, half, sems = refs[-5:]
     where = lax.axis_index("space")
     side = lax.rem(lax.axis_index("dp"), 2)
-    side = 1 - side if far else side
     run = count * piece
     copies = []
-    for layer in range(2):
-        for k in range(count):
-            rows = slice(layer * zs * piece, (layer + 1) * zs * piece)
-            stage[rows, :] = parts[k][rows, :].astype(jnp.float32)
+    jobs = [(near, side, count)] if near else []
+    if far:
+        jobs.append((far, 1 - side, count // 2))
+    index = 0
+    for number, (flips, core, width) in enumerate(jobs):
+        base = len(near) if flips is far else 0
+        low = (where ^ flips[0]) // width * width
+        for layer in range(2):
+            for spot, flip in enumerate(flips):
+                rows = slice(layer * zs * piece, (layer + 1) * zs * piece)
+                stage[rows, :] = parts[base + spot][rows, :].astype(jnp.float32)
+                for z in range(zs):
+                    home = number * 2 * zs + layer * zs + z
+                    start = ((where ^ flip) - low) * piece
+                    whole[home, pl.ds(start, piece), :] = stage[
+                        (layer * zs + z) * piece : (layer * zs + z + 1) * piece, :
+                    ]
             for z in range(zs):
-                spot = (layer * zs + z) * piece
-                whole[pl.ds((layer * zs + z) * run + (where ^ k) * piece, piece), :] = stage[
-                    spot : spot + piece, :
-                ]
-        for z in range(zs):
-            rows = slice((layer * zs + z) * run, (layer * zs + z + 1) * run)
-            half[rows, :] = whole[rows, :].astype(jnp.bfloat16)
-            start = pl.multiple_of((2 * z + side) * run, run)
-            copies.append(
-                pltpu.make_async_copy(
-                    half.at[rows],
-                    out_ref.at[layer, pl.ds(start, run)],
-                    sems.at[layer * zs + z],
+                home = number * 2 * zs + layer * zs + z
+                size = width * piece
+                half[home, :size, :] = whole[home, :size, :].astype(jnp.bfloat16)
+                start = pl.multiple_of((2 * z + core) * run + low * piece, size)
+                copies.append(
+                    pltpu.make_async_copy(
+                        half.at[home, pl.ds(0, size)],
+                        out_ref.at[layer, pl.ds(start, size)],
+                        sems.at[index],
+                    )
                 )
-            )
-            copies[-1].start()
+                copies[-1].start()
+                index += 1
     for copy in copies:
         copy.wait()
 
 
-def place(parts, held, zs, piece, dims):
-    count = len(parts)
-    length = 2 * zs * piece
+def place(near, far, parts, held, zs, piece, count, dims):
     channels = dims[-1]
     spec = pl.BlockSpec(memory_space=pltpu.VMEM)
     anywhere = pl.BlockSpec(memory_space=pl.ANY)
     extra = [] if held is None else [held]
+    homes = 2 * zs * (bool(near) + bool(far))
     return pl.pallas_call(
-        functools.partial(place_kernel, zs, count, piece, held is not None),
+        functools.partial(place_kernel, zs, count, piece, near, far),
         out_shape=shape(dims),
-        in_specs=[spec] * count + [anywhere] * len(extra),
+        in_specs=[spec] * len(parts) + [anywhere] * len(extra),
         out_specs=anywhere,
-        input_output_aliases={count: 0} if extra else {},
+        input_output_aliases={len(parts): 0} if extra else {},
         scratch_shapes=[
-            pltpu.VMEM((length + spare, channels), jnp.float32),
-            pltpu.VMEM((count * length + spare, channels), jnp.float32),
-            pltpu.VMEM((count * length, channels), jnp.bfloat16),
-            pltpu.SemaphoreType.DMA((2 * zs,)),
+            pltpu.VMEM((2 * zs * piece + spare, channels), jnp.float32),
+            pltpu.VMEM((homes, count * piece + spare, channels), jnp.float32),
+            pltpu.VMEM((homes, count * piece, channels), jnp.bfloat16),
+            pltpu.SemaphoreType.DMA((homes,)),
         ],
         name="place_far" if extra else "place_near",
         compiler_params=pltpu.CompilerParams(vmem_limit_bytes=8 << 20),
@@ -375,8 +383,11 @@
     new_piece, own_grad = update(*totals, *bases)
     near = [new_piece] + [swap(new_piece, "space", k) for k in range(1, space_count)]
     other = [swap(value, "dp", 1) for value in near]
-    held = place(near, None, zs, piece, (layers, taps_len, channels))
-    weights_next = place(other, held, zs, piece, (layers, taps_len, channels))
+    dims = (layers, taps_len, channels)
+    every = tuple(range(space_count))
+    early, late = (every[space_count // 2 :], every[: space_count // 2])
+    held = place(every, early, near + other[space_count // 2 :], None, zs, piece, space_count, dims)
+    weights_next = place((), late, other[: space_count // 2], held, zs, piece, space_count, dims)
     gradient = own_grad.reshape(layers, shard_len)
     momentum_next = momentum_rate * momentum + gradient
     master_next = master - learn_rate * momentum_next

time: 37.8 us -> 37.9 us (level)
  no operation moved by 1% of the time
where the time goes in v6:
time: 37.9 us; the launch traced here: 37.7 us
  starting transfers between devices  18.1 us (48%)
  waiting for transfers between devices  12.3 us (32%)
  Pallas kernels  4.93 us (13%)
  local copies, waits for them, and re-layouts  0.92 us (2%)
  between operations  0.76 us (2%)
  other arithmetic  0.73 us (2%)
    ppermute x17, starting transfers between devices, swap(): return lax.ppermute(value, axis, [(i, i ^ bit) for i in range(size)])  18.1 us
    ppermute x17, waiting for transfers between devices, swap(): return lax.ppermute(value, axis, [(i, i ^ bit) for i in range(size)])  12.3 us
    pallas_call x3, Pallas kernels, call(): pl.pallas_call(body, out_shape=outs, in_specs=[spec] * len(args), out_spe...  3.2 us
    pallas_call x2, Pallas kernels, place(): pl.pallas_call(functools.partial(place_kernel, zs, count, piece, near, fa...  1.72 us
    unnamed x9, local copies, waits for them, and re-layouts  0.88 us
  transfers between devices with their start and end apart: 17, of which 7 were waited for; matrix products, arithmetic and copies ran while one was open for 2% of the time, Pallas kernels for 5%

profile of v6, /device:TPU:0, one launch (start us, length us, event | category | flops | bytes accessed | tf_op | source)
XLA Modules:
  0.0 37.7 jit_solution(10478607981712531326)
XLA Ops:
  0.6 0.0 copy-start.3
  0.6 0.0 copy-start
  0.7 0.9 %constant_dynamic-update-slice_fusion.1 = bf16[2,2,96,128]{3,2,1,0:T(8,128)(2,1)S(1)} fusion(bf16[1,2,96,128]{3,2,1,0:T(8,128)(2,1)} %param.5), kind=kLoop, calls=%fused_computation.5 | loop fusion | bytes 98304
  1.5 0.0 copy-done.3
  1.5 4.0 %collective-permute-start.2 = (bf16[2,2,96,128]{3,2,1,0:T(8,128)(2,1)S(1)}, bf16[2,2,96,128]{3,2,1,0:T(8,128)(2,1)S(1)}, u32[]{:S(2)}, u32[]{:S(2)}) collective-permute-start(bf16[2,2,96,128]{3,2,1,0:T(8,128)(2,1)S(1)} %constant_dynamic-update-slice_fusion.refs_0_), channel_id=1, source_target_pairs={{0,3},{1,2},{2,1},{3,0},{4,7},{5,6},{6,5},{7,4},{8,11},{9,10},{10,... | collective-permute-start | bytes 294920 | tf_op jit(solution)/shard_map/ppermute | solution.py:319
  5.5 0.5 %collective-permute-start.1 = (bf16[2,2,96,128]{3,2,1,0:T(8,128)(2,1)S(1)}, bf16[2,2,96,128]{3,2,1,0:T(8,128)(2,1)S(1)}, u32[]{:S(2)}, u32[]{:S(2)}) collective-permute-start(bf16[2,2,96,128]{3,2,1,0:T(8,128)(2,1)S(1)} %constant_dynamic-update-slice_fusion.refs_0_), channel_id=1, source_target_pairs={{0,2},{1,3},{2,0},{3,1},{4,6},{5,7},{6,4},{7,5},{8,10},{9,11},{10,... | collective-permute-start | bytes 294920 | tf_op jit(solution)/shard_map/ppermute | solution.py:319
  6.0 0.1 collective-permute-start
  6.2 0.0 copy-start.1
  6.2 0.0 copy-start.2
  6.2 2.5 %collective-permute-done.2.refs_3_ = bf16[2,2,96,128]{3,2,1,0:T(8,128)(2,1)S(1)} collective-permute-done((bf16[2,2,96,128]{3,2,1,0:T(8,128)(2,1)S(1)}, bf16[2,2,96,128]{3,2,1,0:T(8,128)(2,1)S(1)}, u32[]{:S(2)}, u32[]{:S(2)}) %collective-permute-start.2) | collective-permute-done | bytes 98336 | tf_op jit(solution)/shard_map/ppermute | solution.py:319
  8.7 1.7 %collective-permute-done.1.refs_2_ = bf16[2,2,96,128]{3,2,1,0:T(8,128)(2,1)S(1)} collective-permute-done((bf16[2,2,96,128]{3,2,1,0:T(8,128)(2,1)S(1)}, bf16[2,2,96,128]{3,2,1,0:T(8,128)(2,1)S(1)}, u32[]{:S(2)}, u32[]{:S(2)}) %collective-permute-start.1) | collective-permute-done | bytes 98336 | tf_op jit(solution)/shard_map/ppermute | solution.py:319
  10.4 0.3 collective-permute-done.refs_1_
  10.8 0.0 copy-done
  10.8 2.1 %shard_map.92 = (bf16[192,128]{1,0:T(8,128)(2,1)S(1)}, bf16[384,128]{1,0:T(8,128)(2,1)S(1)}, bf16[288,128]{1,0:T(8,128)(2,1)S(1)}, f32[288,128]{1,0:T(8,128)S(1)}) custom-call(bf16[2,2,96,128]{3,2,1,0:T(8,128)(2,1)S(1)} %constant_dynamic-update-slice_fusion.refs_0_, bf16[2,2,96,128]{3,2,1,0:T(8,128)(2,1)S(1)} %collective-permute-done.refs_1_, ...), custom_call_target="tpu_custom_call" | custom-call | tf_op jit(solution)/shard_map/pallas_call | solution.py:256
  12.9 0.1 collective-permute-start.3
  13.0 0.0 copy-done.1
  13.0 0.0 copy-done.2
  13.1 3.7 %collective-permute-start.9 = (f32[2,36,128]{2,1,0:T(8,128)S(1)}, f32[2,36,128]{2,1,0:T(8,128)S(1)}, u32[]{:S(2)}, u32[]{:S(2)}) collective-permute-start(f32[2,36,128]{2,1,0:T(8,128)S(1)} %reshape.24.refs_4_), channel_id=1, source_target_pairs={{0,24},{4,28},{8,16},{12,20},{16,8},{20,12},{24,0},{28,4},{1,25},{... | collective-permute-start | bytes 110600 | tf_op jit(solution)/shard_map/ppermute | solution.py:319
  16.8 0.0 collective-permute-done.3
  16.8 1.2 %collective-permute-start.6 = (bf16[288,128]{1,0:T(8,128)(2,1)S(1)}, bf16[288,128]{1,0:T(8,128)(2,1)S(1)}, u32[]{:S(2)}, u32[]{:S(2)}) collective-permute-start(bf16[288,128]{1,0:T(8,128)(2,1)S(1)} %add_convert_fusion.refs_0_), channel_id=1, source_target_pairs={{0,24},{4,28},{8,16},{12,20},{16,8},{20,12},{24,0},{28,4},{1,25},{... | collective-permute-start | bytes 221192 | tf_op jit(solution)/shard_map/ppermute | solution.py:319
  17.9 0.0 collective-permute-start.5
  17.9 3.3 %collective-permute-start.4 = (bf16[288,128]{1,0:T(8,128)(2,1)S(1)}, bf16[288,128]{1,0:T(8,128)(2,1)S(1)}, u32[]{:S(2)}, u32[]{:S(2)}) collective-permute-start(bf16[288,128]{1,0:T(8,128)(2,1)S(1)} %add_convert_fusion.refs_0_), channel_id=1, source_target_pairs={{0,8},{4,12},{8,0},{12,4},{16,24},{20,28},{24,16},{28,20},{1,9},{5... | collective-permute-start | bytes 221192 | tf_op jit(solution)/shard_map/ppermute | solution.py:319
  21.2 0.0 collective-permute-start.8
  21.2 0.0 collective-permute-done.9.refs_7_
  21.2 1.6 %collective-permute-start.7 = (f32[2,36,128]{2,1,0:T(8,128)S(1)}, f32[2,36,128]{2,1,0:T(8,128)S(1)}, u32[]{:S(2)}, u32[]{:S(2)}) collective-permute-start(f32[2,36,128]{2,1,0:T(8,128)S(1)} %reshape.24.refs_4_), channel_id=1, source_target_pairs={{0,8},{4,12},{8,0},{12,4},{16,24},{20,28},{24,16},{28,20},{1,9},{5... | collective-permute-start | bytes 110600 | tf_op jit(solution)/shard_map/ppermute | solution.py:319
  22.9 4.9 %collective-permute-done.8.refs_6_ = f32[2,36,128]{2,1,0:T(8,128)S(1)} collective-permute-done((f32[2,36,128]{2,1,0:T(8,128)S(1)}, f32[2,36,128]{2,1,0:T(8,128)S(1)}, u32[]{:S(2)}, u32[]{:S(2)}) %collective-permute-start.8) | collective-permute-done | bytes 36896 | tf_op jit(solution)/shard_map/ppermute | solution.py:319
  27.8 0.0 collective-permute-done.7.refs_5_
  27.8 0.0 collective-permute-done.6.refs_3_
  27.8 0.0 collective-permute-done.5.refs_2_
  27.8 0.0 collective-permute-done.4.refs_1_
  27.8 0.1 shard_map.94
  27.9 1.7 %collective-permute-start.14 = (bf16[288,128]{1,0:T(8,128)(2,1)S(1)}, bf16[288,128]{1,0:T(8,128)(2,1)S(1)}, u32[]{:S(2)}, u32[]{:S(2)}) collective-permute-start(bf16[288,128]{1,0:T(8,128)(2,1)S(1)} %get-tuple-element.20.refs_0_), channel_id=1, source_target_pairs={{0,3},{1,2},{2,1},{3,0},{4,7},{5,6},{6,5},{7,4},{8,11},{9,10},{10,... | collective-permute-start | bytes 221192 | tf_op jit(solution)/shard_map/ppermute | solution.py:319
  29.6 1.3 %collective-permute-start.13 = (bf16[288,128]{1,0:T(8,128)(2,1)S(1)}, bf16[288,128]{1,0:T(8,128)(2,1)S(1)}, u32[]{:S(2)}, u32[]{:S(2)}) collective-permute-start(bf16[288,128]{1,0:T(8,128)(2,1)S(1)} %get-tuple-element.20.refs_0_), channel_id=1, source_target_pairs={{0,2},{1,3},{2,0},{3,1},{4,6},{5,7},{6,4},{7,5},{8,10},{9,11},{10,... | collective-permute-start | bytes 221192 | tf_op jit(solution)/shard_map/ppermute | solution.py:319
  30.9 0.6 %collective-permute-start.11 = (bf16[288,128]{1,0:T(8,128)(2,1)S(1)}, bf16[288,128]{1,0:T(8,128)(2,1)S(1)}, u32[]{:S(2)}, u32[]{:S(2)}) collective-permute-start(bf16[288,128]{1,0:T(8,128)(2,1)S(1)} %get-tuple-element.20.refs_0_), channel_id=1, source_target_pairs={{0,1},{1,0},{2,3},{3,2},{4,5},{5,4},{6,7},{7,6},{8,9},{9,8},{10,11... | collective-permute-start | bytes 221192 | tf_op jit(solution)/shard_map/ppermute | solution.py:319
  31.5 0.9 %shard_map.93 = (bf16[192,128]{1,0:T(8,128)(2,1)}, bf16[192,128]{1,0:T(8,128)(2,1)}) custom-call(bf16[192,128]{1,0:T(8,128)(2,1)S(1)} %get-tuple-element.13.smooth_ref, bf16[384,128]{1,0:T(8,128)(2,1)S(1)} %get-tuple-element.14.edge_ref, bf16[2,1152,128]{2,1,0:T(8,128)(2,1)S(1)} %copy-done), custom_call_target="tpu_custom_call" | custom-call | tf_op jit(solution)/shard_map/pallas_call | solution.py:256
  32.5 0.0 collective-permute-start.10
  32.5 1.2 %collective-permute-done.14.refs_3_ = bf16[288,128]{1,0:T(8,128)(2,1)S(1)} collective-permute-done((bf16[288,128]{1,0:T(8,128)(2,1)S(1)}, bf16[288,128]{1,0:T(8,128)(2,1)S(1)}, u32[]{:S(2)}, u32[]{:S(2)}) %collective-permute-start.14) | collective-permute-done | bytes 73760 | tf_op jit(solution)/shard_map/ppermute | solution.py:319
  33.7 0.0 collective-permute-start.16
  33.7 0.7 %collective-permute-done.13.refs_2_ = bf16[288,128]{1,0:T(8,128)(2,1)S(1)} collective-permute-done((bf16[288,128]{1,0:T(8,128)(2,1)S(1)}, bf16[288,128]{1,0:T(8,128)(2,1)S(1)}, u32[]{:S(2)}, u32[]{:S(2)}) %collective-permute-start.13) | collective-permute-done | bytes 73760 | tf_op jit(solution)/shard_map/ppermute | solution.py:319
  34.4 0.0 collective-permute-start.15
  34.4 0.9 %collective-permute-done.11.refs_1_ = bf16[288,128]{1,0:T(8,128)(2,1)S(1)} collective-permute-done((bf16[288,128]{1,0:T(8,128)(2,1)S(1)}, bf16[288,128]{1,0:T(8,128)(2,1)S(1)}, u32[]{:S(2)}, u32[]{:S(2)}) %collective-permute-start.11) | collective-permute-done | bytes 73760 | tf_op jit(solution)/shard_map/ppermute | solution.py:319
  35.3 0.0 collective-permute-start.12
  35.3 0.7 %multiply_subtract_fusion = (f32[2,4608]{1,0:T(2,128)}, f32[2,4608]{1,0:T(2,128)}) fusion(f32[2,4608]{1,0:T(2,128)S(1)} %copy-done.1, f32[1,2,36,128]{3,2,1,0:T(8,128)S(1)} %bitcast.6, f32[2,4608]{1,0:T(2,128)S(1)} %copy-done.2), kind=kLoop, calls=%fused_computation.2 | loop fusion | flops 36864 | bytes 184320 | tf_op jit(solution)/shard_map/sub | solution.py:393
  36.0 0.0 collective-permute-done.16.refs_5_
  36.0 0.0 collective-permute-done.15.refs_4_
  36.0 1.0 %place_near.1.refs_2_ = bf16[2,1152,128]{2,1,0:T(8,128)(2,1)} custom-call(bf16[288,128]{1,0:T(8,128)(2,1)S(1)} %get-tuple-element.20.refs_0_, bf16[288,128]{1,0:T(8,128)(2,1)S(1)} %collective-permute-done.11.refs_1_, bf16[288,128]{1,0:T(8,128)(2,1)S(1)} %collective-permute-done.13.refs_2_, bf16[288,128]{1,0:T(8,128)(2,1)S(1)} %collective-permute-done.14.refs_3_, ...), custom_call_target="tpu_custom_call" | custom-call | tf_op jit(solution)/shard_map/place_near/pallas_call | solution.py:235
  36.9 0.0 collective-permute-done.10.refs_0_
  37.0 0.0 collective-permute-done.12.refs_1_
  37.0 0.8 %place_far.1 = bf16[2,1152,128]{2,1,0:T(8,128)(2,1)} custom-call(bf16[288,128]{1,0:T(8,128)(2,1)S(1)} %collective-permute-done.10.refs_0_, bf16[288,128]{1,0:T(8,128)(2,1)S(1)} %collective-permute-done.12.refs_1_, bf16[2,1152,128]{2,1,0:T(8,128)(2,1)} %place_near.1.refs_2_), custom_call_target="tpu_custom_call", output_to_operand_aliasing={{}: (2, {})} | custom-call | tf_op jit(solution)/shard_map/place_far/pallas_call | solution.py:235
  (5 shorter events, 0.1 us)
Async XLA Ops:
  0.6 0.9 %copy-start.3 = (bf16[1,2,96,128]{3,2,1,0:T(8,128)(2,1)S(1)}, bf16[1,2,96,128]{3,2,1,0:T(8,128)(2,1)}, u32[]{:S(2)}) copy-start(bf16[1,2,96,128]{3,2,1,0:T(8,128)(2,1)} %param.6) | copy-start | bytes 147460
  0.6 10.1 %copy-start = (bf16[2,1152,128]{2,1,0:T(8,128)(2,1)S(1)}, bf16[2,1152,128]{2,1,0:T(8,128)(2,1)}, u32[]{:S(2)}) copy-start(bf16[2,1152,128]{2,1,0:T(8,128)(2,1)} %weight_ref.3) | copy-start | bytes 1769476
  1.5 7.2 %collective-permute-start.2 = (bf16[2,2,96,128]{3,2,1,0:T(8,128)(2,1)S(1)}, bf16[2,2,96,128]{3,2,1,0:T(8,128)(2,1)S(1)}, u32[]{:S(2)}, u32[]{:S(2)}) collective-permute-start(bf16[2,2,96,128]{3,2,1,0:T(8,128)(2,1)S(1)} %constant_dynamic-update-slice_fusion.refs_0_), channel_id=1, source_target_pairs={{0,3},{1,2},{2,1},{3,0},{4,7},{5,6},{6,5},{7,4},{8,11},{9,10},{10,... | collective-permute-start | bytes 294920 | tf_op jit(solution)/shard_map/ppermute | solution.py:319
  5.5 4.9 %collective-permute-start.1 = (bf16[2,2,96,128]{3,2,1,0:T(8,128)(2,1)S(1)}, bf16[2,2,96,128]{3,2,1,0:T(8,128)(2,1)S(1)}, u32[]{:S(2)}, u32[]{:S(2)}) collective-permute-start(bf16[2,2,96,128]{3,2,1,0:T(8,128)(2,1)S(1)} %constant_dynamic-update-slice_fusion.refs_0_), channel_id=1, source_target_pairs={{0,2},{1,3},{2,0},{3,1},{4,6},{5,7},{6,4},{7,5},{8,10},{9,11},{10,... | collective-permute-start | bytes 294920 | tf_op jit(solution)/shard_map/ppermute | solution.py:319
  6.0 4.7 %collective-permute-start = (bf16[2,2,96,128]{3,2,1,0:T(8,128)(2,1)S(1)}, bf16[2,2,96,128]{3,2,1,0:T(8,128)(2,1)S(1)}, u32[]{:S(2)}, u32[]{:S(2)}) collective-permute-start(bf16[2,2,96,128]{3,2,1,0:T(8,128)(2,1)S(1)} %constant_dynamic-update-slice_fusion.refs_0_), channel_id=1, source_target_pairs={{0,1},{1,0},{2,3},{3,2},{4,5},{5,4},{6,7},{7,6},{8,9},{9,8},{10,11... | collective-permute-start | bytes 294920 | tf_op jit(solution)/shard_map/ppermute | solution.py:319
  6.2 6.8 %copy-start.1 = (f32[2,4608]{1,0:T(2,128)S(1)}, f32[2,4608]{1,0:T(2,128)}, u32[]{:S(2)}) copy-start(f32[2,4608]{1,0:T(2,128)} %param.8) | copy-start | bytes 110596
  6.2 6.8 %copy-start.2 = (f32[2,4608]{1,0:T(2,128)S(1)}, f32[2,4608]{1,0:T(2,128)}, u32[]{:S(2)}) copy-start(f32[2,4608]{1,0:T(2,128)} %param.9) | copy-start | bytes 110596
  12.9 3.9 %collective-permute-start.3 = (bf16[288,128]{1,0:T(8,128)(2,1)S(1)}, bf16[288,128]{1,0:T(8,128)(2,1)S(1)}, u32[]{:S(2)}, u32[]{:S(2)}) collective-permute-start(bf16[288,128]{1,0:T(8,128)(2,1)S(1)} %get-tuple-element.18), channel_id=1, source_target_pairs={{0,4},{4,0},{8,12},{12,8},{16,20},{20,16},{24,28},{28,24},{1,5},{5... | collective-permute-start | bytes 221192 | tf_op jit(solution)/shard_map/ppermute | solution.py:319
  13.1 8.2 %collective-permute-start.9 = (f32[2,36,128]{2,1,0:T(8,128)S(1)}, f32[2,36,128]{2,1,0:T(8,128)S(1)}, u32[]{:S(2)}, u32[]{:S(2)}) collective-permute-start(f32[2,36,128]{2,1,0:T(8,128)S(1)} %reshape.24.refs_4_), channel_id=1, source_target_pairs={{0,24},{4,28},{8,16},{12,20},{16,8},{20,12},{24,0},{28,4},{1,25},{... | collective-permute-start | bytes 110600 | tf_op jit(solution)/shard_map/ppermute | solution.py:319
  16.8 11.0 %collective-permute-start.6 = (bf16[288,128]{1,0:T(8,128)(2,1)S(1)}, bf16[288,128]{1,0:T(8,128)(2,1)S(1)}, u32[]{:S(2)}, u32[]{:S(2)}) collective-permute-start(bf16[288,128]{1,0:T(8,128)(2,1)S(1)} %add_convert_fusion.refs_0_), channel_id=1, source_target_pairs={{0,24},{4,28},{8,16},{12,20},{16,8},{20,12},{24,0},{28,4},{1,25},{... | collective-permute-start | bytes 221192 | tf_op jit(solution)/shard_map/ppermute | solution.py:319
  17.9 9.9 %collective-permute-start.5 = (bf16[288,128]{1,0:T(8,128)(2,1)S(1)}, bf16[288,128]{1,0:T(8,128)(2,1)S(1)}, u32[]{:S(2)}, u32[]{:S(2)}) collective-permute-start(bf16[288,128]{1,0:T(8,128)(2,1)S(1)} %add_convert_fusion.refs_0_), channel_id=1, source_target_pairs={{0,16},{4,20},{8,24},{12,28},{16,0},{20,4},{24,8},{28,12},{1,17},{... | collective-permute-start | bytes 221192 | tf_op jit(solution)/shard_map/ppermute | solution.py:319
  17.9 9.9 %collective-permute-start.4 = (bf16[288,128]{1,0:T(8,128)(2,1)S(1)}, bf16[288,128]{1,0:T(8,128)(2,1)S(1)}, u32[]{:S(2)}, u32[]{:S(2)}) collective-permute-start(bf16[288,128]{1,0:T(8,128)(2,1)S(1)} %add_convert_fusion.refs_0_), channel_id=1, source_target_pairs={{0,8},{4,12},{8,0},{12,4},{16,24},{20,28},{24,16},{28,20},{1,9},{5... | collective-permute-start | bytes 221192 | tf_op jit(solution)/shard_map/ppermute | solution.py:319
  21.2 6.6 %collective-permute-start.8 = (f32[2,36,128]{2,1,0:T(8,128)S(1)}, f32[2,36,128]{2,1,0:T(8,128)S(1)}, u32[]{:S(2)}, u32[]{:S(2)}) collective-permute-start(f32[2,36,128]{2,1,0:T(8,128)S(1)} %reshape.24.refs_4_), channel_id=1, source_target_pairs={{0,16},{4,20},{8,24},{12,28},{16,0},{20,4},{24,8},{28,12},{1,17},{... | collective-permute-start | bytes 110600 | tf_op jit(solution)/shard_map/ppermute | solution.py:319
  21.2 6.6 %collective-permute-start.7 = (f32[2,36,128]{2,1,0:T(8,128)S(1)}, f32[2,36,128]{2,1,0:T(8,128)S(1)}, u32[]{:S(2)}, u32[]{:S(2)}) collective-permute-start(f32[2,36,128]{2,1,0:T(8,128)S(1)} %reshape.24.refs_4_), channel_id=1, source_target_pairs={{0,8},{4,12},{8,0},{12,4},{16,24},{20,28},{24,16},{28,20},{1,9},{5... | collective-permute-start | bytes 110600 | tf_op jit(solution)/shard_map/ppermute | solution.py:319
  27.9 5.7 %collective-permute-start.14 = (bf16[288,128]{1,0:T(8,128)(2,1)S(1)}, bf16[288,128]{1,0:T(8,128)(2,1)S(1)}, u32[]{:S(2)}, u32[]{:S(2)}) collective-permute-start(bf16[288,128]{1,0:T(8,128)(2,1)S(1)} %get-tuple-element.20.refs_0_), channel_id=1, source_target_pairs={{0,3},{1,2},{2,1},{3,0},{4,7},{5,6},{6,5},{7,4},{8,11},{9,10},{10,... | collective-permute-start | bytes 221192 | tf_op jit(solution)/shard_map/ppermute | solution.py:319
  29.6 4.8 %collective-permute-start.13 = (bf16[288,128]{1,0:T(8,128)(2,1)S(1)}, bf16[288,128]{1,0:T(8,128)(2,1)S(1)}, u32[]{:S(2)}, u32[]{:S(2)}) collective-permute-start(bf16[288,128]{1,0:T(8,128)(2,1)S(1)} %get-tuple-element.20.refs_0_), channel_id=1, source_target_pairs={{0,2},{1,3},{2,0},{3,1},{4,6},{5,7},{6,4},{7,5},{8,10},{9,11},{10,... | collective-permute-start | bytes 221192 | tf_op jit(solution)/shard_map/ppermute | solution.py:319
  30.9 4.4 %collective-permute-start.11 = (bf16[288,128]{1,0:T(8,128)(2,1)S(1)}, bf16[288,128]{1,0:T(8,128)(2,1)S(1)}, u32[]{:S(2)}, u32[]{:S(2)}) collective-permute-start(bf16[288,128]{1,0:T(8,128)(2,1)S(1)} %get-tuple-element.20.refs_0_), channel_id=1, source_target_pairs={{0,1},{1,0},{2,3},{3,2},{4,5},{5,4},{6,7},{7,6},{8,9},{9,8},{10,11... | collective-permute-start | bytes 221192 | tf_op jit(solution)/shard_map/ppermute | solution.py:319
  32.5 4.5 %collective-permute-start.10 = (bf16[288,128]{1,0:T(8,128)(2,1)S(1)}, bf16[288,128]{1,0:T(8,128)(2,1)S(1)}, u32[]{:S(2)}, u32[]{:S(2)}) collective-permute-start(bf16[288,128]{1,0:T(8,128)(2,1)S(1)} %get-tuple-element.20.refs_0_), channel_id=1, source_target_pairs={{0,4},{4,0},{8,12},{12,8},{16,20},{20,16},{24,28},{28,24},{1,5},{5... | collective-permute-start | bytes 221192 | tf_op jit(solution)/shard_map/ppermute | solution.py:319
  33.7 2.3 %collective-permute-start.16 = (bf16[288,128]{1,0:T(8,128)(2,1)S(1)}, bf16[288,128]{1,0:T(8,128)(2,1)S(1)}, u32[]{:S(2)}, u32[]{:S(2)}) collective-permute-start(bf16[288,128]{1,0:T(8,128)(2,1)S(1)} %collective-permute-done.14.refs_3_), channel_id=1, source_target_pairs={{0,4},{4,0},{8,12},{12,8},{16,20},{20,16},{24,28},{28,24},{1,5},{5... | collective-permute-start | bytes 221192 | tf_op jit(solution)/shard_map/ppermute | solution.py:319
  34.4 1.6 %collective-permute-start.15 = (bf16[288,128]{1,0:T(8,128)(2,1)S(1)}, bf16[288,128]{1,0:T(8,128)(2,1)S(1)}, u32[]{:S(2)}, u32[]{:S(2)}) collective-permute-start(bf16[288,128]{1,0:T(8,128)(2,1)S(1)} %collective-permute-done.13.refs_2_), channel_id=1, source_target_pairs={{0,4},{4,0},{8,12},{12,8},{16,20},{20,16},{24,28},{28,24},{1,5},{5... | collective-permute-start | bytes 221192 | tf_op jit(solution)/shard_map/ppermute | solution.py:319
  35.3 1.7 %collective-permute-start.12 = (bf16[288,128]{1,0:T(8,128)(2,1)S(1)}, bf16[288,128]{1,0:T(8,128)(2,1)S(1)}, u32[]{:S(2)}, u32[]{:S(2)}) collective-permute-start(bf16[288,128]{1,0:T(8,128)(2,1)S(1)} %collective-permute-done.11.refs_1_), channel_id=1, source_target_pairs={{0,4},{4,0},{8,12},{12,8},{16,20},{20,16},{24,28},{28,24},{1,5},{5... | collective-permute-start | bytes 221192 | tf_op jit(solution)/shard_map/ppermute | solution.py:319
